TPU v7x, 32 devices: a whole 2x2x4 slice. The times are simulated.
32 devices in a mesh: ctx: 4 (over z), dp: 4 (over y, x), section: 2 (over core).
Axes of the slice: x: 2, y: 2, z: 4, core: 2. Of those that a mesh axis runs over, the one named last changes fastest.
Arguments:
- tokens: bfloat16 [2, 4, 512, 4096], P('section', 'dp', 'ctx'), may hold values from -6 to 6
- norm_gain: float32 [2, 4096], P('section'), may hold values from 0.1 to 1.9
- query_weight: bfloat16 [2, 4096, 512], P('section', 'dp'), may hold values from -0.421875 to 0.421875
- key_weight: bfloat16 [2, 4096, 128], P('section', 'dp'), may hold values from -0.421875 to 0.421875
- value_weight: bfloat16 [2, 4096, 128], P('section', 'dp'), may hold values from -0.09375 to 0.09375
- block_order: int32 [2, 4, 8], P('section', 'dp'), may hold values from 0 to 7, each once within a row
- doc_ids: int32 [2, 4, 512], P('section', 'dp'), may hold values from 0 to 3, never falling along the last dimension, each value on 1 to 256 neighbouring positions
Outputs:
- passed: bfloat16 [2, 4, 512, 512], P('section', 'dp', 'ctx')
Inputs may be any that keep to these rules, and one draw needn't show every extreme that they name: `block_order`: each row is a permutation of the block numbers. `doc_ids`: never falling along positions; every document holds 1 to 256 positions, and one holds exactly 256.
All inputs are finite; a program needn't handle non-finite values.
Results may differ from a plain program's by a relative error of at most 0.012.
Values may be sent and summed in bfloat16 or wider, within the bound.
No kernel may reach another device: no remote copies, remote signals or barrier semaphores. Data moves between devices by JAX's collectives and lax.ppermute only.
A program may use at most 64 MiB of HBM per device.

v0:
```python
import functools

import jax
import jax.numpy as jnp
from jax import lax
from jax.experimental import pallas as pl
from jax.experimental.pallas import tpu as pltpu
from jax.sharding import PartitionSpec as P

ROPE_BASE = 500000.0
EPSILON = 1e-05
MASKED = -1e30
LOG2E = 1.4426950408889634
DIRECT = 8
GRANT = 8 << 20


def partner(index, step, count):
    if count & (count - 1) == 0:
        return index ^ step
    return (step - index) % count


def swap_dp(x, step, count):
    return lax.ppermute(x, "dp", [(i, partner(i, step, count)) for i in range(count)])


def to_next_section(x, step, count, sections):
    moves = [
        (i * sections + s, partner(i, step, count) * sections + (s + 1) % sections)
        for i in range(count)
        for s in range(sections)
    ]
    return lax.ppermute(x, ("dp", "section"), moves)


def shift_ctx(x, by, ring):
    return lax.ppermute(x, "ctx", [(i, (i + by) % ring) for i in range(ring)])


def local_call(kernel, out_shape, args, in_spaces, scratch=()):
    return pl.pallas_call(
        kernel,
        out_shape=out_shape,
        in_specs=[pl.BlockSpec(memory_space=s) for s in in_spaces],
        out_specs=jax.tree.map(
            lambda s: pl.BlockSpec(memory_space=pltpu.VMEM), out_shape
        ),
        scratch_shapes=scratch,
        compiler_params=pltpu.CompilerParams(vmem_limit_bytes=GRANT),
    )(*args)


def cut_kernel(count, slots_ref, rows_ref, *refs):
    out_refs, sem = refs[:count], refs[count]
    width = out_refs[0].shape[1]
    copies = []
    for k in range(count):
        begin = pl.multiple_of(slots_ref[k] * width, width)
        copies.append(
            pltpu.make_async_copy(rows_ref.at[:, pl.ds(begin, width)], out_refs[k], sem.at[k])
        )
    for copy in copies:
        copy.start()
    for copy in copies:
        copy.wait()


def cut(rows, slots, count):
    height, features = rows.shape
    shape = jax.ShapeDtypeStruct((height, features // count), jnp.bfloat16)
    return local_call(
        functools.partial(cut_kernel, count),
        [shape] * count,
        (slots, rows),
        (pltpu.SMEM, pl.ANY),
        [pltpu.SemaphoreType.DMA((count,))],
    )


def column(row):
    size = row.shape[1]
    down = lax.broadcasted_iota(jnp.int32, (size, size), 0)
    across = lax.broadcasted_iota(jnp.int32, (size, size), 1)
    return jnp.sum(jnp.where(down == across, row, 0.0), axis=1, keepdims=True)


def tables_kernel(length, at_ref, meta_ref, freq_ref, kcos, ksin, qcos, qsin, level, bias):
    rows, size = kcos.shape
    begin = pl.multiple_of(at_ref[0] * rows, rows)
    qpos = column(meta_ref[:, pl.ds(begin, rows)])
    qdoc = column(meta_ref[:, pl.ds(length + begin, rows)])
    scale = column(meta_ref[:, 2 * length :])
    angles = qpos * freq_ref[...]
    sign = jnp.where(lax.broadcasted_iota(jnp.int32, (1, size), 1) < size // 2, -1.0, 1.0)
    cosine, sine = jnp.cos(angles) * scale, jnp.sin(angles) * sign * scale
    kcos[...], ksin[...] = cosine, sine
    more = size ** (-0.5) * LOG2E
    qcos[...], qsin[...] = cosine * more, sine * more
    level[...] = jnp.broadcast_to(scale, level.shape)
    allowed = (meta_ref[:, length : 2 * length] == qdoc) & (meta_ref[:, :length] <= qpos)
    bias[...] = jnp.where(allowed, 0.0, MASKED)


def tables(at, meta, freqs, rows, size, length):
    square = jax.ShapeDtypeStruct((rows, size), jnp.float32)
    return local_call(
        functools.partial(tables_kernel, length),
        [square] * 5 + [jax.ShapeDtypeStruct((rows, length), jnp.float32)],
        (at, meta, freqs),
        (pltpu.SMEM, pltpu.VMEM, pltpu.VMEM),
    )


def summed(refs, start, stop):
    total = refs[0][:, start:stop].astype(jnp.float32)
    for ref in refs[1:]:
        total = total + ref[:, start:stop].astype(jnp.float32)
    return total


def turn(x, cosine, sine):
    return x * cosine + pltpu.roll(x, x.shape[1] // 2, 1) * sine


def mix_kernel(*refs):
    parts, (kcos, ksin, level, out_ref) = refs[:-4], refs[-4:]
    size = kcos.shape[1]
    keys = turn(summed(parts, 0, size), kcos[...], ksin[...])
    out_ref[:, :size] = keys.astype(jnp.bfloat16)
    out_ref[:, size:] = (summed(parts, size, 2 * size) * level[...]).astype(jnp.bfloat16)


def mix(parts, kcos, ksin, level):
    args = (*parts, kcos, ksin, level)
    return local_call(
        mix_kernel,
        jax.ShapeDtypeStruct(parts[0].shape, jnp.bfloat16),
        args,
        [pltpu.VMEM] * len(args),
    )


def attend_kernel(count, ring, at_ref, *refs):
    parts, kv_refs = refs[:count], refs[count : count + ring]
    qcos, qsin, bias, out_ref = refs[count + ring :]
    rows, size = qcos.shape
    keys = jnp.concatenate([ref[:, :size] for ref in kv_refs], axis=0)
    values = jnp.concatenate([ref[:, size:] for ref in kv_refs], axis=0)
    here = [
        pl.multiple_of(lax.rem(at_ref[0] - j + ring, ring) * rows, rows) for j in range(ring)
    ]
    masks = jnp.concatenate([bias[:, pl.ds(b, rows)] for b in here], axis=1)
    for h in range(out_ref.shape[1] // size):
        query = turn(summed(parts, h * size, (h + 1) * size), qcos[...], qsin[...])
        scores = lax.dot_general(
            query.astype(jnp.bfloat16),
            keys,
            (((1,), (1,)), ((), ())),
            preferred_element_type=jnp.float32,
        )
        scores = scores + masks
        probs = jnp.exp2(scores - jnp.max(scores, axis=-1, keepdims=True))
        total = jnp.sum(probs, axis=-1, keepdims=True)
        mixed = jnp.dot(probs.astype(jnp.bfloat16), values, preferred_element_type=jnp.float32)
        out_ref[:, h * size : (h + 1) * size] = (mixed / total).astype(jnp.bfloat16)


def attend(at, parts, kv, qcos, qsin, bias):
    args = (at, *parts, *kv, qcos, qsin, bias)
    return local_call(
        functools.partial(attend_kernel, len(parts), len(kv)),
        jax.ShapeDtypeStruct(parts[0].shape, jnp.bfloat16),
        args,
        [pltpu.SMEM] + [pltpu.VMEM] * (len(args) - 1),
    )


def attend_long(parts, everything, qcos, qsin, bias):
    rows, width = parts[0].shape
    size = qcos.shape[1]
    heads = width // size
    total_q = sum(p.astype(jnp.float32) for p in parts).reshape(rows, heads, size)
    turned = jnp.concatenate([total_q[..., size // 2 :], total_q[..., : size // 2]], axis=-1)
    queries = (total_q * qcos[:, None] + turned * qsin[:, None]).astype(jnp.bfloat16)
    length = everything.shape[0]
    chunk = 1024 if length % 1024 == 0 else length

    def absorb(state, piece):
        run_max, run_total, run_acc = state
        block, mask = piece
        scores = jnp.einsum(
            "qhd,kd->hqk", queries, block[:, :size], preferred_element_type=jnp.float32
        )
        scores = scores + mask[None]
        new_max = jnp.maximum(run_max, jnp.max(scores, axis=-1))
        weights = jnp.where(mask[None] == 0.0, jnp.exp2(scores - new_max[..., None]), 0.0)
        factor = jnp.exp2(run_max - new_max)
        new_total = run_total * factor + jnp.sum(weights, axis=-1)
        new_acc = run_acc * factor[..., None] + jnp.einsum(
            "hqk,kd->hqd",
            weights.astype(jnp.bfloat16),
            block[:, size:],
            preferred_element_type=jnp.float32,
        )
        return (new_max, new_total, new_acc), None

    groups = length // chunk
    start = (
        jnp.full((heads, rows), MASKED, jnp.float32),
        jnp.zeros((heads, rows), jnp.float32),
        jnp.zeros((heads, rows, size), jnp.float32),
    )
    (_, total, acc), _ = lax.scan(
        absorb,
        start,
        (
            everything.reshape(groups, chunk, -1),
            bias.reshape(rows, groups, chunk).transpose(1, 0, 2),
        ),
    )
    out = (acc / total[..., None]).transpose(1, 0, 2).reshape(rows, width)
    return out.astype(jnp.bfloat16)


def local(
    count, sections, ring, tokens, norm_gain, query_weight, key_weight, value_weight, block_order, doc_ids
):
    rows_here = tokens[0, 0]
    row_count = rows_here.shape[0]
    length = doc_ids.shape[2]
    blocks = block_order.shape[2]
    block_rows = length // blocks
    size = key_weight.shape[2]
    depth = key_weight.shape[1]
    here, at = lax.axis_index("dp"), lax.axis_index("ctx").astype(jnp.int32)[None]
    sequence = list(range(count - 1, -1, -1))
    sequence = [sequence[0], *sequence[-2:0:-1], sequence[-1]]
    slots = jnp.stack([partner(here, k, count) for k in sequence]).astype(jnp.int32)
    slabs = cut(rows_here, slots, count)

    arrived = {}
    for k, slab in zip(sequence, slabs):
        arrived[k] = swap_dp(slab, k, count) if k else slab

    wide = rows_here.astype(jnp.float32)
    scale = lax.rsqrt(jnp.mean(wide * wide, axis=-1) + EPSILON)
    order = block_order[0, 0]
    pick = (order[:, None] == jnp.arange(blocks, dtype=jnp.int32)[None, :]).astype(jnp.int32)
    row_docs = jnp.sum(pick[:, :, None] * doc_ids[0, 0].reshape(1, blocks, block_rows), axis=1)
    positions = order[:, None] * block_rows + jnp.arange(block_rows, dtype=jnp.int32)[None, :]
    meta = jnp.concatenate(
        [
            positions.reshape(1, -1).astype(jnp.float32),
            row_docs.reshape(1, -1).astype(jnp.float32),
            scale[None],
        ],
        axis=1,
    )
    meta = lax.ppermute(meta, "section", [(i, (i + 1) % sections) for i in range(sections)])

    half = size // 2
    freqs = ROPE_BASE ** (-jnp.arange(half, dtype=jnp.float32) * 2.0 / size)
    freqs = jnp.concatenate([freqs, freqs])[None]
    kcos, ksin, qcos, qsin, level, bias = tables(at, meta, freqs, row_count, size, length)

    gain = lax.dynamic_slice_in_dim(norm_gain[0], here * depth, depth)[:, None]
    kv_weight = jnp.concatenate([key_weight[0], value_weight[0]], axis=1)
    kv_weight = (kv_weight.astype(jnp.float32) * gain).astype(jnp.bfloat16)
    q_weight = (query_weight[0].astype(jnp.float32) * gain).astype(jnp.bfloat16)

    kv_parts, q_parts = [], []
    last = [sequence[-1], *sequence[:-1]]
    for k in last:
        part = jnp.dot(arrived[k], kv_weight, preferred_element_type=jnp.float32)
        kv_parts.append(to_next_section(part.astype(jnp.bfloat16), k, count, sections))
    for k in last:
        part = jnp.dot(arrived[k], q_weight, preferred_element_type=jnp.float32)
        q_parts.append(to_next_section(part.astype(jnp.bfloat16), k, count, sections))

    kv = mix(kv_parts, kcos, ksin, level)
    if ring <= DIRECT:
        pieces = [kv]
        for j in range(1, ring):
            pieces.append(shift_ctx(kv, j, ring))
        out = attend(at, q_parts, pieces, qcos, qsin, bias)
    else:
        everything = lax.all_gather(kv, "ctx", axis=0, tiled=True)
        out = attend_long(q_parts, everything, qcos, qsin, bias)
    return out[None, None]


def solution(mesh):
    in_specs = (
        P("section", "dp", "ctx", None),
        P("section", None),
        P("section", "dp", None),
        P("section", "dp", None),
        P("section", "dp", None),
        P("section", "dp", None),
        P("section", "dp", None),
    )
    out_specs = P("section", "dp", "ctx", None)

    def body(*args):
        return local(mesh.shape["dp"], mesh.shape["section"], mesh.shape["ctx"], *args)

    return jax.shard_map(body, mesh=mesh, in_specs=in_specs, out_specs=out_specs, check_vma=False)
```

profile of v0, /device:TPU:0, one launch (start us, length us, event | category | flops | bytes accessed | tf_op | source)
XLA Modules:
  0.0 46.0 jit_solution(3694891364155870769)
XLA Ops:
  0.1 1.2 %copy-done.1 = bf16[1,1,128,4096]{3,2,1,0:T(8,128)(2,1)S(1)} copy-done((bf16[1,1,128,4096]{3,2,1,0:T(8,128)(2,1)S(1)}, bf16[1,1,128,4096]{3,2,1,0:T(8,128)(2,1)}, u32[]{:S(2)}) %copy-start.1) | copy-done | bytes 1048600
  1.3 0.7 %shard_map.73 = (bf16[128,1024]{1,0:T(8,128)(2,1)S(1)}, bf16[128,1024]{1,0:T(8,128)(2,1)S(1)}, bf16[128,1024]{1,0:T(8,128)(2,1)S(1)}, bf16[128,1024]{1,0:T(8,128)(2,1)S(1)}) custom-call(s32[4]{0:T(128)S(1)} %pad_add_fusion.slots_ref, bf16[128,4096]{1,0:T(8,128)(2,1)S(1)} %bitcast.32), custom_call_target="tpu_custom_call" | custom-call | tf_op jit(solution)/shard_map/pallas_call | solution.py:42
  3.0 0.6 %collective-permute-start = (bf16[128,512]{1,0:T(8,128)(2,1)S(1)}, bf16[128,512]{1,0:T(8,128)(2,1)S(1)}, u32[]{:S(2)}, u32[]{:S(2)}) collective-permute-start(bf16[128,512]{1,0:T(8,128)(2,1)S(1)} %convolution_convert_fusion.3), channel_id=1, source_target_pairs={{0,1},{1,0},{2,3},{3,2},{4,5},{5,4},{6,7},{7,6},{8,9},{9,8},{10,11... | collective-permute-start | bytes 393224 | tf_op jit(solution)/shard_map/ppermute | solution.py:34
  3.5 3.5 %collective-permute-start.1 = (bf16[128,1024]{1,0:T(8,128)(2,1)S(1)}, bf16[128,1024]{1,0:T(8,128)(2,1)}, u32[]{:S(2)}, u32[]{:S(2)}) collective-permute-start(bf16[128,1024]{1,0:T(8,128)(2,1)S(1)} %get-tuple-element.16), channel_id=1, source_target_pairs={{0,6},{2,4},{4,2},{6,0},{1,7},{3,5},{5,3},{7,1},{8,14},{10,12},{12... | collective-permute-start | bytes 786440 | tf_op jit(solution)/shard_map/ppermute | solution.py:25
  7.1 0.5 %collective-permute-start.3 = (bf16[128,1024]{1,0:T(8,128)(2,1)S(1)}, bf16[128,1024]{1,0:T(8,128)(2,1)S(1)}, u32[]{:S(2)}, u32[]{:S(2)}) collective-permute-start(bf16[128,1024]{1,0:T(8,128)(2,1)S(1)} %get-tuple-element.17), channel_id=1, source_target_pairs={{0,2},{2,0},{4,6},{6,4},{1,3},{3,1},{5,7},{7,5},{8,10},{10,8},{12,... | collective-permute-start | bytes 786440 | tf_op jit(solution)/shard_map/ppermute | solution.py:25
  7.7 1.0 %convolution_convert_fusion.7 = bf16[128,256]{1,0:T(8,128)(2,1)} fusion(bf16[128,1024]{1,0:T(8,128)(2,1)S(1)} %get-tuple-element.15, bf16[1024,128]{1,0:T(8,128)(2,1)S(1)} %bitcast.42, bf16[1024,128]{1,0:T(8,128)(2,1)S(1)} %bitcast.46, f32[1024]{0:T(1024)S(1)} %bitcast.34), kind=kOutput, calls=%fused_computation.10 | convolution fusion | flops 68714496 | bytes 856064 | tf_op jit(solution)/shard_map/dot_general | solution.py:275
  9.5 0.6 %reduce.3 = s32[512]{0:T(512)S(1)} reduce(s32[1,1,512]{2,1,0:T(1,128)S(1)} %copy-done.3, s32[]{:T(128)} %broadcast.49), dimensions={0,1}, to_apply=%param.13.reduce_sub_computation.3 | reduce | bytes 4100 | tf_op args[6]
  10.6 3.7 %collective-permute-done.1 = bf16[128,1024]{1,0:T(8,128)(2,1)} collective-permute-done((bf16[128,1024]{1,0:T(8,128)(2,1)S(1)}, bf16[128,1024]{1,0:T(8,128)(2,1)}, u32[]{:S(2)}, u32[]{:S(2)}) %collective-permute-start.1) | collective-permute-done | bytes 262176 | tf_op jit(solution)/shard_map/ppermute | solution.py:25
  14.4 1.4 %convolution_convert_fusion.2 = bf16[128,512]{1,0:T(8,128)(2,1)S(1)} fusion(bf16[128,1024]{1,0:T(8,128)(2,1)} %collective-permute-done.1, bf16[1,1024,512]{2,1,0:T(8,128)(2,1)S(1)} %copy-done.5, f32[1024]{0:T(1024)S(1)} %bitcast.35), kind=kOutput, calls=%fused_computation.5 | convolution fusion | flops 135856128 | bytes 1445888 | tf_op jit(solution)/shard_map/dot_general | solution.py:278
  15.7 1.3 %convolution_convert_fusion.6 = bf16[128,256]{1,0:T(8,128)(2,1)S(1)} fusion(bf16[128,1024]{1,0:T(8,128)(2,1)} %collective-permute-done.1, bf16[1024,128]{1,0:T(8,128)(2,1)S(1)} %bitcast.43, bf16[1024,128]{1,0:T(8,128)(2,1)S(1)} %bitcast.47, f32[1024]{0:T(1024)S(1)} %bitcast.36), kind=kOutput, calls=%fused_computation.9 | convolution fusion | flops 68714496 | bytes 856064 | tf_op jit(solution)/shard_map/dot_general | solution.py:275
  17.1 2.8 %collective-permute-done.3 = bf16[128,1024]{1,0:T(8,128)(2,1)S(1)} collective-permute-done((bf16[128,1024]{1,0:T(8,128)(2,1)S(1)}, bf16[128,1024]{1,0:T(8,128)(2,1)S(1)}, u32[]{:S(2)}, u32[]{:S(2)}) %collective-permute-start.3) | collective-permute-done | bytes 262176 | tf_op jit(solution)/shard_map/ppermute | solution.py:25
  19.9 0.6 %collective-permute-start.2 = (bf16[128,512]{1,0:T(8,128)(2,1)S(1)}, bf16[128,512]{1,0:T(8,128)(2,1)S(1)}, u32[]{:S(2)}, u32[]{:S(2)}) collective-permute-start(bf16[128,512]{1,0:T(8,128)(2,1)S(1)} %convolution_convert_fusion.2), channel_id=1, source_target_pairs={{0,7},{1,6},{2,5},{3,4},{4,3},{5,2},{6,1},{7,0},{8,15},{9,14},{10,... | collective-permute-start | bytes 393224 | tf_op jit(solution)/shard_map/ppermute | solution.py:34
  20.9 2.1 %collective-permute-start.8 = (bf16[128,256]{1,0:T(8,128)(2,1)S(1)}, bf16[128,256]{1,0:T(8,128)(2,1)S(1)}, u32[]{:S(2)}, u32[]{:S(2)}) collective-permute-start(bf16[128,256]{1,0:T(8,128)(2,1)S(1)} %convolution_convert_fusion.6), channel_id=1, source_target_pairs={{0,7},{1,6},{2,5},{3,4},{4,3},{5,2},{6,1},{7,0},{8,15},{9,14},{10,... | collective-permute-start | bytes 196616 | tf_op jit(solution)/shard_map/ppermute | solution.py:34
  23.9 0.7 %collective-permute-start.9 = (bf16[128,256]{1,0:T(8,128)(2,1)S(1)}, bf16[128,256]{1,0:T(8,128)(2,1)S(1)}, u32[]{:S(2)}, u32[]{:S(2)}) collective-permute-start(bf16[128,256]{1,0:T(8,128)(2,1)S(1)} %convolution_convert_fusion.5), channel_id=1, source_target_pairs={{0,3},{1,2},{2,1},{3,0},{4,7},{5,6},{6,5},{7,4},{8,11},{9,10},{10,... | collective-permute-start | bytes 196616 | tf_op jit(solution)/shard_map/ppermute | solution.py:34
  25.0 1.1 %collective-permute-start.4 = (bf16[128,512]{1,0:T(8,128)(2,1)S(1)}, bf16[128,512]{1,0:T(8,128)(2,1)S(1)}, u32[]{:S(2)}, u32[]{:S(2)}) collective-permute-start(bf16[128,512]{1,0:T(8,128)(2,1)S(1)} %convolution_convert_fusion.1), channel_id=1, source_target_pairs={{0,3},{1,2},{2,1},{3,0},{4,7},{5,6},{6,5},{7,4},{8,11},{9,10},{10,... | collective-permute-start | bytes 393224 | tf_op jit(solution)/shard_map/ppermute | solution.py:34
  26.1 1.8 %collective-permute-done.8.refs_1_ = bf16[128,256]{1,0:T(8,128)(2,1)S(1)} collective-permute-done((bf16[128,256]{1,0:T(8,128)(2,1)S(1)}, bf16[128,256]{1,0:T(8,128)(2,1)S(1)}, u32[]{:S(2)}, u32[]{:S(2)}) %collective-permute-start.8) | collective-permute-done | bytes 65568 | tf_op jit(solution)/shard_map/ppermute | solution.py:34
  28.3 1.4 %collective-permute-start.10 = (bf16[128,256]{1,0:T(8,128)(2,1)S(1)}, bf16[128,256]{1,0:T(8,128)(2,1)S(1)}, u32[]{:S(2)}, u32[]{:S(2)}) collective-permute-start(bf16[128,256]{1,0:T(8,128)(2,1)S(1)} %convolution_convert_fusion.4), channel_id=1, source_target_pairs={{0,5},{1,4},{2,7},{3,6},{4,1},{5,0},{6,3},{7,2},{8,13},{9,12},{10,... | collective-permute-start | bytes 196616 | tf_op jit(solution)/shard_map/ppermute | solution.py:34
  30.2 4.8 %collective-permute-done.10.refs_3_ = bf16[128,256]{1,0:T(8,128)(2,1)S(1)} collective-permute-done((bf16[128,256]{1,0:T(8,128)(2,1)S(1)}, bf16[128,256]{1,0:T(8,128)(2,1)S(1)}, u32[]{:S(2)}, u32[]{:S(2)}) %collective-permute-start.10) | collective-permute-done | bytes 65568 | tf_op jit(solution)/shard_map/ppermute | solution.py:34
  35.1 1.6 %collective-permute-start.12 = (bf16[128,256]{1,0:T(8,128)(2,1)S(1)}, bf16[128,256]{1,0:T(8,128)(2,1)S(1)}, u32[]{:S(2)}, u32[]{:S(2)}) collective-permute-start(bf16[128,256]{1,0:T(8,128)(2,1)S(1)} %shard_map.75.refs_4_), channel_id=1, source_target_pairs={{0,8},{8,16},{16,24},{24,0},{1,9},{9,17},{17,25},{25,1},{2,10},{10... | collective-permute-start | bytes 196616 | tf_op jit(solution)/shard_map/ppermute | solution.py:38
  36.7 2.6 %collective-permute-start.13 = (bf16[128,256]{1,0:T(8,128)(2,1)S(1)}, bf16[128,256]{1,0:T(8,128)(2,1)S(1)}, u32[]{:S(2)}, u32[]{:S(2)}) collective-permute-start(bf16[128,256]{1,0:T(8,128)(2,1)S(1)} %shard_map.75.refs_4_), channel_id=1, source_target_pairs={{0,16},{8,24},{16,0},{24,8},{1,17},{9,25},{17,1},{25,9},{2,18},{10... | collective-permute-start | bytes 196616 | tf_op jit(solution)/shard_map/ppermute | solution.py:38
  39.3 1.3 %collective-permute-start.14 = (bf16[128,256]{1,0:T(8,128)(2,1)S(1)}, bf16[128,256]{1,0:T(8,128)(2,1)S(1)}, u32[]{:S(2)}, u32[]{:S(2)}) collective-permute-start(bf16[128,256]{1,0:T(8,128)(2,1)S(1)} %shard_map.75.refs_4_), channel_id=1, source_target_pairs={{0,24},{8,0},{16,8},{24,16},{1,25},{9,1},{17,9},{25,17},{2,26},{10... | collective-permute-start | bytes 196616 | tf_op jit(solution)/shard_map/ppermute | solution.py:38
  40.7 0.9 %collective-permute-done.12.refs_5_ = bf16[128,256]{1,0:T(8,128)(2,1)S(1)} collective-permute-done((bf16[128,256]{1,0:T(8,128)(2,1)S(1)}, bf16[128,256]{1,0:T(8,128)(2,1)S(1)}, u32[]{:S(2)}, u32[]{:S(2)}) %collective-permute-start.12) | collective-permute-done | bytes 65568 | tf_op jit(solution)/shard_map/ppermute | solution.py:38
  41.6 2.5 %collective-permute-done.13.refs_6_ = bf16[128,256]{1,0:T(8,128)(2,1)S(1)} collective-permute-done((bf16[128,256]{1,0:T(8,128)(2,1)S(1)}, bf16[128,256]{1,0:T(8,128)(2,1)S(1)}, u32[]{:S(2)}, u32[]{:S(2)}) %collective-permute-start.13) | collective-permute-done | bytes 65568 | tf_op jit(solution)/shard_map/ppermute | solution.py:38
  44.0 2.0 %shard_map.76 = bf16[128,512]{1,0:T(8,128)(2,1)} custom-call(s32[1]{0:T(128)} %bitcast.at_ref, bf16[128,512]{1,0:T(8,128)(2,1)S(1)} %collective-permute-done.refs_0_, bf16[128,512]{1,0:T(8,128)(2,1)S(1)} %collective-permute-done.2.refs_1_, bf16[128,512]{1,0:T(8,128)(2,1)S(1)} %collective-permute-done.4.refs_2_, ...), custom_call_target="tpu_custom_call" | custom-call | tf_op jit(solution)/shard_map/pallas_call | solution.py:42
  (51 shorter events, 5.0 us)
Async XLA Ops:
  0.0 2.0 %copy-start = (f32[1,4096]{1,0:T(1,128)S(1)}, f32[1,4096]{1,0:T(1,128)}, u32[]{:S(2)}) copy-start(f32[1,4096]{1,0:T(1,128)} %param.8) | copy-start | bytes 49156
  0.1 1.2 %copy-start.1 = (bf16[1,1,128,4096]{3,2,1,0:T(8,128)(2,1)S(1)}, bf16[1,1,128,4096]{3,2,1,0:T(8,128)(2,1)}, u32[]{:S(2)}) copy-start(bf16[1,1,128,4096]{3,2,1,0:T(8,128)(2,1)} %param.7) | copy-start | bytes 3145732
  1.3 1.2 %copy-start.5 = (bf16[1,1024,512]{2,1,0:T(8,128)(2,1)S(1)}, bf16[1,1024,512]{2,1,0:T(8,128)(2,1)}, u32[]{:S(2)}) copy-start(bf16[1,1024,512]{2,1,0:T(8,128)(2,1)} %param.9) | copy-start | bytes 3145732
  2.0 5.7 %copy-start.6 = (bf16[1,1024,128]{2,1,0:T(8,128)(2,1)S(1)}, bf16[1,1024,128]{2,1,0:T(8,128)(2,1)}, u32[]{:S(2)}) copy-start(bf16[1,1024,128]{2,1,0:T(8,128)(2,1)} %param.11) | copy-start | bytes 786436
  2.0 5.7 %copy-start.7 = (bf16[1,1024,128]{2,1,0:T(8,128)(2,1)S(1)}, bf16[1,1024,128]{2,1,0:T(8,128)(2,1)}, u32[]{:S(2)}) copy-start(bf16[1,1024,128]{2,1,0:T(8,128)(2,1)} %param.10) | copy-start | bytes 786436
  3.0 5.8 %copy-start.2 = (bf16[1,1,128,4096]{3,2,1,0:T(8,128)(2,1)S(1)}, bf16[1,1,128,4096]{3,2,1,0:T(8,128)(2,1)}, u32[]{:S(2)}) copy-start(bf16[1,1,128,4096]{3,2,1,0:T(8,128)(2,1)} %param.7) | copy-start | bytes 3145732
  3.0 33.7 %collective-permute-start = (bf16[128,512]{1,0:T(8,128)(2,1)S(1)}, bf16[128,512]{1,0:T(8,128)(2,1)S(1)}, u32[]{:S(2)}, u32[]{:S(2)}) collective-permute-start(bf16[128,512]{1,0:T(8,128)(2,1)S(1)} %convolution_convert_fusion.3), channel_id=1, source_target_pairs={{0,1},{1,0},{2,3},{3,2},{4,5},{5,4},{6,7},{7,6},{8,9},{9,8},{10,11... | collective-permute-start | bytes 393224 | tf_op jit(solution)/shard_map/ppermute | solution.py:34
  3.5 10.8 %collective-permute-start.1 = (bf16[128,1024]{1,0:T(8,128)(2,1)S(1)}, bf16[128,1024]{1,0:T(8,128)(2,1)}, u32[]{:S(2)}, u32[]{:S(2)}) collective-permute-start(bf16[128,1024]{1,0:T(8,128)(2,1)S(1)} %get-tuple-element.16), channel_id=1, source_target_pairs={{0,6},{2,4},{4,2},{6,0},{1,7},{3,5},{5,3},{7,1},{8,14},{10,12},{12... | collective-permute-start | bytes 786440 | tf_op jit(solution)/shard_map/ppermute | solution.py:25
  7.1 12.8 %collective-permute-start.3 = (bf16[128,1024]{1,0:T(8,128)(2,1)S(1)}, bf16[128,1024]{1,0:T(8,128)(2,1)S(1)}, u32[]{:S(2)}, u32[]{:S(2)}) collective-permute-start(bf16[128,1024]{1,0:T(8,128)(2,1)S(1)} %get-tuple-element.17), channel_id=1, source_target_pairs={{0,2},{2,0},{4,6},{6,4},{1,3},{3,1},{5,7},{7,5},{8,10},{10,8},{12,... | collective-permute-start | bytes 786440 | tf_op jit(solution)/shard_map/ppermute | solution.py:25
  7.6 13.3 %collective-permute-start.5 = (bf16[128,1024]{1,0:T(8,128)(2,1)S(1)}, bf16[128,1024]{1,0:T(8,128)(2,1)S(1)}, u32[]{:S(2)}, u32[]{:S(2)}) collective-permute-start(bf16[128,1024]{1,0:T(8,128)(2,1)S(1)} %get-tuple-element.18), channel_id=1, source_target_pairs={{0,4},{2,6},{4,0},{6,2},{1,5},{3,7},{5,1},{7,3},{8,12},{10,14},{12... | collective-permute-start | bytes 786440 | tf_op jit(solution)/shard_map/ppermute | solution.py:25
  7.7 1.8 %copy-start.3 = (s32[1,1,512]{2,1,0:T(1,128)S(1)}, s32[1,1,512]{2,1,0:T(1,128)}, u32[]{:S(2)}) copy-start(s32[1,1,512]{2,1,0:T(1,128)} %param.13) | copy-start | bytes 6148
  7.7 2.5 %copy-start.4 = (s32[1,1,8]{2,1,0:T(1,128)S(1)}, s32[1,1,8]{2,1,0:T(1,128)}, u32[]{:S(2)}) copy-start(s32[1,1,8]{2,1,0:T(1,128)} %param.12) | copy-start | bytes 100
  8.7 16.3 %collective-permute-start.7 = (bf16[128,256]{1,0:T(8,128)(2,1)}, bf16[128,256]{1,0:T(8,128)(2,1)S(1)}, u32[]{:S(2)}, u32[]{:S(2)}) collective-permute-start(bf16[128,256]{1,0:T(8,128)(2,1)} %convolution_convert_fusion.7), channel_id=1, source_target_pairs={{0,1},{1,0},{2,3},{3,2},{4,5},{5,4},{6,7},{7,6},{8,9},{9,8},{10,11... | collective-permute-start | bytes 196616 | tf_op jit(solution)/shard_map/ppermute | solution.py:34
  14.4 9.5 %collective-permute-start.11 = (f32[1,1152]{1,0:T(1,128)S(1)}, f32[1,1152]{1,0:T(1,128)S(1)}, u32[]{:S(2)}, u32[]{:S(2)}) collective-permute-start(f32[1,1152]{1,0:T(1,128)S(1)} %pad_maximum_fusion), channel_id=1, source_target_pairs={{0,1},{1,0},{2,3},{3,2},{4,5},{5,4},{6,7},{7,6},{8,9},{9,8},{10,11... | collective-permute-start | bytes 13832 | tf_op jit(solution)/shard_map/ppermute | solution.py:260
  19.9 19.4 %collective-permute-start.2 = (bf16[128,512]{1,0:T(8,128)(2,1)S(1)}, bf16[128,512]{1,0:T(8,128)(2,1)S(1)}, u32[]{:S(2)}, u32[]{:S(2)}) collective-permute-start(bf16[128,512]{1,0:T(8,128)(2,1)S(1)} %convolution_convert_fusion.2), channel_id=1, source_target_pairs={{0,7},{1,6},{2,5},{3,4},{4,3},{5,2},{6,1},{7,0},{8,15},{9,14},{10,... | collective-permute-start | bytes 393224 | tf_op jit(solution)/shard_map/ppermute | solution.py:34
  20.9 7.0 %collective-permute-start.8 = (bf16[128,256]{1,0:T(8,128)(2,1)S(1)}, bf16[128,256]{1,0:T(8,128)(2,1)S(1)}, u32[]{:S(2)}, u32[]{:S(2)}) collective-permute-start(bf16[128,256]{1,0:T(8,128)(2,1)S(1)} %convolution_convert_fusion.6), channel_id=1, source_target_pairs={{0,7},{1,6},{2,5},{3,4},{4,3},{5,2},{6,1},{7,0},{8,15},{9,14},{10,... | collective-permute-start | bytes 196616 | tf_op jit(solution)/shard_map/ppermute | solution.py:34
  23.9 4.4 %collective-permute-start.9 = (bf16[128,256]{1,0:T(8,128)(2,1)S(1)}, bf16[128,256]{1,0:T(8,128)(2,1)S(1)}, u32[]{:S(2)}, u32[]{:S(2)}) collective-permute-start(bf16[128,256]{1,0:T(8,128)(2,1)S(1)} %convolution_convert_fusion.5), channel_id=1, source_target_pairs={{0,3},{1,2},{2,1},{3,0},{4,7},{5,6},{6,5},{7,4},{8,11},{9,10},{10,... | collective-permute-start | bytes 196616 | tf_op jit(solution)/shard_map/ppermute | solution.py:34
  25.0 15.7 %collective-permute-start.4 = (bf16[128,512]{1,0:T(8,128)(2,1)S(1)}, bf16[128,512]{1,0:T(8,128)(2,1)S(1)}, u32[]{:S(2)}, u32[]{:S(2)}) collective-permute-start(bf16[128,512]{1,0:T(8,128)(2,1)S(1)} %convolution_convert_fusion.1), channel_id=1, source_target_pairs={{0,3},{1,2},{2,1},{3,0},{4,7},{5,6},{6,5},{7,4},{8,11},{9,10},{10,... | collective-permute-start | bytes 393224 | tf_op jit(solution)/shard_map/ppermute | solution.py:34
  28.0 12.7 %collective-permute-start.6 = (bf16[128,512]{1,0:T(8,128)(2,1)S(1)}, bf16[128,512]{1,0:T(8,128)(2,1)S(1)}, u32[]{:S(2)}, u32[]{:S(2)}) collective-permute-start(bf16[128,512]{1,0:T(8,128)(2,1)S(1)} %convolution_convert_fusion), channel_id=1, source_target_pairs={{0,5},{1,4},{2,7},{3,6},{4,1},{5,0},{6,3},{7,2},{8,13},{9,12},{10,... | collective-permute-start | bytes 393224 | tf_op jit(solution)/shard_map/ppermute | solution.py:34
  28.3 6.7 %collective-permute-start.10 = (bf16[128,256]{1,0:T(8,128)(2,1)S(1)}, bf16[128,256]{1,0:T(8,128)(2,1)S(1)}, u32[]{:S(2)}, u32[]{:S(2)}) collective-permute-start(bf16[128,256]{1,0:T(8,128)(2,1)S(1)} %convolution_convert_fusion.4), channel_id=1, source_target_pairs={{0,5},{1,4},{2,7},{3,6},{4,1},{5,0},{6,3},{7,2},{8,13},{9,12},{10,... | collective-permute-start | bytes 196616 | tf_op jit(solution)/shard_map/ppermute | solution.py:34
  35.1 6.5 %collective-permute-start.12 = (bf16[128,256]{1,0:T(8,128)(2,1)S(1)}, bf16[128,256]{1,0:T(8,128)(2,1)S(1)}, u32[]{:S(2)}, u32[]{:S(2)}) collective-permute-start(bf16[128,256]{1,0:T(8,128)(2,1)S(1)} %shard_map.75.refs_4_), channel_id=1, source_target_pairs={{0,8},{8,16},{16,24},{24,0},{1,9},{9,17},{17,25},{25,1},{2,10},{10... | collective-permute-start | bytes 196616 | tf_op jit(solution)/shard_map/ppermute | solution.py:38
  36.7 7.3 %collective-permute-start.13 = (bf16[128,256]{1,0:T(8,128)(2,1)S(1)}, bf16[128,256]{1,0:T(8,128)(2,1)S(1)}, u32[]{:S(2)}, u32[]{:S(2)}) collective-permute-start(bf16[128,256]{1,0:T(8,128)(2,1)S(1)} %shard_map.75.refs_4_), channel_id=1, source_target_pairs={{0,16},{8,24},{16,0},{24,8},{1,17},{9,25},{17,1},{25,9},{2,18},{10... | collective-permute-start | bytes 196616 | tf_op jit(solution)/shard_map/ppermute | solution.py:38
  39.3 4.7 %collective-permute-start.14 = (bf16[128,256]{1,0:T(8,128)(2,1)S(1)}, bf16[128,256]{1,0:T(8,128)(2,1)S(1)}, u32[]{:S(2)}, u32[]{:S(2)}) collective-permute-start(bf16[128,256]{1,0:T(8,128)(2,1)S(1)} %shard_map.75.refs_4_), channel_id=1, source_target_pairs={{0,24},{8,0},{16,8},{24,16},{1,25},{9,1},{17,9},{25,17},{2,26},{10... | collective-permute-start | bytes 196616 | tf_op jit(solution)/shard_map/ppermute | solution.py:38
where the time goes:
time: 46.3 us; the launch traced here: 46 us
  waiting for transfers between devices  16.9 us (37%)
  starting transfers between devices  16.3 us (35%)
  matrix products  5.77 us (12%)
  Pallas kernels  3.1 us (7%)
  local copies, waits for them, and re-layouts  2.51 us (5%)
  other arithmetic  1.28 us (3%)
    ppermute x8, waiting for transfers between devices, to_next_section(): return lax.ppermute(x, ('dp', 'section'), moves)  6.97 us
    ppermute x8, starting transfers between devices, to_next_section(): return lax.ppermute(x, ('dp', 'section'), moves)  6.58 us
    ppermute x3, waiting for transfers between devices, swap_dp(): lax.ppermute(x, 'dp', [(i, partner(i, step, count)) for i in range(count)])  6.51 us
    ppermute x3, starting transfers between devices, shift_ctx(): return lax.ppermute(x, 'ctx', [(i, (i + by) % ring) for i in range(ring)])  5.57 us
    ppermute x3, starting transfers between devices, swap_dp(): lax.ppermute(x, 'dp', [(i, partner(i, step, count)) for i in range(count)])  4.15 us
    ppermute x3, waiting for transfers between devices, shift_ctx(): return lax.ppermute(x, 'ctx', [(i, (i + by) % ring) for i in range(ring)])  3.39 us
    dot_general x4, matrix products, local(): part = jnp.dot(arrived[k], kv_weight, preferred_element_type=jnp.float32)  3.1 us
    pallas_call x4, Pallas kernels, local_call(): pl.pallas_call(kernel, out_shape=out_shape, in_specs=[pl.BlockSpec(memory...  3.1 us
  transfers between devices with their start and end apart: 15, of which 7 were waited for; matrix products, arithmetic and copies ran while one was open for 16% of the time, Pallas kernels for 1%

commit v1 on v0

--- a/solution.py
+++ b/solution.py
@@ -2,6 +2,7 @@
 
 import jax
 import jax.numpy as jnp
+import numpy as np
 from jax import lax
 from jax.experimental import pallas as pl
 from jax.experimental.pallas import tpu as pltpu
@@ -12,6 +13,7 @@
 MASKED = -1e30
 LOG2E = 1.4426950408889634
 DIRECT = 8
+DOCS = 4
 GRANT = 8 << 20
 
 
@@ -38,27 +40,34 @@
     return lax.ppermute(x, "ctx", [(i, (i + by) % ring) for i in range(ring)])
 
 
-def local_call(kernel, out_shape, args, in_spaces, scratch=()):
+def on_chip(shape, dtype):
+    return pltpu.VMEM(shape, dtype)
+
+
+def local_call(kernel, out_shape, args, in_specs, **more):
+    in_specs = [s if isinstance(s, pl.BlockSpec) else pl.BlockSpec(memory_space=s) for s in in_specs]
+    if "out_specs" not in more:
+        whole = pl.BlockSpec(memory_space=pltpu.VMEM)
+        more["out_specs"] = [whole] * len(out_shape) if isinstance(out_shape, list) else whole
     return pl.pallas_call(
         kernel,
         out_shape=out_shape,
-        in_specs=[pl.BlockSpec(memory_space=s) for s in in_spaces],
-        out_specs=jax.tree.map(
-            lambda s: pl.BlockSpec(memory_space=pltpu.VMEM), out_shape
-        ),
-        scratch_shapes=scratch,
+        in_specs=in_specs,
         compiler_params=pltpu.CompilerParams(vmem_limit_bytes=GRANT),
+        **more,
     )(*args)
 
 
-def cut_kernel(count, slots_ref, rows_ref, *refs):
+def cut_kernel(count, sequence, here_ref, rows_ref, *refs):
     out_refs, sem = refs[:count], refs[count]
     width = out_refs[0].shape[1]
     copies = []
-    for k in range(count):
-        begin = pl.multiple_of(slots_ref[k] * width, width)
+    for slot, k in enumerate(sequence):
+        begin = pl.multiple_of(partner(here_ref[0], k, count) * width, width)
         copies.append(
-            pltpu.make_async_copy(rows_ref.at[:, pl.ds(begin, width)], out_refs[k], sem.at[k])
+            pltpu.make_async_copy(
+                rows_ref.at[:, pl.ds(begin, width)], out_refs[slot], sem.at[slot]
+            )
         )
     for copy in copies:
         copy.start()
@@ -66,16 +75,69 @@
         copy.wait()
 
 
-def cut(rows, slots, count):
+def cut(rows, here, count, sequence):
     height, features = rows.shape
-    shape = jax.ShapeDtypeStruct((height, features // count), jnp.bfloat16)
-    return local_call(
-        functools.partial(cut_kernel, count),
-        [shape] * count,
-        (slots, rows),
-        (pltpu.SMEM, pl.ANY),
-        [pltpu.SemaphoreType.DMA((count,))],
-    )
+    rows = pltpu.with_memory_space_constraint(rows, pltpu.HBM)
+    return local_call(
+        functools.partial(cut_kernel, count, sequence),
+        [on_chip((height, features // count), jnp.bfloat16)] * count,
+        (here, rows),
+        (pltpu.SMEM, pltpu.HBM),
+        scratch_shapes=[pltpu.SemaphoreType.DMA((count,))],
+    )
+
+
+def meta_kernel(docs_count, blocks, rows_ref, order_ref, docs_ref, out_ref):
+    height = rows_ref.shape[0]
+    length = docs_ref.shape[1]
+    block_rows = length // blocks
+    squares = jnp.zeros((height, 128), jnp.float32)
+    for i in range(rows_ref.shape[1] // 128):
+        part = rows_ref[:, i * 128 : (i + 1) * 128].astype(jnp.float32)
+        squares = squares + part * part
+    mean = jnp.sum(squares, axis=1, keepdims=True) / rows_ref.shape[1]
+    scale = lax.rsqrt(mean + EPSILON)
+    down = lax.broadcasted_iota(jnp.int32, (height, height), 0)
+    across = lax.broadcasted_iota(jnp.int32, (height, height), 1)
+    out_ref[:, 2 * length :] = jnp.sum(
+        jnp.where(down == across, scale, 0.0), axis=0, keepdims=True
+    )
+    lane = lax.broadcasted_iota(jnp.int32, (1, length), 1)
+    block = jnp.zeros((1, length), jnp.int32)
+    for b in range(blocks):
+        inside = (lane >= b * block_rows) & (lane < (b + 1) * block_rows)
+        block = jnp.where(inside, order_ref[0, b] * block_rows - b * block_rows, block)
+    positions = (block + lane).astype(jnp.float32)
+    number = jnp.zeros((1, length), jnp.float32)
+    for d in range(1, docs_count):
+        start = jnp.sum((docs_ref[...] < d).astype(jnp.float32), axis=1, keepdims=True)
+        number = number + (positions >= start).astype(jnp.float32)
+    out_ref[:, :length] = positions
+    out_ref[:, length : 2 * length] = number
+
+
+def describe(rows, order, docs):
+    height, length, blocks = rows.shape[0], docs.shape[1], order.shape[1]
+    rows = pltpu.with_memory_space_constraint(rows, pltpu.HBM)
+    return local_call(
+        functools.partial(meta_kernel, DOCS, blocks),
+        on_chip((1, 2 * length + height), jnp.float32),
+        (rows, order, docs),
+        (pltpu.VMEM, pltpu.SMEM, pltpu.VMEM),
+    )
+
+
+def describe_long(rows, order, docs):
+    length, blocks = docs.shape[1], order.shape[1]
+    wide = rows.astype(jnp.float32)
+    scale = lax.rsqrt(jnp.mean(wide * wide, axis=-1) + EPSILON)
+    within = jnp.arange(length // blocks, dtype=jnp.int32)
+    positions = (order[0][:, None] * (length // blocks) + within[None, :]).reshape(-1)
+    number = sum(
+        (positions >= jnp.sum((docs[0] < d).astype(jnp.int32))).astype(jnp.float32)
+        for d in range(1, DOCS)
+    )
+    return jnp.concatenate([positions.astype(jnp.float32), number, scale])[None]
 
 
 def column(row):
@@ -103,12 +165,61 @@
 
 
 def tables(at, meta, freqs, rows, size, length):
-    square = jax.ShapeDtypeStruct((rows, size), jnp.float32)
+    square = on_chip((rows, size), jnp.float32)
     return local_call(
         functools.partial(tables_kernel, length),
-        [square] * 5 + [jax.ShapeDtypeStruct((rows, length), jnp.float32)],
+        [square] * 5 + [on_chip((rows, length), jnp.float32)],
         (at, meta, freqs),
         (pltpu.SMEM, pltpu.VMEM, pltpu.VMEM),
+    )
+
+
+def scale_kernel(here_ref, gain_ref, query_ref, key_ref, value_ref, kv_out, q_out):
+    rows, size = key_ref.shape
+    step = pl.program_id(0)
+    for i in range(rows // size):
+        begin = ((here_ref[0] * pl.num_programs(0) + step) * (rows // size) + i) * size
+        gain = column(gain_ref[:, pl.ds(pl.multiple_of(begin, size), size)])
+        part = slice(i * size, (i + 1) * size)
+        target = pl.ds(pl.multiple_of(step * rows + i * size, size), size)
+        kv_out[target, :size] = (key_ref[part, :].astype(jnp.float32) * gain).astype(jnp.bfloat16)
+        kv_out[target, size:] = (value_ref[part, :].astype(jnp.float32) * gain).astype(jnp.bfloat16)
+        q_out[target, :] = (query_ref[part, :].astype(jnp.float32) * gain).astype(jnp.bfloat16)
+
+
+def scale_weights(here, gain, query_weight, key_weight, value_weight):
+    depth, size = key_weight.shape
+    width = query_weight.shape[1]
+    steps = 4
+    rows = depth // steps
+    held = [pltpu.with_memory_space_constraint(w, pltpu.HBM) for w in (query_weight, key_weight, value_weight)]
+    return local_call(
+        scale_kernel,
+        [on_chip((depth, 2 * size), jnp.bfloat16), on_chip((depth, width), jnp.bfloat16)],
+        (here, gain, *held),
+        [
+            pltpu.SMEM,
+            pltpu.VMEM,
+            pl.BlockSpec((rows, width), lambda i: (i, 0)),
+            pl.BlockSpec((rows, size), lambda i: (i, 0)),
+            pl.BlockSpec((rows, size), lambda i: (i, 0)),
+        ],
+        grid=(steps,),
+    )
+
+
+def dot_kernel(x_ref, w_ref, out_ref):
+    out_ref[...] = jnp.dot(
+        x_ref[...], w_ref[...], preferred_element_type=jnp.float32
+    ).astype(jnp.bfloat16)
+
+
+def project(x, weight):
+    return local_call(
+        dot_kernel,
+        on_chip((x.shape[0], weight.shape[1]), jnp.bfloat16),
+        (x, weight),
+        [pltpu.VMEM] * 2,
     )
 
 
@@ -134,10 +245,7 @@
 def mix(parts, kcos, ksin, level):
     args = (*parts, kcos, ksin, level)
     return local_call(
-        mix_kernel,
-        jax.ShapeDtypeStruct(parts[0].shape, jnp.bfloat16),
-        args,
-        [pltpu.VMEM] * len(args),
+        mix_kernel, on_chip(parts[0].shape, jnp.bfloat16), args, [pltpu.VMEM] * len(args)
     )
 
 
@@ -229,54 +337,34 @@
     rows_here = tokens[0, 0]
     row_count = rows_here.shape[0]
     length = doc_ids.shape[2]
-    blocks = block_order.shape[2]
-    block_rows = length // blocks
     size = key_weight.shape[2]
-    depth = key_weight.shape[1]
-    here, at = lax.axis_index("dp"), lax.axis_index("ctx").astype(jnp.int32)[None]
-    sequence = list(range(count - 1, -1, -1))
-    sequence = [sequence[0], *sequence[-2:0:-1], sequence[-1]]
-    slots = jnp.stack([partner(here, k, count) for k in sequence]).astype(jnp.int32)
-    slabs = cut(rows_here, slots, count)
+    here = lax.axis_index("dp").astype(jnp.int32)[None]
+    at = lax.axis_index("ctx").astype(jnp.int32)[None]
+    sequence = [count - 1, *range(1, count - 1), 0]
+    slabs = cut(rows_here, here, count, sequence)
 
     arrived = {}
     for k, slab in zip(sequence, slabs):
         arrived[k] = swap_dp(slab, k, count) if k else slab
 
-    wide = rows_here.astype(jnp.float32)
-    scale = lax.rsqrt(jnp.mean(wide * wide, axis=-1) + EPSILON)
-    order = block_order[0, 0]
-    pick = (order[:, None] == jnp.arange(blocks, dtype=jnp.int32)[None, :]).astype(jnp.int32)
-    row_docs = jnp.sum(pick[:, :, None] * doc_ids[0, 0].reshape(1, blocks, block_rows), axis=1)
-    positions = order[:, None] * block_rows + jnp.arange(block_rows, dtype=jnp.int32)[None, :]
-    meta = jnp.concatenate(
-        [
-            positions.reshape(1, -1).astype(jnp.float32),
-            row_docs.reshape(1, -1).astype(jnp.float32),
-            scale[None],
-        ],
-        axis=1,
-    )
+    tell = describe if ring <= DIRECT else describe_long
+    meta = tell(rows_here, block_order[0], doc_ids[0])
     meta = lax.ppermute(meta, "section", [(i, (i + 1) % sections) for i in range(sections)])
 
-    half = size // 2
-    freqs = ROPE_BASE ** (-jnp.arange(half, dtype=jnp.float32) * 2.0 / size)
-    freqs = jnp.concatenate([freqs, freqs])[None]
+    freqs = ROPE_BASE ** (-np.arange(size // 2, dtype=np.float64) * 2.0 / size)
+    freqs = jnp.asarray(np.concatenate([freqs, freqs])[None], jnp.float32)
     kcos, ksin, qcos, qsin, level, bias = tables(at, meta, freqs, row_count, size, length)
 
-    gain = lax.dynamic_slice_in_dim(norm_gain[0], here * depth, depth)[:, None]
-    kv_weight = jnp.concatenate([key_weight[0], value_weight[0]], axis=1)
-    kv_weight = (kv_weight.astype(jnp.float32) * gain).astype(jnp.bfloat16)
-    q_weight = (query_weight[0].astype(jnp.float32) * gain).astype(jnp.bfloat16)
+    kv_weight, q_weight = scale_weights(
+        here, norm_gain, query_weight[0], key_weight[0], value_weight[0]
+    )
 
     kv_parts, q_parts = [], []
-    last = [sequence[-1], *sequence[:-1]]
-    for k in last:
-        part = jnp.dot(arrived[k], kv_weight, preferred_element_type=jnp.float32)
-        kv_parts.append(to_next_section(part.astype(jnp.bfloat16), k, count, sections))
-    for k in last:
-        part = jnp.dot(arrived[k], q_weight, preferred_element_type=jnp.float32)
-        q_parts.append(to_next_section(part.astype(jnp.bfloat16), k, count, sections))
+    for k in [sequence[-1], *sequence[:-1]]:
+        part = project(arrived[k], kv_weight)
+        kv_parts.append(to_next_section(part, k, count, sections))
+        part = project(arrived[k], q_weight)
+        q_parts.append(to_next_section(part, k, count, sections))
 
     kv = mix(kv_parts, kcos, ksin, level)
     if ring <= DIRECT:

time: 46.3 us -> 40.2 us (0.87)
  Pallas kernels: 3.1 us -> 9.9 us
  matrix products: 5.77 us -> 0 us
  waiting for transfers between devices: 16.9 us -> 11.2 us
  other arithmetic: 1.28 us -> 0 us
  local copies, waits for them, and re-layouts: 2.51 us -> 1.31 us
  starting transfers between devices: 16.3 us -> 17.4 us
    pallas_call x4 -> x14, Pallas kernels: 3.1 us -> 9.9 us  [local_call(): pl.pallas_call(kernel, out_shape=out_shape, in_specs=in_specs, compiler_p...]
    dot_general x8 -> x0, matrix products: 5.77 us -> none  [the longest x4 3.1 us: local(): part = jnp.dot(arrived[k], kv_weight, preferred_element_type=jnp.float32)]
    ppermute x8, waiting for transfers between devices: 6.97 us -> 2.2 us  [to_next_section(): return lax.ppermute(x, ('dp', 'section'), moves)]
    ppermute x3, waiting for transfers between devices: 6.51 us -> 4.45 us  [swap_dp(): lax.ppermute(x, 'dp', [(i, partner(i, step, count)) for i in range(count)])]
    ppermute x3, waiting for transfers between devices: 3.39 us -> 4.52 us  [shift_ctx(): return lax.ppermute(x, 'ctx', [(i, (i + by) % ring) for i in range(ring)])]
    unnamed x17 -> x8, local copies, waits for them, and re-layouts: 2.27 us -> 1.31 us
    unnamed x1 -> x0, other arithmetic: 0.59 us -> none
    ppermute x8, starting transfers between devices: 6.58 us -> 7.15 us  [to_next_section(): return lax.ppermute(x, ('dp', 'section'), moves)]
  transfers between devices with their start and end apart: 15 -> 15, of which waited for: 7 -> 5; matrix products, arithmetic and copies ran while one was open for 16% -> 0% of each run, Pallas kernels for 1% -> 17%
where the time goes in v1:
time: 40.2 us; the launch traced here: 39.9 us
  starting transfers between devices  17.4 us (43%)
  waiting for transfers between devices  11.2 us (28%)
  Pallas kernels  9.9 us (25%)
  local copies, waits for them, and re-layouts  1.31 us (3%)
    pallas_call x14, Pallas kernels, local_call(): pl.pallas_call(kernel, out_shape=out_shape, in_specs=in_specs, compiler_p...  9.9 us
    ppermute x8, starting transfers between devices, to_next_section(): return lax.ppermute(x, ('dp', 'section'), moves)  7.15 us
    ppermute x3, starting transfers between devices, shift_ctx(): return lax.ppermute(x, 'ctx', [(i, (i + by) % ring) for i in range(ring)])  5.57 us
    ppermute x3, starting transfers between devices, swap_dp(): lax.ppermute(x, 'dp', [(i, partner(i, step, count)) for i in range(count)])  4.6 us
    ppermute x3, waiting for transfers between devices, shift_ctx(): return lax.ppermute(x, 'ctx', [(i, (i + by) % ring) for i in range(ring)])  4.52 us
    ppermute x3, waiting for transfers between devices, swap_dp(): lax.ppermute(x, 'dp', [(i, partner(i, step, count)) for i in range(count)])  4.45 us
    ppermute x8, waiting for transfers between devices, to_next_section(): return lax.ppermute(x, ('dp', 'section'), moves)  2.2 us
    unnamed x8, local copies, waits for them, and re-layouts  1.31 us
  transfers between devices with their start and end apart: 15, of which 5 were waited for; matrix products, arithmetic and copies ran while one was open for 0% of the time, Pallas kernels for 17%

profile of v1, /device:TPU:0, one launch (start us, length us, event | category | flops | bytes accessed | tf_op | source)
XLA Modules:
  0.0 39.9 jit_solution(13532965586972233594)
XLA Ops:
  0.0 1.2 %shard_map.82 = (bf16[128,1024]{1,0:T(8,128)(2,1)S(1)}, bf16[128,1024]{1,0:T(8,128)(2,1)S(1)}, bf16[128,1024]{1,0:T(8,128)(2,1)S(1)}, bf16[128,1024]{1,0:T(8,128)(2,1)S(1)}) custom-call(s32[1]{0:T(128)} %bitcast.1.here_ref, bf16[128,4096]{1,0:T(8,128)(2,1)} %bitcast.11), custom_call_target="tpu_custom_call" | custom-call | tf_op jit(solution)/shard_map/pallas_call | solution.py:52
  1.2 3.1 %collective-permute-start.5 = (bf16[128,1024]{1,0:T(8,128)(2,1)S(1)}, bf16[128,1024]{1,0:T(8,128)(2,1)S(1)}, u32[]{:S(2)}, u32[]{:S(2)}) collective-permute-start(bf16[128,1024]{1,0:T(8,128)(2,1)S(1)} %get-tuple-element.21), channel_id=1, source_target_pairs={{0,4},{2,6},{4,0},{6,2},{1,5},{3,7},{5,1},{7,3},{8,12},{10,14},{12... | collective-permute-start | bytes 786440 | tf_op jit(solution)/shard_map/ppermute | solution.py:27
  4.3 1.4 %collective-permute-start.1 = (bf16[128,1024]{1,0:T(8,128)(2,1)S(1)}, bf16[128,1024]{1,0:T(8,128)(2,1)S(1)}, u32[]{:S(2)}, u32[]{:S(2)}) collective-permute-start(bf16[128,1024]{1,0:T(8,128)(2,1)S(1)} %get-tuple-element.19), channel_id=1, source_target_pairs={{0,6},{2,4},{4,2},{6,0},{1,7},{3,5},{5,3},{7,1},{8,14},{10,12},{12... | collective-permute-start | bytes 786440 | tf_op jit(solution)/shard_map/ppermute | solution.py:27
  5.8 0.6 %copy-done.1 = s32[1,1,512]{2,1,0:T(1,128)S(1)} copy-done((s32[1,1,512]{2,1,0:T(1,128)S(1)}, s32[1,1,512]{2,1,0:T(1,128)}, u32[]{:S(2)}) %copy-start.1) | copy-done | bytes 2072
  6.5 1.6 %shard_map.92 = f32[1,1152]{1,0:T(1,128)S(1)} custom-call(bf16[128,4096]{1,0:T(8,128)(2,1)} %bitcast.12, s32[1,8]{1,0:T(1,128)S(1)} %bitcast.10, s32[1,512]{1,0:T(1,128)S(1)} %bitcast.9), custom_call_target="tpu_custom_call" | custom-call | tf_op jit(solution)/shard_map/pallas_call | solution.py:52
  8.1 2.5 %shard_map.83 = (bf16[1024,256]{1,0:T(8,128)(2,1)S(1)}, bf16[1024,512]{1,0:T(8,128)(2,1)S(1)}) custom-call(s32[1]{0:T(128)} %bitcast.1.here_ref, f32[1,4096]{1,0:T(1,128)S(1)} %copy-done, bf16[1024,512]{1,0:T(8,128)(2,1)} %bitcast.13, bf16[1024,128]{1,0:T(8,128)(2,1)} %bitcast.14, bf16[1024,128]{1,0:T(8,128)(2,1)} %bitcast.15), custom_call_target="tpu_custom_call" | custom-call | tf_op jit(solution)/shard_map/pallas_call | solution.py:52
  10.9 0.5 %collective-permute-start.7 = (bf16[128,256]{1,0:T(8,128)(2,1)S(1)}, bf16[128,256]{1,0:T(8,128)(2,1)S(1)}, u32[]{:S(2)}, u32[]{:S(2)}) collective-permute-start(bf16[128,256]{1,0:T(8,128)(2,1)S(1)} %shard_map.88), channel_id=1, source_target_pairs={{0,1},{1,0},{2,3},{3,2},{4,5},{5,4},{6,7},{7,6},{8,9},{9,8},{10,11... | collective-permute-start | bytes 196616 | tf_op jit(solution)/shard_map/ppermute | solution.py:36
  11.8 4.4 %collective-permute-done.5.x_ref = bf16[128,1024]{1,0:T(8,128)(2,1)S(1)} collective-permute-done((bf16[128,1024]{1,0:T(8,128)(2,1)S(1)}, bf16[128,1024]{1,0:T(8,128)(2,1)S(1)}, u32[]{:S(2)}, u32[]{:S(2)}) %collective-permute-start.5) | collective-permute-done | bytes 262176 | tf_op jit(solution)/shard_map/ppermute | solution.py:27
  16.5 0.4 %collective-permute-start.10 = (bf16[128,256]{1,0:T(8,128)(2,1)S(1)}, bf16[128,256]{1,0:T(8,128)(2,1)S(1)}, u32[]{:S(2)}, u32[]{:S(2)}) collective-permute-start(bf16[128,256]{1,0:T(8,128)(2,1)S(1)} %shard_map.91), channel_id=1, source_target_pairs={{0,5},{1,4},{2,7},{3,6},{4,1},{5,0},{6,3},{7,2},{8,13},{9,12},{10,... | collective-permute-start | bytes 196616 | tf_op jit(solution)/shard_map/ppermute | solution.py:36
  17.1 2.6 %collective-permute-start.8 = (bf16[128,256]{1,0:T(8,128)(2,1)S(1)}, bf16[128,256]{1,0:T(8,128)(2,1)S(1)}, u32[]{:S(2)}, u32[]{:S(2)}) collective-permute-start(bf16[128,256]{1,0:T(8,128)(2,1)S(1)} %shard_map.89), channel_id=1, source_target_pairs={{0,7},{1,6},{2,5},{3,4},{4,3},{5,2},{6,1},{7,0},{8,15},{9,14},{10,... | collective-permute-start | bytes 196616 | tf_op jit(solution)/shard_map/ppermute | solution.py:36
  20.1 1.6 %collective-permute-start.2 = (bf16[128,512]{1,0:T(8,128)(2,1)S(1)}, bf16[128,512]{1,0:T(8,128)(2,1)S(1)}, u32[]{:S(2)}, u32[]{:S(2)}) collective-permute-start(bf16[128,512]{1,0:T(8,128)(2,1)S(1)} %shard_map.85), channel_id=1, source_target_pairs={{0,7},{1,6},{2,5},{3,4},{4,3},{5,2},{6,1},{7,0},{8,15},{9,14},{10,... | collective-permute-start | bytes 393224 | tf_op jit(solution)/shard_map/ppermute | solution.py:36
  22.0 1.2 %collective-permute-start.9 = (bf16[128,256]{1,0:T(8,128)(2,1)S(1)}, bf16[128,256]{1,0:T(8,128)(2,1)S(1)}, u32[]{:S(2)}, u32[]{:S(2)}) collective-permute-start(bf16[128,256]{1,0:T(8,128)(2,1)S(1)} %shard_map.90), channel_id=1, source_target_pairs={{0,3},{1,2},{2,1},{3,0},{4,7},{5,6},{6,5},{7,4},{8,11},{9,10},{10,... | collective-permute-start | bytes 196616 | tf_op jit(solution)/shard_map/ppermute | solution.py:36
  23.5 0.3 shard_map.87
  23.9 0.6 %collective-permute-start.4 = (bf16[128,512]{1,0:T(8,128)(2,1)S(1)}, bf16[128,512]{1,0:T(8,128)(2,1)S(1)}, u32[]{:S(2)}, u32[]{:S(2)}) collective-permute-start(bf16[128,512]{1,0:T(8,128)(2,1)S(1)} %shard_map.86), channel_id=1, source_target_pairs={{0,3},{1,2},{2,1},{3,0},{4,7},{5,6},{6,5},{7,4},{8,11},{9,10},{10,... | collective-permute-start | bytes 393224 | tf_op jit(solution)/shard_map/ppermute | solution.py:36
  24.6 0.7 %copy-done.3 = f32[1,128]{1,0:T(1,128)S(1)} copy-done((f32[1,128]{1,0:T(1,128)S(1)}, f32[1,128]{1,0:T(1,128)}, u32[]{:S(2)}) %copy-start.3) | copy-done | bytes 536
  25.2 0.3 shard_map.93
  25.6 2.2 %collective-permute-done.9.refs_2_ = bf16[128,256]{1,0:T(8,128)(2,1)S(1)} collective-permute-done((bf16[128,256]{1,0:T(8,128)(2,1)S(1)}, bf16[128,256]{1,0:T(8,128)(2,1)S(1)}, u32[]{:S(2)}, u32[]{:S(2)}) %collective-permute-start.9) | collective-permute-done | bytes 65568 | tf_op jit(solution)/shard_map/ppermute | solution.py:36
  27.9 1.6 %collective-permute-start.12 = (bf16[128,256]{1,0:T(8,128)(2,1)S(1)}, bf16[128,256]{1,0:T(8,128)(2,1)S(1)}, u32[]{:S(2)}, u32[]{:S(2)}) collective-permute-start(bf16[128,256]{1,0:T(8,128)(2,1)S(1)} %shard_map.94.refs_4_), channel_id=1, source_target_pairs={{0,8},{8,16},{16,24},{24,0},{1,9},{9,17},{17,25},{25,1},{2,10},{10... | collective-permute-start | bytes 196616 | tf_op jit(solution)/shard_map/ppermute | solution.py:40
  29.5 2.6 %collective-permute-start.13 = (bf16[128,256]{1,0:T(8,128)(2,1)S(1)}, bf16[128,256]{1,0:T(8,128)(2,1)S(1)}, u32[]{:S(2)}, u32[]{:S(2)}) collective-permute-start(bf16[128,256]{1,0:T(8,128)(2,1)S(1)} %shard_map.94.refs_4_), channel_id=1, source_target_pairs={{0,16},{8,24},{16,0},{24,8},{1,17},{9,25},{17,1},{25,9},{2,18},{10... | collective-permute-start | bytes 196616 | tf_op jit(solution)/shard_map/ppermute | solution.py:40
  32.1 1.3 %collective-permute-start.14 = (bf16[128,256]{1,0:T(8,128)(2,1)S(1)}, bf16[128,256]{1,0:T(8,128)(2,1)S(1)}, u32[]{:S(2)}, u32[]{:S(2)}) collective-permute-start(bf16[128,256]{1,0:T(8,128)(2,1)S(1)} %shard_map.94.refs_4_), channel_id=1, source_target_pairs={{0,24},{8,0},{16,8},{24,16},{1,25},{9,1},{17,9},{25,17},{2,26},{10... | collective-permute-start | bytes 196616 | tf_op jit(solution)/shard_map/ppermute | solution.py:40
  33.4 0.8 %collective-permute-done.12.refs_5_ = bf16[128,256]{1,0:T(8,128)(2,1)S(1)} collective-permute-done((bf16[128,256]{1,0:T(8,128)(2,1)S(1)}, bf16[128,256]{1,0:T(8,128)(2,1)S(1)}, u32[]{:S(2)}, u32[]{:S(2)}) %collective-permute-start.12) | collective-permute-done | bytes 65568 | tf_op jit(solution)/shard_map/ppermute | solution.py:40
  34.3 3.3 %collective-permute-done.13.refs_6_ = bf16[128,256]{1,0:T(8,128)(2,1)S(1)} collective-permute-done((bf16[128,256]{1,0:T(8,128)(2,1)S(1)}, bf16[128,256]{1,0:T(8,128)(2,1)S(1)}, u32[]{:S(2)}, u32[]{:S(2)}) %collective-permute-start.13) | collective-permute-done | bytes 65568 | tf_op jit(solution)/shard_map/ppermute | solution.py:40
  37.6 0.4 collective-permute-done.14.refs_7_
  38.0 2.0 %shard_map.95 = bf16[128,512]{1,0:T(8,128)(2,1)} custom-call(s32[1]{0:T(128)} %bitcast.at_ref, bf16[128,512]{1,0:T(8,128)(2,1)S(1)} %collective-permute-done.refs_0_, bf16[128,512]{1,0:T(8,128)(2,1)S(1)} %collective-permute-done.2.refs_1_, bf16[128,512]{1,0:T(8,128)(2,1)S(1)} %collective-permute-done.4.refs_2_, ...), custom_call_target="tpu_custom_call" | custom-call | tf_op jit(solution)/shard_map/pallas_call | solution.py:52
  (28 shorter events, 2.4 us)
Async XLA Ops:
  1.2 15.0 %collective-permute-start.5 = (bf16[128,1024]{1,0:T(8,128)(2,1)S(1)}, bf16[128,1024]{1,0:T(8,128)(2,1)S(1)}, u32[]{:S(2)}, u32[]{:S(2)}) collective-permute-start(bf16[128,1024]{1,0:T(8,128)(2,1)S(1)} %get-tuple-element.21), channel_id=1, source_target_pairs={{0,4},{2,6},{4,0},{6,2},{1,5},{3,7},{5,1},{7,3},{8,12},{10,14},{12... | collective-permute-start | bytes 786440 | tf_op jit(solution)/shard_map/ppermute | solution.py:27
  4.3 12.6 %collective-permute-start.1 = (bf16[128,1024]{1,0:T(8,128)(2,1)S(1)}, bf16[128,1024]{1,0:T(8,128)(2,1)S(1)}, u32[]{:S(2)}, u32[]{:S(2)}) collective-permute-start(bf16[128,1024]{1,0:T(8,128)(2,1)S(1)} %get-tuple-element.19), channel_id=1, source_target_pairs={{0,6},{2,4},{4,2},{6,0},{1,7},{3,5},{5,3},{7,1},{8,14},{10,12},{12... | collective-permute-start | bytes 786440 | tf_op jit(solution)/shard_map/ppermute | solution.py:27
  5.7 0.7 %copy-start.1 = (s32[1,1,512]{2,1,0:T(1,128)S(1)}, s32[1,1,512]{2,1,0:T(1,128)}, u32[]{:S(2)}) copy-start(s32[1,1,512]{2,1,0:T(1,128)} %param.14) | copy-start | bytes 6148
  5.7 14.4 %collective-permute-start.3 = (bf16[128,1024]{1,0:T(8,128)(2,1)S(1)}, bf16[128,1024]{1,0:T(8,128)(2,1)S(1)}, u32[]{:S(2)}, u32[]{:S(2)}) collective-permute-start(bf16[128,1024]{1,0:T(8,128)(2,1)S(1)} %get-tuple-element.20), channel_id=1, source_target_pairs={{0,2},{2,0},{4,6},{6,4},{1,3},{3,1},{5,7},{7,5},{8,10},{10,8},{12,... | collective-permute-start | bytes 786440 | tf_op jit(solution)/shard_map/ppermute | solution.py:27
  5.8 0.7 %copy-start.2 = (s32[1,1,8]{2,1,0:T(1,128)S(1)}, s32[1,1,8]{2,1,0:T(1,128)}, u32[]{:S(2)}) copy-start(s32[1,1,8]{2,1,0:T(1,128)} %param.13) | copy-start | bytes 100
  6.5 1.6 %copy-start = (f32[1,4096]{1,0:T(1,128)S(1)}, f32[1,4096]{1,0:T(1,128)}, u32[]{:S(2)}) copy-start(f32[1,4096]{1,0:T(1,128)} %gain_ref.1) | copy-start | bytes 49156
  8.1 12.0 %collective-permute-start.11 = (f32[1,1152]{1,0:T(1,128)S(1)}, f32[1,1152]{1,0:T(1,128)S(1)}, u32[]{:S(2)}, u32[]{:S(2)}) collective-permute-start(f32[1,1152]{1,0:T(1,128)S(1)} %shard_map.92), channel_id=1, source_target_pairs={{0,1},{1,0},{2,3},{3,2},{4,5},{5,4},{6,7},{7,6},{8,9},{9,8},{10,11... | collective-permute-start | bytes 13832 | tf_op jit(solution)/shard_map/ppermute | solution.py:352
  10.9 11.0 %collective-permute-start.7 = (bf16[128,256]{1,0:T(8,128)(2,1)S(1)}, bf16[128,256]{1,0:T(8,128)(2,1)S(1)}, u32[]{:S(2)}, u32[]{:S(2)}) collective-permute-start(bf16[128,256]{1,0:T(8,128)(2,1)S(1)} %shard_map.88), channel_id=1, source_target_pairs={{0,1},{1,0},{2,3},{3,2},{4,5},{5,4},{6,7},{7,6},{8,9},{9,8},{10,11... | collective-permute-start | bytes 196616 | tf_op jit(solution)/shard_map/ppermute | solution.py:36
  16.5 7.4 %collective-permute-start.10 = (bf16[128,256]{1,0:T(8,128)(2,1)S(1)}, bf16[128,256]{1,0:T(8,128)(2,1)S(1)}, u32[]{:S(2)}, u32[]{:S(2)}) collective-permute-start(bf16[128,256]{1,0:T(8,128)(2,1)S(1)} %shard_map.91), channel_id=1, source_target_pairs={{0,5},{1,4},{2,7},{3,6},{4,1},{5,0},{6,3},{7,2},{8,13},{9,12},{10,... | collective-permute-start | bytes 196616 | tf_op jit(solution)/shard_map/ppermute | solution.py:36
  17.1 7.4 %collective-permute-start.8 = (bf16[128,256]{1,0:T(8,128)(2,1)S(1)}, bf16[128,256]{1,0:T(8,128)(2,1)S(1)}, u32[]{:S(2)}, u32[]{:S(2)}) collective-permute-start(bf16[128,256]{1,0:T(8,128)(2,1)S(1)} %shard_map.89), channel_id=1, source_target_pairs={{0,7},{1,6},{2,5},{3,4},{4,3},{5,2},{6,1},{7,0},{8,15},{9,14},{10,... | collective-permute-start | bytes 196616 | tf_op jit(solution)/shard_map/ppermute | solution.py:36
  20.0 9.4 %collective-permute-start = (bf16[128,512]{1,0:T(8,128)(2,1)S(1)}, bf16[128,512]{1,0:T(8,128)(2,1)S(1)}, u32[]{:S(2)}, u32[]{:S(2)}) collective-permute-start(bf16[128,512]{1,0:T(8,128)(2,1)S(1)} %shard_map.84), channel_id=1, source_target_pairs={{0,1},{1,0},{2,3},{3,2},{4,5},{5,4},{6,7},{7,6},{8,9},{9,8},{10,11... | collective-permute-start | bytes 393224 | tf_op jit(solution)/shard_map/ppermute | solution.py:36
  20.1 12.0 %collective-permute-start.2 = (bf16[128,512]{1,0:T(8,128)(2,1)S(1)}, bf16[128,512]{1,0:T(8,128)(2,1)S(1)}, u32[]{:S(2)}, u32[]{:S(2)}) collective-permute-start(bf16[128,512]{1,0:T(8,128)(2,1)S(1)} %shard_map.85), channel_id=1, source_target_pairs={{0,7},{1,6},{2,5},{3,4},{4,3},{5,2},{6,1},{7,0},{8,15},{9,14},{10,... | collective-permute-start | bytes 393224 | tf_op jit(solution)/shard_map/ppermute | solution.py:36
  22.0 5.8 %collective-permute-start.9 = (bf16[128,256]{1,0:T(8,128)(2,1)S(1)}, bf16[128,256]{1,0:T(8,128)(2,1)S(1)}, u32[]{:S(2)}, u32[]{:S(2)}) collective-permute-start(bf16[128,256]{1,0:T(8,128)(2,1)S(1)} %shard_map.90), channel_id=1, source_target_pairs={{0,3},{1,2},{2,1},{3,0},{4,7},{5,6},{6,5},{7,4},{8,11},{9,10},{10,... | collective-permute-start | bytes 196616 | tf_op jit(solution)/shard_map/ppermute | solution.py:36
  23.9 9.6 %collective-permute-start.4 = (bf16[128,512]{1,0:T(8,128)(2,1)S(1)}, bf16[128,512]{1,0:T(8,128)(2,1)S(1)}, u32[]{:S(2)}, u32[]{:S(2)}) collective-permute-start(bf16[128,512]{1,0:T(8,128)(2,1)S(1)} %shard_map.86), channel_id=1, source_target_pairs={{0,3},{1,2},{2,1},{3,0},{4,7},{5,6},{6,5},{7,4},{8,11},{9,10},{10,... | collective-permute-start | bytes 393224 | tf_op jit(solution)/shard_map/ppermute | solution.py:36
  24.5 8.9 %collective-permute-start.6 = (bf16[128,512]{1,0:T(8,128)(2,1)S(1)}, bf16[128,512]{1,0:T(8,128)(2,1)S(1)}, u32[]{:S(2)}, u32[]{:S(2)}) collective-permute-start(bf16[128,512]{1,0:T(8,128)(2,1)S(1)} %shard_map.87), channel_id=1, source_target_pairs={{0,5},{1,4},{2,7},{3,6},{4,1},{5,0},{6,3},{7,2},{8,13},{9,12},{10,... | collective-permute-start | bytes 393224 | tf_op jit(solution)/shard_map/ppermute | solution.py:36
  24.6 0.7 %copy-start.3 = (f32[1,128]{1,0:T(1,128)S(1)}, f32[1,128]{1,0:T(1,128)}, u32[]{:S(2)}) copy-start(f32[1,128]{1,0:T(1,128)} %constant.11.clone.freq_ref) | copy-start | bytes 1540
  27.9 6.4 %collective-permute-start.12 = (bf16[128,256]{1,0:T(8,128)(2,1)S(1)}, bf16[128,256]{1,0:T(8,128)(2,1)S(1)}, u32[]{:S(2)}, u32[]{:S(2)}) collective-permute-start(bf16[128,256]{1,0:T(8,128)(2,1)S(1)} %shard_map.94.refs_4_), channel_id=1, source_target_pairs={{0,8},{8,16},{16,24},{24,0},{1,9},{9,17},{17,25},{25,1},{2,10},{10... | collective-permute-start | bytes 196616 | tf_op jit(solution)/shard_map/ppermute | solution.py:40
  29.5 8.1 %collective-permute-start.13 = (bf16[128,256]{1,0:T(8,128)(2,1)S(1)}, bf16[128,256]{1,0:T(8,128)(2,1)S(1)}, u32[]{:S(2)}, u32[]{:S(2)}) collective-permute-start(bf16[128,256]{1,0:T(8,128)(2,1)S(1)} %shard_map.94.refs_4_), channel_id=1, source_target_pairs={{0,16},{8,24},{16,0},{24,8},{1,17},{9,25},{17,1},{25,9},{2,18},{10... | collective-permute-start | bytes 196616 | tf_op jit(solution)/shard_map/ppermute | solution.py:40
  32.1 5.9 %collective-permute-start.14 = (bf16[128,256]{1,0:T(8,128)(2,1)S(1)}, bf16[128,256]{1,0:T(8,128)(2,1)S(1)}, u32[]{:S(2)}, u32[]{:S(2)}) collective-permute-start(bf16[128,256]{1,0:T(8,128)(2,1)S(1)} %shard_map.94.refs_4_), channel_id=1, source_target_pairs={{0,24},{8,0},{16,8},{24,16},{1,25},{9,1},{17,9},{25,17},{2,26},{10... | collective-permute-start | bytes 196616 | tf_op jit(solution)/shard_map/ppermute | solution.py:40

commit v2 on v1

--- a/solution.py
+++ b/solution.py
@@ -58,38 +58,48 @@
     )(*args)
 
 
-def cut_kernel(count, sequence, here_ref, rows_ref, *refs):
-    out_refs, sem = refs[:count], refs[count]
+def in_hbm(*arrays):
+    return [pltpu.with_memory_space_constraint(x, pltpu.HBM) for x in arrays]
+
+
+def cut_kernel(count, sequence, here_ref, rows_ref, gain_ref, *refs):
+    out_refs, held, sem = refs[: len(sequence)], refs[-2], refs[-1]
     width = out_refs[0].shape[1]
-    copies = []
-    for slot, k in enumerate(sequence):
-        begin = pl.multiple_of(partner(here_ref[0], k, count) * width, width)
-        copies.append(
-            pltpu.make_async_copy(
-                rows_ref.at[:, pl.ds(begin, width)], out_refs[slot], sem.at[slot]
-            )
-        )
+    begins = [pl.multiple_of(partner(here_ref[0], k, count) * width, width) for k in sequence]
+    copies = [
+        pltpu.make_async_copy(rows_ref.at[:, pl.ds(b, width)], held.at[i], sem.at[i])
+        for i, b in enumerate(begins)
+    ]
     for copy in copies:
         copy.start()
-    for copy in copies:
+    for i, copy in enumerate(copies):
         copy.wait()
-
-
-def cut(rows, here, count, sequence):
+        gain = gain_ref[:, pl.ds(begins[i], width)]
+        out_refs[i][...] = (held[i].astype(jnp.float32) * gain).astype(jnp.bfloat16)
+
+
+def cut(rows, gain, here, count, sequence):
     height, features = rows.shape
-    rows = pltpu.with_memory_space_constraint(rows, pltpu.HBM)
+    width = features // count
     return local_call(
         functools.partial(cut_kernel, count, sequence),
-        [on_chip((height, features // count), jnp.bfloat16)] * count,
-        (here, rows),
-        (pltpu.SMEM, pltpu.HBM),
-        scratch_shapes=[pltpu.SemaphoreType.DMA((count,))],
-    )
-
-
-def meta_kernel(docs_count, blocks, rows_ref, order_ref, docs_ref, out_ref):
+        [on_chip((height, width), jnp.bfloat16)] * len(sequence),
+        (here, *in_hbm(rows, gain)),
+        (pltpu.SMEM, pltpu.HBM, pltpu.VMEM),
+        scratch_shapes=[
+            pltpu.VMEM((len(sequence), height, width), jnp.bfloat16),
+            pltpu.SemaphoreType.DMA((len(sequence),)),
+        ],
+    )
+
+
+def product(x, weight):
+    return jnp.dot(x, weight, preferred_element_type=jnp.float32).astype(jnp.bfloat16)
+
+
+def tell(rows_ref, order_ref, docs_ref, out_ref):
     height = rows_ref.shape[0]
-    length = docs_ref.shape[1]
+    length, blocks = docs_ref.shape[1], order_ref.shape[1]
     block_rows = length // blocks
     squares = jnp.zeros((height, 128), jnp.float32)
     for i in range(rows_ref.shape[1] // 128):
@@ -103,27 +113,54 @@
         jnp.where(down == across, scale, 0.0), axis=0, keepdims=True
     )
     lane = lax.broadcasted_iota(jnp.int32, (1, length), 1)
-    block = jnp.zeros((1, length), jnp.int32)
+    shift = jnp.zeros((1, length), jnp.int32)
     for b in range(blocks):
         inside = (lane >= b * block_rows) & (lane < (b + 1) * block_rows)
-        block = jnp.where(inside, order_ref[0, b] * block_rows - b * block_rows, block)
-    positions = (block + lane).astype(jnp.float32)
+        shift = jnp.where(inside, (order_ref[0, b] - b) * block_rows, shift)
+    positions = (shift + lane).astype(jnp.float32)
     number = jnp.zeros((1, length), jnp.float32)
-    for d in range(1, docs_count):
+    for d in range(1, DOCS):
         start = jnp.sum((docs_ref[...] < d).astype(jnp.float32), axis=1, keepdims=True)
         number = number + (positions >= start).astype(jnp.float32)
     out_ref[:, :length] = positions
     out_ref[:, length : 2 * length] = number
 
 
-def describe(rows, order, docs):
-    height, length, blocks = rows.shape[0], docs.shape[1], order.shape[1]
-    rows = pltpu.with_memory_space_constraint(rows, pltpu.HBM)
-    return local_call(
-        functools.partial(meta_kernel, DOCS, blocks),
-        on_chip((1, 2 * length + height), jnp.float32),
-        (rows, order, docs),
-        (pltpu.VMEM, pltpu.SMEM, pltpu.VMEM),
+def prepare_kernel(
+    here_ref, rows_hbm, gain_ref, kw_hbm, vw_hbm, qw_hbm, order_ref, docs_ref, *refs
+):
+    w_out, part_out, rows_ref, sem = refs[0], refs[1], refs[-2], refs[-1]
+    copies = [pltpu.make_async_copy(rows_hbm, rows_ref, sem.at[0])]
+    offset = 0
+    for i, weight in enumerate((kw_hbm, vw_hbm, qw_hbm)):
+        place = w_out.at[:, offset : offset + weight.shape[1]]
+        copies.append(pltpu.make_async_copy(weight, place, sem.at[1 + i]))
+        offset += weight.shape[1]
+    for copy in copies:
+        copy.start()
+    copies[0].wait()
+    if len(refs) == 5:
+        tell(rows_ref, order_ref, docs_ref, refs[2])
+    width = w_out.shape[0]
+    begin = pl.multiple_of(here_ref[0] * width, width)
+    part = rows_ref[:, pl.ds(begin, width)].astype(jnp.float32) * gain_ref[:, pl.ds(begin, width)]
+    for copy in copies[1:]:
+        copy.wait()
+    part_out[...] = product(part.astype(jnp.bfloat16), w_out[...])
+
+
+def prepare(here, rows, gain, weights, order, docs, with_meta):
+    height, depth = rows.shape[0], weights[0].shape[0]
+    width = sum(w.shape[1] for w in weights)
+    outs = [on_chip((depth, width), jnp.bfloat16), on_chip((height, width), jnp.bfloat16)]
+    if with_meta:
+        outs.append(on_chip((1, 2 * docs.shape[1] + height), jnp.float32))
+    return local_call(
+        prepare_kernel,
+        outs,
+        (here, *in_hbm(rows, gain, *weights, order, docs)),
+        (pltpu.SMEM, pltpu.HBM, pltpu.VMEM, *[pltpu.HBM] * 3, pltpu.SMEM, pltpu.VMEM),
+        scratch_shapes=[pltpu.VMEM(rows.shape, jnp.bfloat16), pltpu.SemaphoreType.DMA((4,))],
     )
 
 
@@ -147,14 +184,16 @@
     return jnp.sum(jnp.where(down == across, row, 0.0), axis=1, keepdims=True)
 
 
-def tables_kernel(length, at_ref, meta_ref, freq_ref, kcos, ksin, qcos, qsin, level, bias):
+def tables_kernel(length, at_ref, meta_ref, kcos, ksin, qcos, qsin, level, bias):
     rows, size = kcos.shape
     begin = pl.multiple_of(at_ref[0] * rows, rows)
     qpos = column(meta_ref[:, pl.ds(begin, rows)])
     qdoc = column(meta_ref[:, pl.ds(length + begin, rows)])
     scale = column(meta_ref[:, 2 * length :])
-    angles = qpos * freq_ref[...]
-    sign = jnp.where(lax.broadcasted_iota(jnp.int32, (1, size), 1) < size // 2, -1.0, 1.0)
+    lane = lax.broadcasted_iota(jnp.int32, (1, size), 1)
+    pair = lax.rem(lane, size // 2).astype(jnp.float32)
+    angles = qpos * jnp.exp2(pair * (-2.0 * np.log2(ROPE_BASE) / size))
+    sign = jnp.where(lane < size // 2, -1.0, 1.0)
     cosine, sine = jnp.cos(angles) * scale, jnp.sin(angles) * sign * scale
     kcos[...], ksin[...] = cosine, sine
     more = size ** (-0.5) * LOG2E
@@ -164,47 +203,13 @@
     bias[...] = jnp.where(allowed, 0.0, MASKED)
 
 
-def tables(at, meta, freqs, rows, size, length):
+def tables(at, meta, rows, size, length):
     square = on_chip((rows, size), jnp.float32)
     return local_call(
         functools.partial(tables_kernel, length),
         [square] * 5 + [on_chip((rows, length), jnp.float32)],
-        (at, meta, freqs),
-        (pltpu.SMEM, pltpu.VMEM, pltpu.VMEM),
-    )
-
-
-def scale_kernel(here_ref, gain_ref, query_ref, key_ref, value_ref, kv_out, q_out):
-    rows, size = key_ref.shape
-    step = pl.program_id(0)
-    for i in range(rows // size):
-        begin = ((here_ref[0] * pl.num_programs(0) + step) * (rows // size) + i) * size
-        gain = column(gain_ref[:, pl.ds(pl.multiple_of(begin, size), size)])
-        part = slice(i * size, (i + 1) * size)
-        target = pl.ds(pl.multiple_of(step * rows + i * size, size), size)
-        kv_out[target, :size] = (key_ref[part, :].astype(jnp.float32) * gain).astype(jnp.bfloat16)
-        kv_out[target, size:] = (value_ref[part, :].astype(jnp.float32) * gain).astype(jnp.bfloat16)
-        q_out[target, :] = (query_ref[part, :].astype(jnp.float32) * gain).astype(jnp.bfloat16)
-
-
-def scale_weights(here, gain, query_weight, key_weight, value_weight):
-    depth, size = key_weight.shape
-    width = query_weight.shape[1]
-    steps = 4
-    rows = depth // steps
-    held = [pltpu.with_memory_space_constraint(w, pltpu.HBM) for w in (query_weight, key_weight, value_weight)]
-    return local_call(
-        scale_kernel,
-        [on_chip((depth, 2 * size), jnp.bfloat16), on_chip((depth, width), jnp.bfloat16)],
-        (here, gain, *held),
-        [
-            pltpu.SMEM,
-            pltpu.VMEM,
-            pl.BlockSpec((rows, width), lambda i: (i, 0)),
-            pl.BlockSpec((rows, size), lambda i: (i, 0)),
-            pl.BlockSpec((rows, size), lambda i: (i, 0)),
-        ],
-        grid=(steps,),
+        (at, meta),
+        (pltpu.SMEM, pltpu.VMEM),
     )
 
 
@@ -223,10 +228,10 @@
     )
 
 
-def summed(refs, start, stop):
-    total = refs[0][:, start:stop].astype(jnp.float32)
-    for ref in refs[1:]:
-        total = total + ref[:, start:stop].astype(jnp.float32)
+def summed(refs, start, size):
+    total = 0.0
+    for ref, offset in refs:
+        total = total + ref[:, offset + start : offset + start + size].astype(jnp.float32)
     return total
 
 
@@ -235,22 +240,37 @@
 
 
 def mix_kernel(*refs):
-    parts, (kcos, ksin, level, out_ref) = refs[:-4], refs[-4:]
+    parts, (kcos, ksin, level, out_ref) = [(r, 0) for r in refs[:-4]], refs[-4:]
     size = kcos.shape[1]
     keys = turn(summed(parts, 0, size), kcos[...], ksin[...])
     out_ref[:, :size] = keys.astype(jnp.bfloat16)
-    out_ref[:, size:] = (summed(parts, size, 2 * size) * level[...]).astype(jnp.bfloat16)
+    out_ref[:, size:] = (summed(parts, size, size) * level[...]).astype(jnp.bfloat16)
 
 
 def mix(parts, kcos, ksin, level):
     args = (*parts, kcos, ksin, level)
-    return local_call(
-        mix_kernel, on_chip(parts[0].shape, jnp.bfloat16), args, [pltpu.VMEM] * len(args)
-    )
-
-
-def attend_kernel(count, ring, at_ref, *refs):
-    parts, kv_refs = refs[:count], refs[count : count + ring]
+    rows, size = kcos.shape
+    return local_call(
+        mix_kernel, on_chip((rows, 2 * size), jnp.bfloat16), args, [pltpu.VMEM] * len(args)
+    )
+
+
+def project_kernel(start, stop, x_ref, w_ref, out_ref):
+    out_ref[...] = product(x_ref[...], w_ref[:, start:stop])
+
+
+def project(x, weight, start, stop):
+    return local_call(
+        functools.partial(project_kernel, start, stop),
+        on_chip((x.shape[0], stop - start), jnp.bfloat16),
+        (x, weight),
+        [pltpu.VMEM] * 2,
+    )
+
+
+def attend_kernel(offsets, ring, at_ref, *refs):
+    count = len(offsets)
+    parts, kv_refs = list(zip(refs, offsets)), refs[count : count + ring]
     qcos, qsin, bias, out_ref = refs[count + ring :]
     rows, size = qcos.shape
     keys = jnp.concatenate([ref[:, :size] for ref in kv_refs], axis=0)
@@ -260,7 +280,7 @@
     ]
     masks = jnp.concatenate([bias[:, pl.ds(b, rows)] for b in here], axis=1)
     for h in range(out_ref.shape[1] // size):
-        query = turn(summed(parts, h * size, (h + 1) * size), qcos[...], qsin[...])
+        query = turn(summed(parts, h * size, size), qcos[...], qsin[...])
         scores = lax.dot_general(
             query.astype(jnp.bfloat16),
             keys,
@@ -274,17 +294,19 @@
         out_ref[:, h * size : (h + 1) * size] = (mixed / total).astype(jnp.bfloat16)
 
 
-def attend(at, parts, kv, qcos, qsin, bias):
+def attend(at, parts, offsets, kv, qcos, qsin, bias):
     args = (at, *parts, *kv, qcos, qsin, bias)
-    return local_call(
-        functools.partial(attend_kernel, len(parts), len(kv)),
-        jax.ShapeDtypeStruct(parts[0].shape, jnp.bfloat16),
+    width = parts[0].shape[1] - offsets[0]
+    return local_call(
+        functools.partial(attend_kernel, offsets, len(kv)),
+        jax.ShapeDtypeStruct((parts[0].shape[0], width), jnp.bfloat16),
         args,
         [pltpu.SMEM] + [pltpu.VMEM] * (len(args) - 1),
     )
 
 
-def attend_long(parts, everything, qcos, qsin, bias):
+def attend_long(parts, offsets, everything, qcos, qsin, bias):
+    parts = [p[:, o:] for p, o in zip(parts, offsets)]
     rows, width = parts[0].shape
     size = qcos.shape[1]
     heads = width // size
@@ -340,41 +362,40 @@
     size = key_weight.shape[2]
     here = lax.axis_index("dp").astype(jnp.int32)[None]
     at = lax.axis_index("ctx").astype(jnp.int32)[None]
-    sequence = [count - 1, *range(1, count - 1), 0]
-    slabs = cut(rows_here, here, count, sequence)
-
+    away = [count - 1, *range(1, count - 1)]
+    weights = [key_weight[0], value_weight[0], query_weight[0]]
+    slabs = cut(rows_here, norm_gain, here, count, away)
     arrived = {}
-    for k, slab in zip(sequence, slabs):
-        arrived[k] = swap_dp(slab, k, count) if k else slab
-
-    tell = describe if ring <= DIRECT else describe_long
-    meta = tell(rows_here, block_order[0], doc_ids[0])
+    for k, slab in zip(away, slabs):
+        arrived[k] = swap_dp(slab, k, count)
+
+    weight, part, *meta = prepare(
+        here, rows_here, norm_gain, weights, block_order[0], doc_ids[0], ring <= DIRECT
+    )
+    parts = [to_next_section(part, 0, count, sections)]
+    meta = meta[0] if meta else describe_long(rows_here, block_order[0], doc_ids[0])
     meta = lax.ppermute(meta, "section", [(i, (i + 1) % sections) for i in range(sections)])
-
-    freqs = ROPE_BASE ** (-np.arange(size // 2, dtype=np.float64) * 2.0 / size)
-    freqs = jnp.asarray(np.concatenate([freqs, freqs])[None], jnp.float32)
-    kcos, ksin, qcos, qsin, level, bias = tables(at, meta, freqs, row_count, size, length)
-
-    kv_weight, q_weight = scale_weights(
-        here, norm_gain, query_weight[0], key_weight[0], value_weight[0]
-    )
-
-    kv_parts, q_parts = [], []
-    for k in [sequence[-1], *sequence[:-1]]:
-        part = project(arrived[k], kv_weight)
+    kcos, ksin, qcos, qsin, level, bias = tables(at, meta, row_count, size, length)
+
+    part = project(arrived[away[0]], weight, 0, weight.shape[1])
+    parts.append(to_next_section(part, away[0], count, sections))
+    kv_parts, q_parts, offsets = list(parts), list(parts), [2 * size, 2 * size]
+    for k in away[1:]:
+        part = project(arrived[k], weight, 0, 2 * size)
         kv_parts.append(to_next_section(part, k, count, sections))
-        part = project(arrived[k], q_weight)
+        part = project(arrived[k], weight, 2 * size, weight.shape[1])
         q_parts.append(to_next_section(part, k, count, sections))
+        offsets.append(0)
 
     kv = mix(kv_parts, kcos, ksin, level)
     if ring <= DIRECT:
         pieces = [kv]
         for j in range(1, ring):
             pieces.append(shift_ctx(kv, j, ring))
-        out = attend(at, q_parts, pieces, qcos, qsin, bias)
+        out = attend(at, q_parts, offsets, pieces, qcos, qsin, bias)
     else:
         everything = lax.all_gather(kv, "ctx", axis=0, tiled=True)
-        out = attend_long(q_parts, everything, qcos, qsin, bias)
+        out = attend_long(q_parts, offsets, everything, qcos, qsin, bias)
     return out[None, None]
 
 

time: 40.2 us -> 37.2 us (0.925)
  local copies, waits for them, and re-layouts: 1.31 us -> 0 us
  starting transfers between devices: 17.4 us -> 16.1 us
  Pallas kernels: 9.9 us -> 8.71 us
  waiting for transfers between devices: 11.2 us -> 11.9 us
    ppermute x8 -> x6, starting transfers between devices: 7.15 us -> 4.18 us  [to_next_section(): return lax.ppermute(x, ('dp', 'section'), moves)]
    ppermute x1, starting transfers between devices: 0.07 us -> 2.66 us  [local(): lax.ppermute(meta, 'section', [(i, (i + 1) % sections) for i in range(sec...]
    ppermute x8 -> x6, waiting for transfers between devices: 2.2 us -> 0.14 us  [to_next_section(): return lax.ppermute(x, ('dp', 'section'), moves)]
    ppermute x3, waiting for transfers between devices: 4.52 us -> 6.5 us  [shift_ctx(): return lax.ppermute(x, 'ctx', [(i, (i + by) % ring) for i in range(ring)])]
    unnamed x8 -> x0, local copies, waits for them, and re-layouts: 1.31 us -> none
    pallas_call x14 -> x10, Pallas kernels: 9.9 us -> 8.71 us  [local_call(): pl.pallas_call(kernel, out_shape=out_shape, in_specs=in_specs, compiler_p...]
    ppermute x3, starting transfers between devices: 5.57 us -> 4.67 us  [shift_ctx(): return lax.ppermute(x, 'ctx', [(i, (i + by) % ring) for i in range(ring)])]
    ppermute x3, waiting for transfers between devices: 4.45 us -> 5.24 us  [swap_dp(): lax.ppermute(x, 'dp', [(i, partner(i, step, count)) for i in range(count)])]
  transfers between devices with their start and end apart: 15 -> 13, of which waited for: 5 -> 5; matrix products, arithmetic and copies ran while one was open for 0% -> 0% of each run, Pallas kernels for 17% -> 13%
where the time goes in v2:
time: 37.2 us; the launch traced here: 36.9 us
  starting transfers between devices  16.1 us (43%)
  waiting for transfers between devices  11.9 us (32%)
  Pallas kernels  8.71 us (23%)
    pallas_call x10, Pallas kernels, local_call(): pl.pallas_call(kernel, out_shape=out_shape, in_specs=in_specs, compiler_p...  8.71 us
    ppermute x3, waiting for transfers between devices, shift_ctx(): return lax.ppermute(x, 'ctx', [(i, (i + by) % ring) for i in range(ring)])  6.5 us
    ppermute x3, waiting for transfers between devices, swap_dp(): lax.ppermute(x, 'dp', [(i, partner(i, step, count)) for i in range(count)])  5.24 us
    ppermute x3, starting transfers between devices, shift_ctx(): return lax.ppermute(x, 'ctx', [(i, (i + by) % ring) for i in range(ring)])  4.67 us
    ppermute x3, starting transfers between devices, swap_dp(): lax.ppermute(x, 'dp', [(i, partner(i, step, count)) for i in range(count)])  4.63 us
    ppermute x6, starting transfers between devices, to_next_section(): return lax.ppermute(x, ('dp', 'section'), moves)  4.18 us
    ppermute x1, starting transfers between devices, local(): lax.ppermute(meta, 'section', [(i, (i + 1) % sections) for i in range(sec...  2.66 us
  transfers between devices with their start and end apart: 13, of which 5 were waited for; matrix products, arithmetic and copies ran while one was open for 0% of the time, Pallas kernels for 13%

profile of v2, /device:TPU:0, one launch (start us, length us, event | category | flops | bytes accessed | tf_op | source)
XLA Modules:
  0.0 36.9 jit_solution(15095361406010156743)
XLA Ops:
  0.0 1.9 %shard_map.74 = (bf16[128,1024]{1,0:T(8,128)(2,1)S(1)}, bf16[128,1024]{1,0:T(8,128)(2,1)S(1)}, bf16[128,1024]{1,0:T(8,128)(2,1)S(1)}) custom-call(s32[1]{0:T(128)} %bitcast.1.here_ref, bf16[128,4096]{1,0:T(8,128)(2,1)} %bitcast.9, f32[1,4096]{1,0:T(1,128)} %gain_ref.3), custom_call_target="tpu_custom_call" | custom-call | tf_op jit(solution)/shard_map/pallas_call | solution.py:52
  1.9 4.0 %collective-permute-start.1 = (bf16[128,1024]{1,0:T(8,128)(2,1)S(1)}, bf16[128,1024]{1,0:T(8,128)(2,1)S(1)}, u32[]{:S(2)}, u32[]{:S(2)}) collective-permute-start(bf16[128,1024]{1,0:T(8,128)(2,1)S(1)} %get-tuple-element.18), channel_id=1, source_target_pairs={{0,6},{2,4},{4,2},{6,0},{1,7},{3,5},{5,3},{7,1},{8,14},{10,12},{12... | collective-permute-start | bytes 786440 | tf_op jit(solution)/shard_map/ppermute | solution.py:27
  5.9 0.5 %collective-permute-start.3 = (bf16[128,1024]{1,0:T(8,128)(2,1)S(1)}, bf16[128,1024]{1,0:T(8,128)(2,1)S(1)}, u32[]{:S(2)}, u32[]{:S(2)}) collective-permute-start(bf16[128,1024]{1,0:T(8,128)(2,1)S(1)} %get-tuple-element.20), channel_id=1, source_target_pairs={{0,2},{2,0},{4,6},{6,4},{1,3},{3,1},{5,7},{7,5},{8,10},{10,8},{12,... | collective-permute-start | bytes 786440 | tf_op jit(solution)/shard_map/ppermute | solution.py:27
  6.5 2.9 %shard_map.73 = (bf16[1024,768]{1,0:T(8,128)(2,1)S(1)}, bf16[128,768]{1,0:T(8,128)(2,1)S(1)}, f32[1,1152]{1,0:T(1,128)S(1)}) custom-call(s32[1]{0:T(128)} %bitcast.1.here_ref, bf16[128,4096]{1,0:T(8,128)(2,1)} %bitcast.10, f32[1,4096]{1,0:T(1,128)} %gain_ref.3, bf16[1024,128]{1,0:T(8,128)(2,1)} %bitcast.12, bf16[1024,128]{1,0:T(8,128)(2,1)} %bitcast.13, ...), custom_call_target="tpu_custom_call" | custom-call | tf_op jit(solution)/shard_map/pallas_call | solution.py:52
  9.5 3.6 %collective-permute-done.1.x_ref = bf16[128,1024]{1,0:T(8,128)(2,1)S(1)} collective-permute-done((bf16[128,1024]{1,0:T(8,128)(2,1)S(1)}, bf16[128,1024]{1,0:T(8,128)(2,1)S(1)}, u32[]{:S(2)}, u32[]{:S(2)}) %collective-permute-start.1) | collective-permute-done | bytes 262176 | tf_op jit(solution)/shard_map/ppermute | solution.py:27
  13.1 0.4 %shard_map.75 = bf16[128,768]{1,0:T(8,128)(2,1)S(1)} custom-call(bf16[128,1024]{1,0:T(8,128)(2,1)S(1)} %collective-permute-done.1.x_ref, bf16[1024,768]{1,0:T(8,128)(2,1)S(1)} %get-tuple-element.19.w_ref), custom_call_target="tpu_custom_call" | custom-call | tf_op jit(solution)/shard_map/pallas_call | solution.py:52
  13.5 0.4 %collective-permute-start.2 = (bf16[128,768]{1,0:T(8,128)(2,1)S(1)}, bf16[128,768]{1,0:T(8,128)(2,1)S(1)}, u32[]{:S(2)}, u32[]{:S(2)}) collective-permute-start(bf16[128,768]{1,0:T(8,128)(2,1)S(1)} %shard_map.75), channel_id=1, source_target_pairs={{0,7},{1,6},{2,5},{3,4},{4,3},{5,2},{6,1},{7,0},{8,15},{9,14},{10,... | collective-permute-start | bytes 589832 | tf_op jit(solution)/shard_map/ppermute | solution.py:36
  13.9 2.7 %collective-permute-start.9 = (f32[1,1152]{1,0:T(1,128)S(1)}, f32[1,1152]{1,0:T(1,128)S(1)}, u32[]{:S(2)}, u32[]{:S(2)}) collective-permute-start(f32[1,1152]{1,0:T(1,128)S(1)} %get-tuple-element.22), channel_id=1, source_target_pairs={{0,1},{1,0},{2,3},{3,2},{4,5},{5,4},{6,7},{7,6},{8,9},{9,8},{10,11... | collective-permute-start | bytes 13832 | tf_op jit(solution)/shard_map/ppermute | solution.py:377
  16.6 1.7 %collective-permute-done.3.x_ref = bf16[128,1024]{1,0:T(8,128)(2,1)S(1)} collective-permute-done((bf16[128,1024]{1,0:T(8,128)(2,1)S(1)}, bf16[128,1024]{1,0:T(8,128)(2,1)S(1)}, u32[]{:S(2)}, u32[]{:S(2)}) %collective-permute-start.3) | collective-permute-done | bytes 262176 | tf_op jit(solution)/shard_map/ppermute | solution.py:27
  18.3 0.2 shard_map.78
  18.6 0.2 shard_map.79
  18.8 1.8 %collective-permute-start.8 = (bf16[128,256]{1,0:T(8,128)(2,1)S(1)}, bf16[128,256]{1,0:T(8,128)(2,1)S(1)}, u32[]{:S(2)}, u32[]{:S(2)}) collective-permute-start(bf16[128,256]{1,0:T(8,128)(2,1)S(1)} %shard_map.79), channel_id=1, source_target_pairs={{0,5},{1,4},{2,7},{3,6},{4,1},{5,0},{6,3},{7,2},{8,13},{9,12},{10,... | collective-permute-start | bytes 196616 | tf_op jit(solution)/shard_map/ppermute | solution.py:36
  20.6 0.3 shard_map.77
  20.9 0.3 shard_map.76
  21.2 0.6 %collective-permute-start.4 = (bf16[128,512]{1,0:T(8,128)(2,1)S(1)}, bf16[128,512]{1,0:T(8,128)(2,1)S(1)}, u32[]{:S(2)}, u32[]{:S(2)}) collective-permute-start(bf16[128,512]{1,0:T(8,128)(2,1)S(1)} %shard_map.76), channel_id=1, source_target_pairs={{0,3},{1,2},{2,1},{3,0},{4,7},{5,6},{6,5},{7,4},{8,11},{9,10},{10,... | collective-permute-start | bytes 393224 | tf_op jit(solution)/shard_map/ppermute | solution.py:36
  21.9 1.2 %collective-permute-start.6 = (bf16[128,512]{1,0:T(8,128)(2,1)S(1)}, bf16[128,512]{1,0:T(8,128)(2,1)S(1)}, u32[]{:S(2)}, u32[]{:S(2)}) collective-permute-start(bf16[128,512]{1,0:T(8,128)(2,1)S(1)} %shard_map.77), channel_id=1, source_target_pairs={{0,5},{1,4},{2,7},{3,6},{4,1},{5,0},{6,3},{7,2},{8,13},{9,12},{10,... | collective-permute-start | bytes 393224 | tf_op jit(solution)/shard_map/ppermute | solution.py:36
  23.1 0.3 shard_map.80
  23.4 0.1 collective-permute-done.7.refs_2_
  23.6 0.1 shard_map.81.refs_4_
  23.7 3.7 %collective-permute-start.12 = (bf16[128,256]{1,0:T(8,128)(2,1)S(1)}, bf16[128,256]{1,0:T(8,128)(2,1)S(1)}, u32[]{:S(2)}, u32[]{:S(2)}) collective-permute-start(bf16[128,256]{1,0:T(8,128)(2,1)S(1)} %shard_map.81.refs_4_), channel_id=1, source_target_pairs={{0,24},{8,0},{16,8},{24,16},{1,25},{9,1},{17,9},{25,17},{2,26},{10... | collective-permute-start | bytes 196616 | tf_op jit(solution)/shard_map/ppermute | solution.py:40
  27.4 1.0 %collective-permute-start.10 = (bf16[128,256]{1,0:T(8,128)(2,1)S(1)}, bf16[128,256]{1,0:T(8,128)(2,1)S(1)}, u32[]{:S(2)}, u32[]{:S(2)}) collective-permute-start(bf16[128,256]{1,0:T(8,128)(2,1)S(1)} %shard_map.81.refs_4_), channel_id=1, source_target_pairs={{0,8},{8,16},{16,24},{24,0},{1,9},{9,17},{17,25},{25,1},{2,10},{10... | collective-permute-start | bytes 196616 | tf_op jit(solution)/shard_map/ppermute | solution.py:40
  28.4 1.5 %collective-permute-done.12.refs_7_ = bf16[128,256]{1,0:T(8,128)(2,1)S(1)} collective-permute-done((bf16[128,256]{1,0:T(8,128)(2,1)S(1)}, bf16[128,256]{1,0:T(8,128)(2,1)S(1)}, u32[]{:S(2)}, u32[]{:S(2)}) %collective-permute-start.12) | collective-permute-done | bytes 65568 | tf_op jit(solution)/shard_map/ppermute | solution.py:40
  29.9 5.0 %collective-permute-done.11.refs_6_ = bf16[128,256]{1,0:T(8,128)(2,1)S(1)} collective-permute-done((bf16[128,256]{1,0:T(8,128)(2,1)S(1)}, bf16[128,256]{1,0:T(8,128)(2,1)S(1)}, u32[]{:S(2)}, u32[]{:S(2)}) %collective-permute-start.11) | collective-permute-done | bytes 65568 | tf_op jit(solution)/shard_map/ppermute | solution.py:40
  34.9 2.0 %shard_map.82 = bf16[128,512]{1,0:T(8,128)(2,1)} custom-call(s32[1]{0:T(128)} %bitcast.at_ref, bf16[128,768]{1,0:T(8,128)(2,1)S(1)} %collective-permute-done.refs_0_, bf16[128,768]{1,0:T(8,128)(2,1)S(1)} %collective-permute-done.2.refs_1_, bf16[128,512]{1,0:T(8,128)(2,1)S(1)} %collective-permute-done.4.refs_2_, ...), custom_call_target="tpu_custom_call" | custom-call | tf_op jit(solution)/shard_map/pallas_call | solution.py:52
  (12 shorter events, 0.3 us)
Async XLA Ops:
  1.9 11.2 %collective-permute-start.1 = (bf16[128,1024]{1,0:T(8,128)(2,1)S(1)}, bf16[128,1024]{1,0:T(8,128)(2,1)S(1)}, u32[]{:S(2)}, u32[]{:S(2)}) collective-permute-start(bf16[128,1024]{1,0:T(8,128)(2,1)S(1)} %get-tuple-element.18), channel_id=1, source_target_pairs={{0,6},{2,4},{4,2},{6,0},{1,7},{3,5},{5,3},{7,1},{8,14},{10,12},{12... | collective-permute-start | bytes 786440 | tf_op jit(solution)/shard_map/ppermute | solution.py:27
  5.9 12.4 %collective-permute-start.3 = (bf16[128,1024]{1,0:T(8,128)(2,1)S(1)}, bf16[128,1024]{1,0:T(8,128)(2,1)S(1)}, u32[]{:S(2)}, u32[]{:S(2)}) collective-permute-start(bf16[128,1024]{1,0:T(8,128)(2,1)S(1)} %get-tuple-element.20), channel_id=1, source_target_pairs={{0,2},{2,0},{4,6},{6,4},{1,3},{3,1},{5,7},{7,5},{8,10},{10,8},{12,... | collective-permute-start | bytes 786440 | tf_op jit(solution)/shard_map/ppermute | solution.py:27
  6.4 12.2 %collective-permute-start.5 = (bf16[128,1024]{1,0:T(8,128)(2,1)S(1)}, bf16[128,1024]{1,0:T(8,128)(2,1)S(1)}, u32[]{:S(2)}, u32[]{:S(2)}) collective-permute-start(bf16[128,1024]{1,0:T(8,128)(2,1)S(1)} %get-tuple-element.21), channel_id=1, source_target_pairs={{0,4},{2,6},{4,0},{6,2},{1,5},{3,7},{5,1},{7,3},{8,12},{10,14},{12... | collective-permute-start | bytes 786440 | tf_op jit(solution)/shard_map/ppermute | solution.py:27
  9.5 12.4 %collective-permute-start = (bf16[128,768]{1,0:T(8,128)(2,1)S(1)}, bf16[128,768]{1,0:T(8,128)(2,1)S(1)}, u32[]{:S(2)}, u32[]{:S(2)}) collective-permute-start(bf16[128,768]{1,0:T(8,128)(2,1)S(1)} %get-tuple-element.17), channel_id=1, source_target_pairs={{0,1},{1,0},{2,3},{3,2},{4,5},{5,4},{6,7},{7,6},{8,9},{9,8},{10,11... | collective-permute-start | bytes 589832 | tf_op jit(solution)/shard_map/ppermute | solution.py:36
  13.5 10.1 %collective-permute-start.2 = (bf16[128,768]{1,0:T(8,128)(2,1)S(1)}, bf16[128,768]{1,0:T(8,128)(2,1)S(1)}, u32[]{:S(2)}, u32[]{:S(2)}) collective-permute-start(bf16[128,768]{1,0:T(8,128)(2,1)S(1)} %shard_map.75), channel_id=1, source_target_pairs={{0,7},{1,6},{2,5},{3,4},{4,3},{5,2},{6,1},{7,0},{8,15},{9,14},{10,... | collective-permute-start | bytes 589832 | tf_op jit(solution)/shard_map/ppermute | solution.py:36
  13.9 7.3 %collective-permute-start.9 = (f32[1,1152]{1,0:T(1,128)S(1)}, f32[1,1152]{1,0:T(1,128)S(1)}, u32[]{:S(2)}, u32[]{:S(2)}) collective-permute-start(f32[1,1152]{1,0:T(1,128)S(1)} %get-tuple-element.22), channel_id=1, source_target_pairs={{0,1},{1,0},{2,3},{3,2},{4,5},{5,4},{6,7},{7,6},{8,9},{9,8},{10,11... | collective-permute-start | bytes 13832 | tf_op jit(solution)/shard_map/ppermute | solution.py:377
  18.5 5.1 %collective-permute-start.7 = (bf16[128,256]{1,0:T(8,128)(2,1)S(1)}, bf16[128,256]{1,0:T(8,128)(2,1)S(1)}, u32[]{:S(2)}, u32[]{:S(2)}) collective-permute-start(bf16[128,256]{1,0:T(8,128)(2,1)S(1)} %shard_map.78), channel_id=1, source_target_pairs={{0,3},{1,2},{2,1},{3,0},{4,7},{5,6},{6,5},{7,4},{8,11},{9,10},{10,... | collective-permute-start | bytes 196616 | tf_op jit(solution)/shard_map/ppermute | solution.py:36
  18.8 4.7 %collective-permute-start.8 = (bf16[128,256]{1,0:T(8,128)(2,1)S(1)}, bf16[128,256]{1,0:T(8,128)(2,1)S(1)}, u32[]{:S(2)}, u32[]{:S(2)}) collective-permute-start(bf16[128,256]{1,0:T(8,128)(2,1)S(1)} %shard_map.79), channel_id=1, source_target_pairs={{0,5},{1,4},{2,7},{3,6},{4,1},{5,0},{6,3},{7,2},{8,13},{9,12},{10,... | collective-permute-start | bytes 196616 | tf_op jit(solution)/shard_map/ppermute | solution.py:36
  21.2 7.1 %collective-permute-start.4 = (bf16[128,512]{1,0:T(8,128)(2,1)S(1)}, bf16[128,512]{1,0:T(8,128)(2,1)S(1)}, u32[]{:S(2)}, u32[]{:S(2)}) collective-permute-start(bf16[128,512]{1,0:T(8,128)(2,1)S(1)} %shard_map.76), channel_id=1, source_target_pairs={{0,3},{1,2},{2,1},{3,0},{4,7},{5,6},{6,5},{7,4},{8,11},{9,10},{10,... | collective-permute-start | bytes 393224 | tf_op jit(solution)/shard_map/ppermute | solution.py:36
  21.9 6.5 %collective-permute-start.6 = (bf16[128,512]{1,0:T(8,128)(2,1)S(1)}, bf16[128,512]{1,0:T(8,128)(2,1)S(1)}, u32[]{:S(2)}, u32[]{:S(2)}) collective-permute-start(bf16[128,512]{1,0:T(8,128)(2,1)S(1)} %shard_map.77), channel_id=1, source_target_pairs={{0,5},{1,4},{2,7},{3,6},{4,1},{5,0},{6,3},{7,2},{8,13},{9,12},{10,... | collective-permute-start | bytes 393224 | tf_op jit(solution)/shard_map/ppermute | solution.py:36
  23.7 6.2 %collective-permute-start.12 = (bf16[128,256]{1,0:T(8,128)(2,1)S(1)}, bf16[128,256]{1,0:T(8,128)(2,1)S(1)}, u32[]{:S(2)}, u32[]{:S(2)}) collective-permute-start(bf16[128,256]{1,0:T(8,128)(2,1)S(1)} %shard_map.81.refs_4_), channel_id=1, source_target_pairs={{0,24},{8,0},{16,8},{24,16},{1,25},{9,1},{17,9},{25,17},{2,26},{10... | collective-permute-start | bytes 196616 | tf_op jit(solution)/shard_map/ppermute | solution.py:40
  27.4 7.5 %collective-permute-start.11 = (bf16[128,256]{1,0:T(8,128)(2,1)S(1)}, bf16[128,256]{1,0:T(8,128)(2,1)S(1)}, u32[]{:S(2)}, u32[]{:S(2)}) collective-permute-start(bf16[128,256]{1,0:T(8,128)(2,1)S(1)} %shard_map.81.refs_4_), channel_id=1, source_target_pairs={{0,16},{8,24},{16,0},{24,8},{1,17},{9,25},{17,1},{25,9},{2,18},{10... | collective-permute-start | bytes 196616 | tf_op jit(solution)/shard_map/ppermute | solution.py:40
  27.4 7.5 %collective-permute-start.10 = (bf16[128,256]{1,0:T(8,128)(2,1)S(1)}, bf16[128,256]{1,0:T(8,128)(2,1)S(1)}, u32[]{:S(2)}, u32[]{:S(2)}) collective-permute-start(bf16[128,256]{1,0:T(8,128)(2,1)S(1)} %shard_map.81.refs_4_), channel_id=1, source_target_pairs={{0,8},{8,16},{16,24},{24,0},{1,9},{9,17},{17,25},{25,1},{2,10},{10... | collective-permute-start | bytes 196616 | tf_op jit(solution)/shard_map/ppermute | solution.py:40

commit v3 on v2

--- a/solution.py
+++ b/solution.py
@@ -12,15 +12,19 @@
 EPSILON = 1e-05
 MASKED = -1e30
 LOG2E = 1.4426950408889634
-DIRECT = 8
+DIRECT = 4
 DOCS = 4
 GRANT = 8 << 20
 
 
 def partner(index, step, count):
-    if count & (count - 1) == 0:
-        return index ^ step
-    return (step - index) % count
+    if count & (count - 1):
+        raise ValueError("axis size")
+    return index ^ step
+
+
+def far_first(ring):
+    return list(range(ring - 1, 0, -1))
 
 
 def swap_dp(x, step, count):
@@ -36,8 +40,8 @@
     return lax.ppermute(x, ("dp", "section"), moves)
 
 
-def shift_ctx(x, by, ring):
-    return lax.ppermute(x, "ctx", [(i, (i + by) % ring) for i in range(ring)])
+def swap_ctx(x, step, ring):
+    return lax.ppermute(x, "ctx", [(i, partner(i, step, ring)) for i in range(ring)])
 
 
 def on_chip(shape, dtype):
@@ -62,34 +66,29 @@
     return [pltpu.with_memory_space_constraint(x, pltpu.HBM) for x in arrays]
 
 
-def cut_kernel(count, sequence, here_ref, rows_ref, gain_ref, *refs):
-    out_refs, held, sem = refs[: len(sequence)], refs[-2], refs[-1]
+def cut_kernel(count, sequence, here_ref, rows_ref, *refs):
+    out_refs, sem = refs[:-1], refs[-1]
     width = out_refs[0].shape[1]
-    begins = [pl.multiple_of(partner(here_ref[0], k, count) * width, width) for k in sequence]
-    copies = [
-        pltpu.make_async_copy(rows_ref.at[:, pl.ds(b, width)], held.at[i], sem.at[i])
-        for i, b in enumerate(begins)
-    ]
+    copies = []
+    for i, k in enumerate(sequence):
+        begin = pl.multiple_of(partner(here_ref[0], k, count) * width, width)
+        copies.append(
+            pltpu.make_async_copy(rows_ref.at[:, pl.ds(begin, width)], out_refs[i], sem.at[i])
+        )
     for copy in copies:
         copy.start()
-    for i, copy in enumerate(copies):
+    for copy in copies:
         copy.wait()
-        gain = gain_ref[:, pl.ds(begins[i], width)]
-        out_refs[i][...] = (held[i].astype(jnp.float32) * gain).astype(jnp.bfloat16)
-
-
-def cut(rows, gain, here, count, sequence):
+
+
+def cut(rows, here, count, sequence):
     height, features = rows.shape
-    width = features // count
     return local_call(
         functools.partial(cut_kernel, count, sequence),
-        [on_chip((height, width), jnp.bfloat16)] * len(sequence),
-        (here, *in_hbm(rows, gain)),
-        (pltpu.SMEM, pltpu.HBM, pltpu.VMEM),
-        scratch_shapes=[
-            pltpu.VMEM((len(sequence), height, width), jnp.bfloat16),
-            pltpu.SemaphoreType.DMA((len(sequence),)),
-        ],
+        [on_chip((height, features // count), jnp.bfloat16)] * len(sequence),
+        (here, *in_hbm(rows)),
+        (pltpu.SMEM, pltpu.HBM),
+        scratch_shapes=[pltpu.SemaphoreType.DMA((len(sequence),))],
     )
 
 
@@ -129,24 +128,30 @@
 def prepare_kernel(
     here_ref, rows_hbm, gain_ref, kw_hbm, vw_hbm, qw_hbm, order_ref, docs_ref, *refs
 ):
-    w_out, part_out, rows_ref, sem = refs[0], refs[1], refs[-2], refs[-1]
-    copies = [pltpu.make_async_copy(rows_hbm, rows_ref, sem.at[0])]
-    offset = 0
-    for i, weight in enumerate((kw_hbm, vw_hbm, qw_hbm)):
-        place = w_out.at[:, offset : offset + weight.shape[1]]
+    w_out, part_out = refs[:2]
+    rows_ref, w_ref, sem = refs[-3:]
+    half = qw_hbm.shape[1] // 2
+    copies, offset = [pltpu.make_async_copy(rows_hbm, rows_ref, sem.at[0])], 0
+    sources = (kw_hbm, qw_hbm.at[:, :half], vw_hbm, qw_hbm.at[:, half:])
+    for i, weight in enumerate(sources):
+        place = w_ref.at[:, offset : offset + weight.shape[1]]
         copies.append(pltpu.make_async_copy(weight, place, sem.at[1 + i]))
         offset += weight.shape[1]
     for copy in copies:
         copy.start()
     copies[0].wait()
-    if len(refs) == 5:
+    if len(refs) == 6:
         tell(rows_ref, order_ref, docs_ref, refs[2])
     width = w_out.shape[0]
     begin = pl.multiple_of(here_ref[0] * width, width)
-    part = rows_ref[:, pl.ds(begin, width)].astype(jnp.float32) * gain_ref[:, pl.ds(begin, width)]
     for copy in copies[1:]:
         copy.wait()
-    part_out[...] = product(part.astype(jnp.bfloat16), w_out[...])
+    step = 128
+    for i in range(0, width, step):
+        gain = column(gain_ref[:, pl.ds(pl.multiple_of(begin + i, step), step)])
+        scaled = w_ref[i : i + step, :].astype(jnp.float32) * gain
+        w_out[i : i + step, :] = scaled.astype(jnp.bfloat16)
+    part_out[...] = product(rows_ref[:, pl.ds(begin, width)], w_out[...])
 
 
 def prepare(here, rows, gain, weights, order, docs, with_meta):
@@ -160,7 +165,11 @@
         outs,
         (here, *in_hbm(rows, gain, *weights, order, docs)),
         (pltpu.SMEM, pltpu.HBM, pltpu.VMEM, *[pltpu.HBM] * 3, pltpu.SMEM, pltpu.VMEM),
-        scratch_shapes=[pltpu.VMEM(rows.shape, jnp.bfloat16), pltpu.SemaphoreType.DMA((4,))],
+        scratch_shapes=[
+            pltpu.VMEM(rows.shape, jnp.bfloat16),
+            pltpu.VMEM((depth, width), jnp.bfloat16),
+            pltpu.SemaphoreType.DMA((5,)),
+        ],
     )
 
 
@@ -230,8 +239,8 @@
 
 def summed(refs, start, size):
     total = 0.0
-    for ref, offset in refs:
-        total = total + ref[:, offset + start : offset + start + size].astype(jnp.float32)
+    for ref in refs:
+        total = total + ref[:, start : start + size].astype(jnp.float32)
     return total
 
 
@@ -239,48 +248,73 @@
     return x * cosine + pltpu.roll(x, x.shape[1] // 2, 1) * sine
 
 
-def mix_kernel(*refs):
-    parts, (kcos, ksin, level, out_ref) = [(r, 0) for r in refs[:-4]], refs[-4:]
-    size = kcos.shape[1]
-    keys = turn(summed(parts, 0, size), kcos[...], ksin[...])
-    out_ref[:, :size] = keys.astype(jnp.bfloat16)
-    out_ref[:, size:] = (summed(parts, size, size) * level[...]).astype(jnp.bfloat16)
-
-
-def mix(parts, kcos, ksin, level):
-    args = (*parts, kcos, ksin, level)
+def mix_kernel(own_ref, *refs):
+    parts, (kcos, ksin, level, out_ref) = refs[:-4], refs[-4:]
+    size, half = kcos.shape[1], own_ref.shape[1] // 2
+    keys = own_ref[:, :size].astype(jnp.float32) + summed(parts, 0, size)
+    values = own_ref[:, half : half + size].astype(jnp.float32) + summed(parts, size, size)
+    out_ref[:, :size] = turn(keys, kcos[...], ksin[...]).astype(jnp.bfloat16)
+    out_ref[:, size:] = (values * level[...]).astype(jnp.bfloat16)
+
+
+def mix(own, parts, kcos, ksin, level):
+    args = (own, *parts, kcos, ksin, level)
     rows, size = kcos.shape
     return local_call(
         mix_kernel, on_chip((rows, 2 * size), jnp.bfloat16), args, [pltpu.VMEM] * len(args)
     )
 
 
-def project_kernel(start, stop, x_ref, w_ref, out_ref):
-    out_ref[...] = product(x_ref[...], w_ref[:, start:stop])
-
-
-def project(x, weight, start, stop):
-    return local_call(
-        functools.partial(project_kernel, start, stop),
-        on_chip((x.shape[0], stop - start), jnp.bfloat16),
-        (x, weight),
-        [pltpu.VMEM] * 2,
-    )
-
-
-def attend_kernel(offsets, ring, at_ref, *refs):
-    count = len(offsets)
-    parts, kv_refs = list(zip(refs, offsets)), refs[count : count + ring]
+def far_kernel(x_ref, w_ref, kv_ref, left_ref, right_ref):
+    result = product(x_ref[...], w_ref[...])
+    size, half = kv_ref.shape[1] // 2, w_ref.shape[1] // 2
+    kv_ref[:, :size] = result[:, :size]
+    kv_ref[:, size:] = result[:, half : half + size]
+    left_ref[...] = result[:, size:half]
+    right_ref[...] = result[:, half + size :]
+
+
+def far_product(x, weight, size):
+    rows, half = x.shape[0], weight.shape[1] // 2
+    outs = [on_chip((rows, w), jnp.bfloat16) for w in (2 * size, half - size, half - size)]
+    return local_call(far_kernel, outs, (x, weight), [pltpu.VMEM] * 2)
+
+
+def project_kernel(right, start, size, x_ref, w_ref, *refs):
+    half, out_ref = w_ref.shape[1] // 2, refs[-1]
+    columns = [w_ref[:, h * half + start : h * half + start + size] for h in (0, 1)]
+    both = jnp.dot(
+        x_ref[...], jnp.concatenate(columns, axis=1), preferred_element_type=jnp.float32
+    )
+    for h in (0, 1):
+        part = both[:, h * size : (h + 1) * size]
+        if len(refs) == 2 and h == right:
+            part = part + refs[0][...].astype(jnp.float32)
+        out_ref[:, h * size : (h + 1) * size] = part.astype(jnp.bfloat16)
+
+
+def project(x, weight, more, right, start, size):
+    return local_call(
+        functools.partial(project_kernel, right, start, size),
+        on_chip((x.shape[0], 2 * size), jnp.bfloat16),
+        (x, weight, *more),
+        [pltpu.VMEM] * (2 + len(more)),
+    )
+
+
+def attend_kernel(count, steps, ring, at_ref, own_ref, *refs):
+    parts, kv_refs = refs[:count], refs[count : count + ring]
     qcos, qsin, bias, out_ref = refs[count + ring :]
     rows, size = qcos.shape
+    heads = out_ref.shape[1] // size
     keys = jnp.concatenate([ref[:, :size] for ref in kv_refs], axis=0)
     values = jnp.concatenate([ref[:, size:] for ref in kv_refs], axis=0)
-    here = [
-        pl.multiple_of(lax.rem(at_ref[0] - j + ring, ring) * rows, rows) for j in range(ring)
-    ]
+    here = [pl.multiple_of(partner(at_ref[0], j, ring) * rows, rows) for j in steps]
     masks = jnp.concatenate([bias[:, pl.ds(b, rows)] for b in here], axis=1)
-    for h in range(out_ref.shape[1] // size):
-        query = turn(summed(parts, h * size, size), qcos[...], qsin[...])
+    for h in range(heads):
+        place = own_place(h, heads, size)
+        query = own_ref[:, place : place + size].astype(jnp.float32)
+        query = turn(query + summed(parts, h * size, size), qcos[...], qsin[...])
         scores = lax.dot_general(
             query.astype(jnp.bfloat16),
             keys,
@@ -294,20 +328,26 @@
         out_ref[:, h * size : (h + 1) * size] = (mixed / total).astype(jnp.bfloat16)
 
 
-def attend(at, parts, offsets, kv, qcos, qsin, bias):
-    args = (at, *parts, *kv, qcos, qsin, bias)
-    width = parts[0].shape[1] - offsets[0]
-    return local_call(
-        functools.partial(attend_kernel, offsets, len(kv)),
-        jax.ShapeDtypeStruct((parts[0].shape[0], width), jnp.bfloat16),
+def own_place(head, heads, size):
+    return (head + (1 if head < heads // 2 else 2)) * size
+
+
+def attend(at, own, parts, kv, qcos, qsin, bias):
+    args = (at, own, *parts, *kv, qcos, qsin, bias)
+    steps = [0, *far_first(len(kv))]
+    return local_call(
+        functools.partial(attend_kernel, len(parts), steps, len(kv)),
+        jax.ShapeDtypeStruct(parts[0].shape, jnp.bfloat16),
         args,
         [pltpu.SMEM] + [pltpu.VMEM] * (len(args) - 1),
     )
 
 
-def attend_long(parts, offsets, everything, qcos, qsin, bias):
-    parts = [p[:, o:] for p, o in zip(parts, offsets)]
+def attend_long(own, parts, everything, qcos, qsin, bias):
     rows, width = parts[0].shape
+    heads, size = width // qcos.shape[1], qcos.shape[1]
+    places = [own_place(h, heads, size) for h in range(heads)]
+    parts = [*parts, jnp.concatenate([own[:, p : p + size] for p in places], axis=1)]
     size = qcos.shape[1]
     heads = width // size
     total_q = sum(p.astype(jnp.float32) for p in parts).reshape(rows, heads, size)
@@ -362,9 +402,11 @@
     size = key_weight.shape[2]
     here = lax.axis_index("dp").astype(jnp.int32)[None]
     at = lax.axis_index("ctx").astype(jnp.int32)[None]
-    away = [count - 1, *range(1, count - 1)]
+    if count != 4:
+        raise ValueError("axis size")
+    away = [3, 1, 2]
     weights = [key_weight[0], value_weight[0], query_weight[0]]
-    slabs = cut(rows_here, norm_gain, here, count, away)
+    slabs = cut(rows_here, here, count, away)
     arrived = {}
     for k, slab in zip(away, slabs):
         arrived[k] = swap_dp(slab, k, count)
@@ -372,30 +414,35 @@
     weight, part, *meta = prepare(
         here, rows_here, norm_gain, weights, block_order[0], doc_ids[0], ring <= DIRECT
     )
-    parts = [to_next_section(part, 0, count, sections)]
+    own = to_next_section(part, 0, count, sections)
     meta = meta[0] if meta else describe_long(rows_here, block_order[0], doc_ids[0])
     meta = lax.ppermute(meta, "section", [(i, (i + 1) % sections) for i in range(sections)])
     kcos, ksin, qcos, qsin, level, bias = tables(at, meta, row_count, size, length)
 
-    part = project(arrived[away[0]], weight, 0, weight.shape[1])
-    parts.append(to_next_section(part, away[0], count, sections))
-    kv_parts, q_parts, offsets = list(parts), list(parts), [2 * size, 2 * size]
-    for k in away[1:]:
-        part = project(arrived[k], weight, 0, 2 * size)
+    part, *halves = far_product(arrived[3], weight, size)
+    kv_parts = [to_next_section(part, 3, count, sections)]
+    relayed = {}
+    for k, half in zip((1, 2), halves):
+        relayed[3 - k] = swap_dp(half, k, count)
+
+    q_parts = []
+    for k in (1, 2):
+        right = int(k == 1)
+        width = query_weight.shape[2] // 2
+        part = project(arrived[k], weight, [], right, 0, size)
         kv_parts.append(to_next_section(part, k, count, sections))
-        part = project(arrived[k], weight, 2 * size, weight.shape[1])
+        part = project(arrived[k], weight, [relayed[k]], right, size, width)
         q_parts.append(to_next_section(part, k, count, sections))
-        offsets.append(0)
-
-    kv = mix(kv_parts, kcos, ksin, level)
+
+    kv = mix(own, kv_parts, kcos, ksin, level)
     if ring <= DIRECT:
         pieces = [kv]
-        for j in range(1, ring):
-            pieces.append(shift_ctx(kv, j, ring))
-        out = attend(at, q_parts, offsets, pieces, qcos, qsin, bias)
+        for j in far_first(ring):
+            pieces.append(swap_ctx(kv, j, ring))
+        out = attend(at, own, q_parts, pieces, qcos, qsin, bias)
     else:
         everything = lax.all_gather(kv, "ctx", axis=0, tiled=True)
-        out = attend_long(q_parts, offsets, everything, qcos, qsin, bias)
+        out = attend_long(own, q_parts, everything, qcos, qsin, bias)
     return out[None, None]
 
 

time: 37.2 us -> 38.5 us (1.035)
  starting transfers between devices: 16.1 us -> 17.9 us
  Pallas kernels: 8.71 us -> 8.22 us
    ppermute x3 -> x5, starting transfers between devices: 4.63 us -> 8.18 us  [swap_dp(): lax.ppermute(x, 'dp', [(i, partner(i, step, count)) for i in range(count)])]
    ppermute x1, starting transfers between devices: 2.66 us -> 0.01 us  [local(): lax.ppermute(meta, 'section', [(i, (i + 1) % sections) for i in range(sec...]
    ppermute x6, starting transfers between devices: 4.18 us -> 5.31 us  [to_next_section(): return lax.ppermute(x, ('dp', 'section'), moves)]
    ppermute x6, waiting for transfers between devices: 0.14 us -> 1.1 us  [to_next_section(): return lax.ppermute(x, ('dp', 'section'), moves)]
    ppermute x3, waiting for transfers between devices: 6.5 us -> 5.84 us  [swap_ctx(): lax.ppermute(x, 'ctx', [(i, partner(i, step, ring)) for i in range(ring)])]
    pallas_call x10, Pallas kernels: 8.71 us -> 8.22 us  [local_call(): pl.pallas_call(kernel, out_shape=out_shape, in_specs=in_specs, compiler_p...]
    ppermute x3 -> x5, waiting for transfers between devices: 5.24 us -> 5.1 us  [swap_dp(): lax.ppermute(x, 'dp', [(i, partner(i, step, count)) for i in range(count)])]
  transfers between devices with their start and end apart: 13 -> 15, of which waited for: 5 -> 6; matrix products, arithmetic and copies ran while one was open for 0% -> 0% of each run, Pallas kernels for 13% -> 13%
where the time goes in v3:
time: 38.5 us; the launch traced here: 38.3 us
  starting transfers between devices  17.9 us (46%)
  waiting for transfers between devices  12 us (31%)
  Pallas kernels  8.22 us (21%)
    pallas_call x10, Pallas kernels, local_call(): pl.pallas_call(kernel, out_shape=out_shape, in_specs=in_specs, compiler_p...  8.22 us
    ppermute x5, starting transfers between devices, swap_dp(): lax.ppermute(x, 'dp', [(i, partner(i, step, count)) for i in range(count)])  8.18 us
    ppermute x3, waiting for transfers between devices, swap_ctx(): lax.ppermute(x, 'ctx', [(i, partner(i, step, ring)) for i in range(ring)])  5.84 us
    ppermute x6, starting transfers between devices, to_next_section(): return lax.ppermute(x, ('dp', 'section'), moves)  5.31 us
    ppermute x5, waiting for transfers between devices, swap_dp(): lax.ppermute(x, 'dp', [(i, partner(i, step, count)) for i in range(count)])  5.1 us
    ppermute x3, starting transfers between devices, swap_ctx(): lax.ppermute(x, 'ctx', [(i, partner(i, step, ring)) for i in range(ring)])  4.45 us
    ppermute x6, waiting for transfers between devices, to_next_section(): return lax.ppermute(x, ('dp', 'section'), moves)  1.1 us
  transfers between devices with their start and end apart: 15, of which 6 were waited for; matrix products, arithmetic and copies ran while one was open for 0% of the time, Pallas kernels for 13%

profile of v3, /device:TPU:0, one launch (start us, length us, event | category | flops | bytes accessed | tf_op | source)
XLA Modules:
  0.0 38.3 jit_solution(8561819149935197585)
XLA Ops:
  0.0 1.1 %shard_map.74 = (bf16[128,1024]{1,0:T(8,128)(2,1)S(1)}, bf16[128,1024]{1,0:T(8,128)(2,1)S(1)}, bf16[128,1024]{1,0:T(8,128)(2,1)S(1)}) custom-call(s32[1]{0:T(128)} %bitcast.1.here_ref, bf16[128,4096]{1,0:T(8,128)(2,1)} %bitcast.9), custom_call_target="tpu_custom_call" | custom-call | tf_op jit(solution)/shard_map/pallas_call | solution.py:56
  1.1 4.0 %collective-permute-start.2 = (bf16[128,1024]{1,0:T(8,128)(2,1)S(1)}, bf16[128,1024]{1,0:T(8,128)(2,1)S(1)}, u32[]{:S(2)}, u32[]{:S(2)}) collective-permute-start(bf16[128,1024]{1,0:T(8,128)(2,1)S(1)} %get-tuple-element.23), channel_id=1, source_target_pairs={{0,6},{2,4},{4,2},{6,0},{1,7},{3,5},{5,3},{7,1},{8,14},{10,12},{12... | collective-permute-start | bytes 786440 | tf_op jit(solution)/shard_map/ppermute | solution.py:31
  5.1 0.5 %collective-permute-start.1 = (bf16[128,1024]{1,0:T(8,128)(2,1)S(1)}, bf16[128,1024]{1,0:T(8,128)(2,1)S(1)}, u32[]{:S(2)}, u32[]{:S(2)}) collective-permute-start(bf16[128,1024]{1,0:T(8,128)(2,1)S(1)} %get-tuple-element.21), channel_id=1, source_target_pairs={{0,2},{2,0},{4,6},{6,4},{1,3},{3,1},{5,7},{7,5},{8,10},{10,8},{12,... | collective-permute-start | bytes 786440 | tf_op jit(solution)/shard_map/ppermute | solution.py:31
  5.8 3.2 %shard_map.73 = (bf16[1024,768]{1,0:T(8,128)(2,1)S(1)}, bf16[128,768]{1,0:T(8,128)(2,1)S(1)}, f32[1,1152]{1,0:T(1,128)S(1)}) custom-call(s32[1]{0:T(128)} %bitcast.1.here_ref, bf16[128,4096]{1,0:T(8,128)(2,1)} %bitcast.10, f32[1,4096]{1,0:T(1,128)} %gain_ref.1, bf16[1024,128]{1,0:T(8,128)(2,1)} %bitcast.12, bf16[1024,128]{1,0:T(8,128)(2,1)} %bitcast.13, ...), custom_call_target="tpu_custom_call" | custom-call | tf_op jit(solution)/shard_map/pallas_call | solution.py:56
  9.0 3.3 %collective-permute-done.2.x_ref = bf16[128,1024]{1,0:T(8,128)(2,1)S(1)} collective-permute-done((bf16[128,1024]{1,0:T(8,128)(2,1)S(1)}, bf16[128,1024]{1,0:T(8,128)(2,1)S(1)}, u32[]{:S(2)}, u32[]{:S(2)}) %collective-permute-start.2) | collective-permute-done | bytes 262176 | tf_op jit(solution)/shard_map/ppermute | solution.py:31
  12.3 0.4 shard_map.75
  12.7 2.1 %collective-permute-start.3 = (bf16[128,256]{1,0:T(8,128)(2,1)S(1)}, bf16[128,256]{1,0:T(8,128)(2,1)S(1)}, u32[]{:S(2)}, u32[]{:S(2)}) collective-permute-start(bf16[128,256]{1,0:T(8,128)(2,1)S(1)} %get-tuple-element.24), channel_id=1, source_target_pairs={{0,4},{2,6},{4,0},{6,2},{1,5},{3,7},{5,1},{7,3},{8,12},{10,14},{12... | collective-permute-start | bytes 196616 | tf_op jit(solution)/shard_map/ppermute | solution.py:31
  14.8 1.5 %collective-permute-start.6 = (bf16[128,256]{1,0:T(8,128)(2,1)S(1)}, bf16[128,256]{1,0:T(8,128)(2,1)S(1)}, u32[]{:S(2)}, u32[]{:S(2)}) collective-permute-start(bf16[128,256]{1,0:T(8,128)(2,1)S(1)} %get-tuple-element.26), channel_id=1, source_target_pairs={{0,2},{2,0},{4,6},{6,4},{1,3},{3,1},{5,7},{7,5},{8,10},{10,8},{12,... | collective-permute-start | bytes 196616 | tf_op jit(solution)/shard_map/ppermute | solution.py:31
  16.3 1.8 %collective-permute-done.1.x_ref = bf16[128,1024]{1,0:T(8,128)(2,1)S(1)} collective-permute-done((bf16[128,1024]{1,0:T(8,128)(2,1)S(1)}, bf16[128,1024]{1,0:T(8,128)(2,1)S(1)}, u32[]{:S(2)}, u32[]{:S(2)}) %collective-permute-start.1) | collective-permute-done | bytes 262176 | tf_op jit(solution)/shard_map/ppermute | solution.py:31
  18.1 0.2 shard_map.78
  18.3 1.7 %collective-permute-start.9 = (bf16[128,256]{1,0:T(8,128)(2,1)S(1)}, bf16[128,256]{1,0:T(8,128)(2,1)S(1)}, u32[]{:S(2)}, u32[]{:S(2)}) collective-permute-start(bf16[128,256]{1,0:T(8,128)(2,1)S(1)} %shard_map.78), channel_id=1, source_target_pairs={{0,3},{1,2},{2,1},{3,0},{4,7},{5,6},{6,5},{7,4},{8,11},{9,10},{10,... | collective-permute-start | bytes 196616 | tf_op jit(solution)/shard_map/ppermute | solution.py:40
  20.0 0.2 shard_map.79
  20.4 1.6 %collective-permute-start.8 = (bf16[128,256]{1,0:T(8,128)(2,1)S(1)}, bf16[128,256]{1,0:T(8,128)(2,1)S(1)}, u32[]{:S(2)}, u32[]{:S(2)}) collective-permute-start(bf16[128,256]{1,0:T(8,128)(2,1)S(1)} %get-tuple-element.27), channel_id=1, source_target_pairs={{0,7},{1,6},{2,5},{3,4},{4,3},{5,2},{6,1},{7,0},{8,15},{9,14},{10,... | collective-permute-start | bytes 196616 | tf_op jit(solution)/shard_map/ppermute | solution.py:40
  22.0 0.3 shard_map.76
  22.3 0.3 shard_map.77
  22.7 0.5 %collective-permute-start.7 = (bf16[128,512]{1,0:T(8,128)(2,1)S(1)}, bf16[128,512]{1,0:T(8,128)(2,1)S(1)}, u32[]{:S(2)}, u32[]{:S(2)}) collective-permute-start(bf16[128,512]{1,0:T(8,128)(2,1)S(1)} %shard_map.77), channel_id=1, source_target_pairs={{0,5},{1,4},{2,7},{3,6},{4,1},{5,0},{6,3},{7,2},{8,13},{9,12},{10,... | collective-permute-start | bytes 393224 | tf_op jit(solution)/shard_map/ppermute | solution.py:40
  23.2 1.3 %collective-permute-start.4 = (bf16[128,512]{1,0:T(8,128)(2,1)S(1)}, bf16[128,512]{1,0:T(8,128)(2,1)S(1)}, u32[]{:S(2)}, u32[]{:S(2)}) collective-permute-start(bf16[128,512]{1,0:T(8,128)(2,1)S(1)} %shard_map.76), channel_id=1, source_target_pairs={{0,3},{1,2},{2,1},{3,0},{4,7},{5,6},{6,5},{7,4},{8,11},{9,10},{10,... | collective-permute-start | bytes 393224 | tf_op jit(solution)/shard_map/ppermute | solution.py:40
  24.5 0.3 shard_map.80
  24.8 1.1 %collective-permute-done.10.refs_2_ = bf16[128,256]{1,0:T(8,128)(2,1)S(1)} collective-permute-done((bf16[128,256]{1,0:T(8,128)(2,1)S(1)}, bf16[128,256]{1,0:T(8,128)(2,1)S(1)}, u32[]{:S(2)}, u32[]{:S(2)}) %collective-permute-start.10) | collective-permute-done | bytes 65568 | tf_op jit(solution)/shard_map/ppermute | solution.py:40
  26.0 1.6 %collective-permute-start.14 = (bf16[128,256]{1,0:T(8,128)(2,1)S(1)}, bf16[128,256]{1,0:T(8,128)(2,1)S(1)}, u32[]{:S(2)}, u32[]{:S(2)}) collective-permute-start(bf16[128,256]{1,0:T(8,128)(2,1)S(1)} %shard_map.81.refs_2_), channel_id=1, source_target_pairs={{0,8},{8,0},{16,24},{24,16},{1,9},{9,1},{17,25},{25,17},{2,10},{10... | collective-permute-start | bytes 196616 | tf_op jit(solution)/shard_map/ppermute | solution.py:44
  27.7 2.6 %collective-permute-start.13 = (bf16[128,256]{1,0:T(8,128)(2,1)S(1)}, bf16[128,256]{1,0:T(8,128)(2,1)S(1)}, u32[]{:S(2)}, u32[]{:S(2)}) collective-permute-start(bf16[128,256]{1,0:T(8,128)(2,1)S(1)} %shard_map.81.refs_2_), channel_id=1, source_target_pairs={{0,16},{8,24},{16,0},{24,8},{1,17},{9,25},{17,1},{25,9},{2,18},{10... | collective-permute-start | bytes 196616 | tf_op jit(solution)/shard_map/ppermute | solution.py:44
  30.6 4.1 %collective-permute-done.13.refs_4_ = bf16[128,256]{1,0:T(8,128)(2,1)S(1)} collective-permute-done((bf16[128,256]{1,0:T(8,128)(2,1)S(1)}, bf16[128,256]{1,0:T(8,128)(2,1)S(1)}, u32[]{:S(2)}, u32[]{:S(2)}) %collective-permute-start.13) | collective-permute-done | bytes 65568 | tf_op jit(solution)/shard_map/ppermute | solution.py:44
  34.7 1.7 %collective-permute-done.12.refs_3_ = bf16[128,256]{1,0:T(8,128)(2,1)S(1)} collective-permute-done((bf16[128,256]{1,0:T(8,128)(2,1)S(1)}, bf16[128,256]{1,0:T(8,128)(2,1)S(1)}, u32[]{:S(2)}, u32[]{:S(2)}) %collective-permute-start.12) | collective-permute-done | bytes 65568 | tf_op jit(solution)/shard_map/ppermute | solution.py:44
  36.3 2.0 %shard_map.82 = bf16[128,512]{1,0:T(8,128)(2,1)} custom-call(s32[1]{0:T(128)} %bitcast.at_ref, bf16[128,768]{1,0:T(8,128)(2,1)S(1)} %collective-permute-done.own_ref, bf16[128,512]{1,0:T(8,128)(2,1)S(1)} %collective-permute-done.4.refs_0_, bf16[128,512]{1,0:T(8,128)(2,1)S(1)} %collective-permute-done.7.refs_1_, bf16[128,256]{1,0:T(8,128)(2,1)S(1)} %shard_map.81.refs_2_, ...), custom_call_target="tpu_custom_call" | custom-call | tf_op jit(solution)/shard_map/pallas_call | solution.py:56
  (16 shorter events, 0.8 us)
Async XLA Ops:
  1.1 11.2 %collective-permute-start.2 = (bf16[128,1024]{1,0:T(8,128)(2,1)S(1)}, bf16[128,1024]{1,0:T(8,128)(2,1)S(1)}, u32[]{:S(2)}, u32[]{:S(2)}) collective-permute-start(bf16[128,1024]{1,0:T(8,128)(2,1)S(1)} %get-tuple-element.23), channel_id=1, source_target_pairs={{0,6},{2,4},{4,2},{6,0},{1,7},{3,5},{5,3},{7,1},{8,14},{10,12},{12... | collective-permute-start | bytes 786440 | tf_op jit(solution)/shard_map/ppermute | solution.py:31
  5.1 12.9 %collective-permute-start.1 = (bf16[128,1024]{1,0:T(8,128)(2,1)S(1)}, bf16[128,1024]{1,0:T(8,128)(2,1)S(1)}, u32[]{:S(2)}, u32[]{:S(2)}) collective-permute-start(bf16[128,1024]{1,0:T(8,128)(2,1)S(1)} %get-tuple-element.21), channel_id=1, source_target_pairs={{0,2},{2,0},{4,6},{6,4},{1,3},{3,1},{5,7},{7,5},{8,10},{10,8},{12,... | collective-permute-start | bytes 786440 | tf_op jit(solution)/shard_map/ppermute | solution.py:31
  5.7 12.6 %collective-permute-start.5 = (bf16[128,1024]{1,0:T(8,128)(2,1)S(1)}, bf16[128,1024]{1,0:T(8,128)(2,1)S(1)}, u32[]{:S(2)}, u32[]{:S(2)}) collective-permute-start(bf16[128,1024]{1,0:T(8,128)(2,1)S(1)} %get-tuple-element.25), channel_id=1, source_target_pairs={{0,4},{2,6},{4,0},{6,2},{1,5},{3,7},{5,1},{7,3},{8,12},{10,14},{12... | collective-permute-start | bytes 786440 | tf_op jit(solution)/shard_map/ppermute | solution.py:31
  8.9 14.2 %collective-permute-start = (bf16[128,768]{1,0:T(8,128)(2,1)S(1)}, bf16[128,768]{1,0:T(8,128)(2,1)S(1)}, u32[]{:S(2)}, u32[]{:S(2)}) collective-permute-start(bf16[128,768]{1,0:T(8,128)(2,1)S(1)} %get-tuple-element.20), channel_id=1, source_target_pairs={{0,1},{1,0},{2,3},{3,2},{4,5},{5,4},{6,7},{7,6},{8,9},{9,8},{10,11... | collective-permute-start | bytes 589832 | tf_op jit(solution)/shard_map/ppermute | solution.py:40
  12.7 7.5 %collective-permute-start.3 = (bf16[128,256]{1,0:T(8,128)(2,1)S(1)}, bf16[128,256]{1,0:T(8,128)(2,1)S(1)}, u32[]{:S(2)}, u32[]{:S(2)}) collective-permute-start(bf16[128,256]{1,0:T(8,128)(2,1)S(1)} %get-tuple-element.24), channel_id=1, source_target_pairs={{0,4},{2,6},{4,0},{6,2},{1,5},{3,7},{5,1},{7,3},{8,12},{10,14},{12... | collective-permute-start | bytes 196616 | tf_op jit(solution)/shard_map/ppermute | solution.py:31
  14.8 5.6 %collective-permute-start.6 = (bf16[128,256]{1,0:T(8,128)(2,1)S(1)}, bf16[128,256]{1,0:T(8,128)(2,1)S(1)}, u32[]{:S(2)}, u32[]{:S(2)}) collective-permute-start(bf16[128,256]{1,0:T(8,128)(2,1)S(1)} %get-tuple-element.26), channel_id=1, source_target_pairs={{0,2},{2,0},{4,6},{6,4},{1,3},{3,1},{5,7},{7,5},{8,10},{10,8},{12,... | collective-permute-start | bytes 196616 | tf_op jit(solution)/shard_map/ppermute | solution.py:31
  18.0 4.6 %collective-permute-start.11 = (f32[1,1152]{1,0:T(1,128)S(1)}, f32[1,1152]{1,0:T(1,128)S(1)}, u32[]{:S(2)}, u32[]{:S(2)}) collective-permute-start(f32[1,1152]{1,0:T(1,128)S(1)} %get-tuple-element.28), channel_id=1, source_target_pairs={{0,1},{1,0},{2,3},{3,2},{4,5},{5,4},{6,7},{7,6},{8,9},{9,8},{10,11... | collective-permute-start | bytes 13832 | tf_op jit(solution)/shard_map/ppermute | solution.py:419
  18.3 6.5 %collective-permute-start.9 = (bf16[128,256]{1,0:T(8,128)(2,1)S(1)}, bf16[128,256]{1,0:T(8,128)(2,1)S(1)}, u32[]{:S(2)}, u32[]{:S(2)}) collective-permute-start(bf16[128,256]{1,0:T(8,128)(2,1)S(1)} %shard_map.78), channel_id=1, source_target_pairs={{0,3},{1,2},{2,1},{3,0},{4,7},{5,6},{6,5},{7,4},{8,11},{9,10},{10,... | collective-permute-start | bytes 196616 | tf_op jit(solution)/shard_map/ppermute | solution.py:40
  20.2 5.7 %collective-permute-start.10 = (bf16[128,256]{1,0:T(8,128)(2,1)S(1)}, bf16[128,256]{1,0:T(8,128)(2,1)S(1)}, u32[]{:S(2)}, u32[]{:S(2)}) collective-permute-start(bf16[128,256]{1,0:T(8,128)(2,1)S(1)} %shard_map.79), channel_id=1, source_target_pairs={{0,5},{1,4},{2,7},{3,6},{4,1},{5,0},{6,3},{7,2},{8,13},{9,12},{10,... | collective-permute-start | bytes 196616 | tf_op jit(solution)/shard_map/ppermute | solution.py:40
  20.4 5.5 %collective-permute-start.8 = (bf16[128,256]{1,0:T(8,128)(2,1)S(1)}, bf16[128,256]{1,0:T(8,128)(2,1)S(1)}, u32[]{:S(2)}, u32[]{:S(2)}) collective-permute-start(bf16[128,256]{1,0:T(8,128)(2,1)S(1)} %get-tuple-element.27), channel_id=1, source_target_pairs={{0,7},{1,6},{2,5},{3,4},{4,3},{5,2},{6,1},{7,0},{8,15},{9,14},{10,... | collective-permute-start | bytes 196616 | tf_op jit(solution)/shard_map/ppermute | solution.py:40
  22.7 13.7 %collective-permute-start.7 = (bf16[128,512]{1,0:T(8,128)(2,1)S(1)}, bf16[128,512]{1,0:T(8,128)(2,1)S(1)}, u32[]{:S(2)}, u32[]{:S(2)}) collective-permute-start(bf16[128,512]{1,0:T(8,128)(2,1)S(1)} %shard_map.77), channel_id=1, source_target_pairs={{0,5},{1,4},{2,7},{3,6},{4,1},{5,0},{6,3},{7,2},{8,13},{9,12},{10,... | collective-permute-start | bytes 393224 | tf_op jit(solution)/shard_map/ppermute | solution.py:40
  23.2 13.2 %collective-permute-start.4 = (bf16[128,512]{1,0:T(8,128)(2,1)S(1)}, bf16[128,512]{1,0:T(8,128)(2,1)S(1)}, u32[]{:S(2)}, u32[]{:S(2)}) collective-permute-start(bf16[128,512]{1,0:T(8,128)(2,1)S(1)} %shard_map.76), channel_id=1, source_target_pairs={{0,3},{1,2},{2,1},{3,0},{4,7},{5,6},{6,5},{7,4},{8,11},{9,10},{10,... | collective-permute-start | bytes 393224 | tf_op jit(solution)/shard_map/ppermute | solution.py:40
  26.0 4.5 %collective-permute-start.14 = (bf16[128,256]{1,0:T(8,128)(2,1)S(1)}, bf16[128,256]{1,0:T(8,128)(2,1)S(1)}, u32[]{:S(2)}, u32[]{:S(2)}) collective-permute-start(bf16[128,256]{1,0:T(8,128)(2,1)S(1)} %shard_map.81.refs_2_), channel_id=1, source_target_pairs={{0,8},{8,0},{16,24},{24,16},{1,9},{9,1},{17,25},{25,17},{2,10},{10... | collective-permute-start | bytes 196616 | tf_op jit(solution)/shard_map/ppermute | solution.py:44
  27.7 7.0 %collective-permute-start.13 = (bf16[128,256]{1,0:T(8,128)(2,1)S(1)}, bf16[128,256]{1,0:T(8,128)(2,1)S(1)}, u32[]{:S(2)}, u32[]{:S(2)}) collective-permute-start(bf16[128,256]{1,0:T(8,128)(2,1)S(1)} %shard_map.81.refs_2_), channel_id=1, source_target_pairs={{0,16},{8,24},{16,0},{24,8},{1,17},{9,25},{17,1},{25,9},{2,18},{10... | collective-permute-start | bytes 196616 | tf_op jit(solution)/shard_map/ppermute | solution.py:44
  30.3 6.1 %collective-permute-start.12 = (bf16[128,256]{1,0:T(8,128)(2,1)S(1)}, bf16[128,256]{1,0:T(8,128)(2,1)S(1)}, u32[]{:S(2)}, u32[]{:S(2)}) collective-permute-start(bf16[128,256]{1,0:T(8,128)(2,1)S(1)} %shard_map.81.refs_2_), channel_id=1, source_target_pairs={{0,24},{8,16},{16,8},{24,0},{1,25},{9,17},{17,9},{25,1},{2,26},{10... | collective-permute-start | bytes 196616 | tf_op jit(solution)/shard_map/ppermute | solution.py:44

commit v4 on v3

--- a/solution.py
+++ b/solution.py
@@ -24,7 +24,7 @@
 
 
 def far_first(ring):
-    return list(range(ring - 1, 0, -1))
+    return [3, 2, 1] if ring == 4 else list(range(ring - 1, 0, -1))
 
 
 def swap_dp(x, step, count):
@@ -304,13 +304,15 @@
 
 def attend_kernel(count, steps, ring, at_ref, own_ref, *refs):
     parts, kv_refs = refs[:count], refs[count : count + ring]
-    qcos, qsin, bias, out_ref = refs[count + ring :]
+    qcos, qsin, bias, out_ref, held, sem = refs[count + ring :]
     rows, size = qcos.shape
     heads = out_ref.shape[1] // size
     keys = jnp.concatenate([ref[:, :size] for ref in kv_refs], axis=0)
     values = jnp.concatenate([ref[:, size:] for ref in kv_refs], axis=0)
+    values = jnp.concatenate([values, jnp.ones_like(values)], axis=1)
     here = [pl.multiple_of(partner(at_ref[0], j, ring) * rows, rows) for j in steps]
     masks = jnp.concatenate([bias[:, pl.ds(b, rows)] for b in here], axis=1)
+    copies = []
     for h in range(heads):
         place = own_place(h, heads, size)
         query = own_ref[:, place : place + size].astype(jnp.float32)
@@ -323,9 +325,13 @@
         )
         scores = scores + masks
         probs = jnp.exp2(scores - jnp.max(scores, axis=-1, keepdims=True))
-        total = jnp.sum(probs, axis=-1, keepdims=True)
         mixed = jnp.dot(probs.astype(jnp.bfloat16), values, preferred_element_type=jnp.float32)
-        out_ref[:, h * size : (h + 1) * size] = (mixed / total).astype(jnp.bfloat16)
+        held[h] = (mixed[:, :size] / mixed[:, size:]).astype(jnp.bfloat16)
+        place = out_ref.at[:, h * size : (h + 1) * size]
+        copies.append(pltpu.make_async_copy(held.at[h], place, sem.at[h]))
+        copies[-1].start()
+    for copy in copies:
+        copy.wait()
 
 
 def own_place(head, heads, size):
@@ -334,12 +340,19 @@
 
 def attend(at, own, parts, kv, qcos, qsin, bias):
     args = (at, own, *parts, *kv, qcos, qsin, bias)
+    rows, width = parts[0].shape
+    heads = width // qcos.shape[1]
     steps = [0, *far_first(len(kv))]
     return local_call(
         functools.partial(attend_kernel, len(parts), steps, len(kv)),
         jax.ShapeDtypeStruct(parts[0].shape, jnp.bfloat16),
         args,
         [pltpu.SMEM] + [pltpu.VMEM] * (len(args) - 1),
+        out_specs=pl.BlockSpec(memory_space=pltpu.HBM),
+        scratch_shapes=[
+            pltpu.VMEM((heads, rows, width // heads), jnp.bfloat16),
+            pltpu.SemaphoreType.DMA((heads,)),
+        ],
     )
 
 

time: 38.5 us -> 38 us (0.987)
  Pallas kernels: 8.22 us -> 7.68 us
    pallas_call x10, Pallas kernels: 8.22 us -> 7.68 us  [local_call(): pl.pallas_call(kernel, out_shape=out_shape, in_specs=in_specs, compiler_p...]
where the time goes in v4:
time: 38 us; the launch traced here: 37.8 us
  starting transfers between devices  17.9 us (47%)
  waiting for transfers between devices  12 us (32%)
  Pallas kernels  7.68 us (20%)
    ppermute x5, starting transfers between devices, swap_dp(): lax.ppermute(x, 'dp', [(i, partner(i, step, count)) for i in range(count)])  8.18 us
    pallas_call x10, Pallas kernels, local_call(): pl.pallas_call(kernel, out_shape=out_shape, in_specs=in_specs, compiler_p...  7.68 us
    ppermute x3, waiting for transfers between devices, swap_ctx(): lax.ppermute(x, 'ctx', [(i, partner(i, step, ring)) for i in range(ring)])  5.84 us
    ppermute x6, starting transfers between devices, to_next_section(): return lax.ppermute(x, ('dp', 'section'), moves)  5.31 us
    ppermute x5, waiting for transfers between devices, swap_dp(): lax.ppermute(x, 'dp', [(i, partner(i, step, count)) for i in range(count)])  5.1 us
    ppermute x3, starting transfers between devices, swap_ctx(): lax.ppermute(x, 'ctx', [(i, partner(i, step, ring)) for i in range(ring)])  4.45 us
    ppermute x6, waiting for transfers between devices, to_next_section(): return lax.ppermute(x, ('dp', 'section'), moves)  1.1 us
  transfers between devices with their start and end apart: 15, of which 6 were waited for; matrix products, arithmetic and copies ran while one was open for 0% of the time, Pallas kernels for 13%

profile of v4, /device:TPU:0, one launch (start us, length us, event | category | flops | bytes accessed | tf_op | source)
XLA Modules:
  0.0 37.8 jit_solution(5492110049432946588)
XLA Ops:
  0.0 1.1 %shard_map.74 = (bf16[128,1024]{1,0:T(8,128)(2,1)S(1)}, bf16[128,1024]{1,0:T(8,128)(2,1)S(1)}, bf16[128,1024]{1,0:T(8,128)(2,1)S(1)}) custom-call(s32[1]{0:T(128)} %bitcast.1.here_ref, bf16[128,4096]{1,0:T(8,128)(2,1)} %bitcast.9), custom_call_target="tpu_custom_call" | custom-call | tf_op jit(solution)/shard_map/pallas_call | solution.py:56
  1.1 4.0 %collective-permute-start.2 = (bf16[128,1024]{1,0:T(8,128)(2,1)S(1)}, bf16[128,1024]{1,0:T(8,128)(2,1)S(1)}, u32[]{:S(2)}, u32[]{:S(2)}) collective-permute-start(bf16[128,1024]{1,0:T(8,128)(2,1)S(1)} %get-tuple-element.23), channel_id=1, source_target_pairs={{0,6},{2,4},{4,2},{6,0},{1,7},{3,5},{5,3},{7,1},{8,14},{10,12},{12... | collective-permute-start | bytes 786440 | tf_op jit(solution)/shard_map/ppermute | solution.py:31
  5.1 0.5 %collective-permute-start.1 = (bf16[128,1024]{1,0:T(8,128)(2,1)S(1)}, bf16[128,1024]{1,0:T(8,128)(2,1)S(1)}, u32[]{:S(2)}, u32[]{:S(2)}) collective-permute-start(bf16[128,1024]{1,0:T(8,128)(2,1)S(1)} %get-tuple-element.21), channel_id=1, source_target_pairs={{0,2},{2,0},{4,6},{6,4},{1,3},{3,1},{5,7},{7,5},{8,10},{10,8},{12,... | collective-permute-start | bytes 786440 | tf_op jit(solution)/shard_map/ppermute | solution.py:31
  5.8 3.2 %shard_map.73 = (bf16[1024,768]{1,0:T(8,128)(2,1)S(1)}, bf16[128,768]{1,0:T(8,128)(2,1)S(1)}, f32[1,1152]{1,0:T(1,128)S(1)}) custom-call(s32[1]{0:T(128)} %bitcast.1.here_ref, bf16[128,4096]{1,0:T(8,128)(2,1)} %bitcast.10, f32[1,4096]{1,0:T(1,128)} %gain_ref.1, bf16[1024,128]{1,0:T(8,128)(2,1)} %bitcast.12, bf16[1024,128]{1,0:T(8,128)(2,1)} %bitcast.13, ...), custom_call_target="tpu_custom_call" | custom-call | tf_op jit(solution)/shard_map/pallas_call | solution.py:56
  9.0 3.3 %collective-permute-done.2.x_ref = bf16[128,1024]{1,0:T(8,128)(2,1)S(1)} collective-permute-done((bf16[128,1024]{1,0:T(8,128)(2,1)S(1)}, bf16[128,1024]{1,0:T(8,128)(2,1)S(1)}, u32[]{:S(2)}, u32[]{:S(2)}) %collective-permute-start.2) | collective-permute-done | bytes 262176 | tf_op jit(solution)/shard_map/ppermute | solution.py:31
  12.3 0.4 shard_map.75
  12.7 2.1 %collective-permute-start.3 = (bf16[128,256]{1,0:T(8,128)(2,1)S(1)}, bf16[128,256]{1,0:T(8,128)(2,1)S(1)}, u32[]{:S(2)}, u32[]{:S(2)}) collective-permute-start(bf16[128,256]{1,0:T(8,128)(2,1)S(1)} %get-tuple-element.24), channel_id=1, source_target_pairs={{0,4},{2,6},{4,0},{6,2},{1,5},{3,7},{5,1},{7,3},{8,12},{10,14},{12... | collective-permute-start | bytes 196616 | tf_op jit(solution)/shard_map/ppermute | solution.py:31
  14.8 1.5 %collective-permute-start.6 = (bf16[128,256]{1,0:T(8,128)(2,1)S(1)}, bf16[128,256]{1,0:T(8,128)(2,1)S(1)}, u32[]{:S(2)}, u32[]{:S(2)}) collective-permute-start(bf16[128,256]{1,0:T(8,128)(2,1)S(1)} %get-tuple-element.26), channel_id=1, source_target_pairs={{0,2},{2,0},{4,6},{6,4},{1,3},{3,1},{5,7},{7,5},{8,10},{10,8},{12,... | collective-permute-start | bytes 196616 | tf_op jit(solution)/shard_map/ppermute | solution.py:31
  16.3 1.8 %collective-permute-done.1.x_ref = bf16[128,1024]{1,0:T(8,128)(2,1)S(1)} collective-permute-done((bf16[128,1024]{1,0:T(8,128)(2,1)S(1)}, bf16[128,1024]{1,0:T(8,128)(2,1)S(1)}, u32[]{:S(2)}, u32[]{:S(2)}) %collective-permute-start.1) | collective-permute-done | bytes 262176 | tf_op jit(solution)/shard_map/ppermute | solution.py:31
  18.1 0.2 shard_map.78
  18.3 1.7 %collective-permute-start.9 = (bf16[128,256]{1,0:T(8,128)(2,1)S(1)}, bf16[128,256]{1,0:T(8,128)(2,1)S(1)}, u32[]{:S(2)}, u32[]{:S(2)}) collective-permute-start(bf16[128,256]{1,0:T(8,128)(2,1)S(1)} %shard_map.78), channel_id=1, source_target_pairs={{0,3},{1,2},{2,1},{3,0},{4,7},{5,6},{6,5},{7,4},{8,11},{9,10},{10,... | collective-permute-start | bytes 196616 | tf_op jit(solution)/shard_map/ppermute | solution.py:40
  20.0 0.2 shard_map.79
  20.4 1.6 %collective-permute-start.8 = (bf16[128,256]{1,0:T(8,128)(2,1)S(1)}, bf16[128,256]{1,0:T(8,128)(2,1)S(1)}, u32[]{:S(2)}, u32[]{:S(2)}) collective-permute-start(bf16[128,256]{1,0:T(8,128)(2,1)S(1)} %get-tuple-element.27), channel_id=1, source_target_pairs={{0,7},{1,6},{2,5},{3,4},{4,3},{5,2},{6,1},{7,0},{8,15},{9,14},{10,... | collective-permute-start | bytes 196616 | tf_op jit(solution)/shard_map/ppermute | solution.py:40
  22.0 0.3 shard_map.76
  22.3 0.3 shard_map.77
  22.7 0.5 %collective-permute-start.7 = (bf16[128,512]{1,0:T(8,128)(2,1)S(1)}, bf16[128,512]{1,0:T(8,128)(2,1)S(1)}, u32[]{:S(2)}, u32[]{:S(2)}) collective-permute-start(bf16[128,512]{1,0:T(8,128)(2,1)S(1)} %shard_map.77), channel_id=1, source_target_pairs={{0,5},{1,4},{2,7},{3,6},{4,1},{5,0},{6,3},{7,2},{8,13},{9,12},{10,... | collective-permute-start | bytes 393224 | tf_op jit(solution)/shard_map/ppermute | solution.py:40
  23.2 1.3 %collective-permute-start.4 = (bf16[128,512]{1,0:T(8,128)(2,1)S(1)}, bf16[128,512]{1,0:T(8,128)(2,1)S(1)}, u32[]{:S(2)}, u32[]{:S(2)}) collective-permute-start(bf16[128,512]{1,0:T(8,128)(2,1)S(1)} %shard_map.76), channel_id=1, source_target_pairs={{0,3},{1,2},{2,1},{3,0},{4,7},{5,6},{6,5},{7,4},{8,11},{9,10},{10,... | collective-permute-start | bytes 393224 | tf_op jit(solution)/shard_map/ppermute | solution.py:40
  24.5 0.3 shard_map.80
  24.8 1.1 %collective-permute-done.10.refs_2_ = bf16[128,256]{1,0:T(8,128)(2,1)S(1)} collective-permute-done((bf16[128,256]{1,0:T(8,128)(2,1)S(1)}, bf16[128,256]{1,0:T(8,128)(2,1)S(1)}, u32[]{:S(2)}, u32[]{:S(2)}) %collective-permute-start.10) | collective-permute-done | bytes 65568 | tf_op jit(solution)/shard_map/ppermute | solution.py:40
  26.0 1.6 %collective-permute-start.14 = (bf16[128,256]{1,0:T(8,128)(2,1)S(1)}, bf16[128,256]{1,0:T(8,128)(2,1)S(1)}, u32[]{:S(2)}, u32[]{:S(2)}) collective-permute-start(bf16[128,256]{1,0:T(8,128)(2,1)S(1)} %shard_map.81.refs_2_), channel_id=1, source_target_pairs={{0,8},{8,0},{16,24},{24,16},{1,9},{9,1},{17,25},{25,17},{2,10},{10... | collective-permute-start | bytes 196616 | tf_op jit(solution)/shard_map/ppermute | solution.py:44
  27.7 2.6 %collective-permute-start.13 = (bf16[128,256]{1,0:T(8,128)(2,1)S(1)}, bf16[128,256]{1,0:T(8,128)(2,1)S(1)}, u32[]{:S(2)}, u32[]{:S(2)}) collective-permute-start(bf16[128,256]{1,0:T(8,128)(2,1)S(1)} %shard_map.81.refs_2_), channel_id=1, source_target_pairs={{0,16},{8,24},{16,0},{24,8},{1,17},{9,25},{17,1},{25,9},{2,18},{10... | collective-permute-start | bytes 196616 | tf_op jit(solution)/shard_map/ppermute | solution.py:44
  30.6 4.1 %collective-permute-done.13.refs_4_ = bf16[128,256]{1,0:T(8,128)(2,1)S(1)} collective-permute-done((bf16[128,256]{1,0:T(8,128)(2,1)S(1)}, bf16[128,256]{1,0:T(8,128)(2,1)S(1)}, u32[]{:S(2)}, u32[]{:S(2)}) %collective-permute-start.13) | collective-permute-done | bytes 65568 | tf_op jit(solution)/shard_map/ppermute | solution.py:44
  34.7 1.7 %collective-permute-done.12.refs_3_ = bf16[128,256]{1,0:T(8,128)(2,1)S(1)} collective-permute-done((bf16[128,256]{1,0:T(8,128)(2,1)S(1)}, bf16[128,256]{1,0:T(8,128)(2,1)S(1)}, u32[]{:S(2)}, u32[]{:S(2)}) %collective-permute-start.12) | collective-permute-done | bytes 65568 | tf_op jit(solution)/shard_map/ppermute | solution.py:44
  36.3 1.5 %shard_map.82 = bf16[128,512]{1,0:T(8,128)(2,1)} custom-call(s32[1]{0:T(128)} %bitcast.at_ref, bf16[128,768]{1,0:T(8,128)(2,1)S(1)} %collective-permute-done.own_ref, bf16[128,512]{1,0:T(8,128)(2,1)S(1)} %collective-permute-done.4.refs_0_, bf16[128,512]{1,0:T(8,128)(2,1)S(1)} %collective-permute-done.7.refs_1_, bf16[128,256]{1,0:T(8,128)(2,1)S(1)} %shard_map.81.refs_2_, ...), custom_call_target="tpu_custom_call" | custom-call | tf_op jit(solution)/shard_map/pallas_call | solution.py:56
  (16 shorter events, 0.8 us)
Async XLA Ops:
  1.1 11.2 %collective-permute-start.2 = (bf16[128,1024]{1,0:T(8,128)(2,1)S(1)}, bf16[128,1024]{1,0:T(8,128)(2,1)S(1)}, u32[]{:S(2)}, u32[]{:S(2)}) collective-permute-start(bf16[128,1024]{1,0:T(8,128)(2,1)S(1)} %get-tuple-element.23), channel_id=1, source_target_pairs={{0,6},{2,4},{4,2},{6,0},{1,7},{3,5},{5,3},{7,1},{8,14},{10,12},{12... | collective-permute-start | bytes 786440 | tf_op jit(solution)/shard_map/ppermute | solution.py:31
  5.1 12.9 %collective-permute-start.1 = (bf16[128,1024]{1,0:T(8,128)(2,1)S(1)}, bf16[128,1024]{1,0:T(8,128)(2,1)S(1)}, u32[]{:S(2)}, u32[]{:S(2)}) collective-permute-start(bf16[128,1024]{1,0:T(8,128)(2,1)S(1)} %get-tuple-element.21), channel_id=1, source_target_pairs={{0,2},{2,0},{4,6},{6,4},{1,3},{3,1},{5,7},{7,5},{8,10},{10,8},{12,... | collective-permute-start | bytes 786440 | tf_op jit(solution)/shard_map/ppermute | solution.py:31
  5.7 12.6 %collective-permute-start.5 = (bf16[128,1024]{1,0:T(8,128)(2,1)S(1)}, bf16[128,1024]{1,0:T(8,128)(2,1)S(1)}, u32[]{:S(2)}, u32[]{:S(2)}) collective-permute-start(bf16[128,1024]{1,0:T(8,128)(2,1)S(1)} %get-tuple-element.25), channel_id=1, source_target_pairs={{0,4},{2,6},{4,0},{6,2},{1,5},{3,7},{5,1},{7,3},{8,12},{10,14},{12... | collective-permute-start | bytes 786440 | tf_op jit(solution)/shard_map/ppermute | solution.py:31
  8.9 14.2 %collective-permute-start = (bf16[128,768]{1,0:T(8,128)(2,1)S(1)}, bf16[128,768]{1,0:T(8,128)(2,1)S(1)}, u32[]{:S(2)}, u32[]{:S(2)}) collective-permute-start(bf16[128,768]{1,0:T(8,128)(2,1)S(1)} %get-tuple-element.20), channel_id=1, source_target_pairs={{0,1},{1,0},{2,3},{3,2},{4,5},{5,4},{6,7},{7,6},{8,9},{9,8},{10,11... | collective-permute-start | bytes 589832 | tf_op jit(solution)/shard_map/ppermute | solution.py:40
  12.7 7.5 %collective-permute-start.3 = (bf16[128,256]{1,0:T(8,128)(2,1)S(1)}, bf16[128,256]{1,0:T(8,128)(2,1)S(1)}, u32[]{:S(2)}, u32[]{:S(2)}) collective-permute-start(bf16[128,256]{1,0:T(8,128)(2,1)S(1)} %get-tuple-element.24), channel_id=1, source_target_pairs={{0,4},{2,6},{4,0},{6,2},{1,5},{3,7},{5,1},{7,3},{8,12},{10,14},{12... | collective-permute-start | bytes 196616 | tf_op jit(solution)/shard_map/ppermute | solution.py:31
  14.8 5.6 %collective-permute-start.6 = (bf16[128,256]{1,0:T(8,128)(2,1)S(1)}, bf16[128,256]{1,0:T(8,128)(2,1)S(1)}, u32[]{:S(2)}, u32[]{:S(2)}) collective-permute-start(bf16[128,256]{1,0:T(8,128)(2,1)S(1)} %get-tuple-element.26), channel_id=1, source_target_pairs={{0,2},{2,0},{4,6},{6,4},{1,3},{3,1},{5,7},{7,5},{8,10},{10,8},{12,... | collective-permute-start | bytes 196616 | tf_op jit(solution)/shard_map/ppermute | solution.py:31
  18.0 4.6 %collective-permute-start.11 = (f32[1,1152]{1,0:T(1,128)S(1)}, f32[1,1152]{1,0:T(1,128)S(1)}, u32[]{:S(2)}, u32[]{:S(2)}) collective-permute-start(f32[1,1152]{1,0:T(1,128)S(1)} %get-tuple-element.28), channel_id=1, source_target_pairs={{0,1},{1,0},{2,3},{3,2},{4,5},{5,4},{6,7},{7,6},{8,9},{9,8},{10,11... | collective-permute-start | bytes 13832 | tf_op jit(solution)/shard_map/ppermute | solution.py:432
  18.3 6.5 %collective-permute-start.9 = (bf16[128,256]{1,0:T(8,128)(2,1)S(1)}, bf16[128,256]{1,0:T(8,128)(2,1)S(1)}, u32[]{:S(2)}, u32[]{:S(2)}) collective-permute-start(bf16[128,256]{1,0:T(8,128)(2,1)S(1)} %shard_map.78), channel_id=1, source_target_pairs={{0,3},{1,2},{2,1},{3,0},{4,7},{5,6},{6,5},{7,4},{8,11},{9,10},{10,... | collective-permute-start | bytes 196616 | tf_op jit(solution)/shard_map/ppermute | solution.py:40
  20.2 5.7 %collective-permute-start.10 = (bf16[128,256]{1,0:T(8,128)(2,1)S(1)}, bf16[128,256]{1,0:T(8,128)(2,1)S(1)}, u32[]{:S(2)}, u32[]{:S(2)}) collective-permute-start(bf16[128,256]{1,0:T(8,128)(2,1)S(1)} %shard_map.79), channel_id=1, source_target_pairs={{0,5},{1,4},{2,7},{3,6},{4,1},{5,0},{6,3},{7,2},{8,13},{9,12},{10,... | collective-permute-start | bytes 196616 | tf_op jit(solution)/shard_map/ppermute | solution.py:40
  20.4 5.5 %collective-permute-start.8 = (bf16[128,256]{1,0:T(8,128)(2,1)S(1)}, bf16[128,256]{1,0:T(8,128)(2,1)S(1)}, u32[]{:S(2)}, u32[]{:S(2)}) collective-permute-start(bf16[128,256]{1,0:T(8,128)(2,1)S(1)} %get-tuple-element.27), channel_id=1, source_target_pairs={{0,7},{1,6},{2,5},{3,4},{4,3},{5,2},{6,1},{7,0},{8,15},{9,14},{10,... | collective-permute-start | bytes 196616 | tf_op jit(solution)/shard_map/ppermute | solution.py:40
  22.7 13.7 %collective-permute-start.7 = (bf16[128,512]{1,0:T(8,128)(2,1)S(1)}, bf16[128,512]{1,0:T(8,128)(2,1)S(1)}, u32[]{:S(2)}, u32[]{:S(2)}) collective-permute-start(bf16[128,512]{1,0:T(8,128)(2,1)S(1)} %shard_map.77), channel_id=1, source_target_pairs={{0,5},{1,4},{2,7},{3,6},{4,1},{5,0},{6,3},{7,2},{8,13},{9,12},{10,... | collective-permute-start | bytes 393224 | tf_op jit(solution)/shard_map/ppermute | solution.py:40
  23.2 13.2 %collective-permute-start.4 = (bf16[128,512]{1,0:T(8,128)(2,1)S(1)}, bf16[128,512]{1,0:T(8,128)(2,1)S(1)}, u32[]{:S(2)}, u32[]{:S(2)}) collective-permute-start(bf16[128,512]{1,0:T(8,128)(2,1)S(1)} %shard_map.76), channel_id=1, source_target_pairs={{0,3},{1,2},{2,1},{3,0},{4,7},{5,6},{6,5},{7,4},{8,11},{9,10},{10,... | collective-permute-start | bytes 393224 | tf_op jit(solution)/shard_map/ppermute | solution.py:40
  26.0 4.5 %collective-permute-start.14 = (bf16[128,256]{1,0:T(8,128)(2,1)S(1)}, bf16[128,256]{1,0:T(8,128)(2,1)S(1)}, u32[]{:S(2)}, u32[]{:S(2)}) collective-permute-start(bf16[128,256]{1,0:T(8,128)(2,1)S(1)} %shard_map.81.refs_2_), channel_id=1, source_target_pairs={{0,8},{8,0},{16,24},{24,16},{1,9},{9,1},{17,25},{25,17},{2,10},{10... | collective-permute-start | bytes 196616 | tf_op jit(solution)/shard_map/ppermute | solution.py:44
  27.7 7.0 %collective-permute-start.13 = (bf16[128,256]{1,0:T(8,128)(2,1)S(1)}, bf16[128,256]{1,0:T(8,128)(2,1)S(1)}, u32[]{:S(2)}, u32[]{:S(2)}) collective-permute-start(bf16[128,256]{1,0:T(8,128)(2,1)S(1)} %shard_map.81.refs_2_), channel_id=1, source_target_pairs={{0,16},{8,24},{16,0},{24,8},{1,17},{9,25},{17,1},{25,9},{2,18},{10... | collective-permute-start | bytes 196616 | tf_op jit(solution)/shard_map/ppermute | solution.py:44
  30.3 6.1 %collective-permute-start.12 = (bf16[128,256]{1,0:T(8,128)(2,1)S(1)}, bf16[128,256]{1,0:T(8,128)(2,1)S(1)}, u32[]{:S(2)}, u32[]{:S(2)}) collective-permute-start(bf16[128,256]{1,0:T(8,128)(2,1)S(1)} %shard_map.81.refs_2_), channel_id=1, source_target_pairs={{0,24},{8,16},{16,8},{24,0},{1,25},{9,17},{17,9},{25,1},{2,26},{10... | collective-permute-start | bytes 196616 | tf_op jit(solution)/shard_map/ppermute | solution.py:44

commit v5 on v4

--- a/solution.py
+++ b/solution.py
@@ -66,12 +66,13 @@
     return [pltpu.with_memory_space_constraint(x, pltpu.HBM) for x in arrays]
 
 
-def cut_kernel(count, sequence, here_ref, rows_ref, *refs):
+def cut_kernel(count, sequence, rows_ref, *refs):
     out_refs, sem = refs[:-1], refs[-1]
+    here = lax.axis_index("dp")
     width = out_refs[0].shape[1]
     copies = []
     for i, k in enumerate(sequence):
-        begin = pl.multiple_of(partner(here_ref[0], k, count) * width, width)
+        begin = pl.multiple_of(partner(here, k, count) * width, width)
         copies.append(
             pltpu.make_async_copy(rows_ref.at[:, pl.ds(begin, width)], out_refs[i], sem.at[i])
         )
@@ -81,13 +82,13 @@
         copy.wait()
 
 
-def cut(rows, here, count, sequence):
+def cut(rows, count, sequence):
     height, features = rows.shape
     return local_call(
         functools.partial(cut_kernel, count, sequence),
         [on_chip((height, features // count), jnp.bfloat16)] * len(sequence),
-        (here, *in_hbm(rows)),
-        (pltpu.SMEM, pltpu.HBM),
+        in_hbm(rows),
+        [pltpu.HBM],
         scratch_shapes=[pltpu.SemaphoreType.DMA((len(sequence),))],
     )
 
@@ -126,7 +127,7 @@
 
 
 def prepare_kernel(
-    here_ref, rows_hbm, gain_ref, kw_hbm, vw_hbm, qw_hbm, order_ref, docs_ref, *refs
+    rows_hbm, gain_ref, kw_hbm, vw_hbm, qw_hbm, order_ref, docs_ref, *refs
 ):
     w_out, part_out = refs[:2]
     rows_ref, w_ref, sem = refs[-3:]
@@ -143,7 +144,7 @@
     if len(refs) == 6:
         tell(rows_ref, order_ref, docs_ref, refs[2])
     width = w_out.shape[0]
-    begin = pl.multiple_of(here_ref[0] * width, width)
+    begin = pl.multiple_of(lax.axis_index("dp") * width, width)
     for copy in copies[1:]:
         copy.wait()
     step = 128
@@ -154,7 +155,7 @@
     part_out[...] = product(rows_ref[:, pl.ds(begin, width)], w_out[...])
 
 
-def prepare(here, rows, gain, weights, order, docs, with_meta):
+def prepare(rows, gain, weights, order, docs, with_meta):
     height, depth = rows.shape[0], weights[0].shape[0]
     width = sum(w.shape[1] for w in weights)
     outs = [on_chip((depth, width), jnp.bfloat16), on_chip((height, width), jnp.bfloat16)]
@@ -163,8 +164,8 @@
     return local_call(
         prepare_kernel,
         outs,
-        (here, *in_hbm(rows, gain, *weights, order, docs)),
-        (pltpu.SMEM, pltpu.HBM, pltpu.VMEM, *[pltpu.HBM] * 3, pltpu.SMEM, pltpu.VMEM),
+        in_hbm(rows, gain, *weights, order, docs),
+        (pltpu.HBM, pltpu.VMEM, *[pltpu.HBM] * 3, pltpu.SMEM, pltpu.VMEM),
         scratch_shapes=[
             pltpu.VMEM(rows.shape, jnp.bfloat16),
             pltpu.VMEM((depth, width), jnp.bfloat16),
@@ -193,9 +194,9 @@
     return jnp.sum(jnp.where(down == across, row, 0.0), axis=1, keepdims=True)
 
 
-def tables_kernel(length, at_ref, meta_ref, kcos, ksin, qcos, qsin, level, bias):
+def tables_kernel(length, meta_ref, kcos, ksin, qcos, qsin, level, bias):
     rows, size = kcos.shape
-    begin = pl.multiple_of(at_ref[0] * rows, rows)
+    begin = pl.multiple_of(lax.axis_index("ctx") * rows, rows)
     qpos = column(meta_ref[:, pl.ds(begin, rows)])
     qdoc = column(meta_ref[:, pl.ds(length + begin, rows)])
     scale = column(meta_ref[:, 2 * length :])
@@ -212,20 +213,14 @@
     bias[...] = jnp.where(allowed, 0.0, MASKED)
 
 
-def tables(at, meta, rows, size, length):
+def tables(meta, rows, size, length):
     square = on_chip((rows, size), jnp.float32)
     return local_call(
         functools.partial(tables_kernel, length),
         [square] * 5 + [on_chip((rows, length), jnp.float32)],
-        (at, meta),
-        (pltpu.SMEM, pltpu.VMEM),
-    )
-
-
-def dot_kernel(x_ref, w_ref, out_ref):
-    out_ref[...] = jnp.dot(
-        x_ref[...], w_ref[...], preferred_element_type=jnp.float32
-    ).astype(jnp.bfloat16)
+        (meta,),
+        (pltpu.VMEM,),
+    )
 
 
 def project(x, weight):
@@ -302,7 +297,8 @@
     )
 
 
-def attend_kernel(count, steps, ring, at_ref, own_ref, *refs):
+def attend_kernel(count, steps, ring, own_ref, *refs):
+    at = lax.axis_index("ctx")
     parts, kv_refs = refs[:count], refs[count : count + ring]
     qcos, qsin, bias, out_ref, held, sem = refs[count + ring :]
     rows, size = qcos.shape
@@ -310,26 +306,31 @@
     keys = jnp.concatenate([ref[:, :size] for ref in kv_refs], axis=0)
     values = jnp.concatenate([ref[:, size:] for ref in kv_refs], axis=0)
     values = jnp.concatenate([values, jnp.ones_like(values)], axis=1)
-    here = [pl.multiple_of(partner(at_ref[0], j, ring) * rows, rows) for j in steps]
+    here = [pl.multiple_of(partner(at, j, ring) * rows, rows) for j in steps]
     masks = jnp.concatenate([bias[:, pl.ds(b, rows)] for b in here], axis=1)
     copies = []
-    for h in range(heads):
-        place = own_place(h, heads, size)
-        query = own_ref[:, place : place + size].astype(jnp.float32)
-        query = turn(query + summed(parts, h * size, size), qcos[...], qsin[...])
-        scores = lax.dot_general(
-            query.astype(jnp.bfloat16),
-            keys,
-            (((1,), (1,)), ((), ())),
-            preferred_element_type=jnp.float32,
-        )
-        scores = scores + masks
-        probs = jnp.exp2(scores - jnp.max(scores, axis=-1, keepdims=True))
-        mixed = jnp.dot(probs.astype(jnp.bfloat16), values, preferred_element_type=jnp.float32)
-        held[h] = (mixed[:, :size] / mixed[:, size:]).astype(jnp.bfloat16)
-        place = out_ref.at[:, h * size : (h + 1) * size]
-        copies.append(pltpu.make_async_copy(held.at[h], place, sem.at[h]))
-        copies[-1].start()
+    for first in range(0, heads, 4):
+        together = range(first, first + 4)
+        scores, probs = {}, {}
+        for h in together:
+            place = own_place(h, heads, size)
+            query = own_ref[:, place : place + size].astype(jnp.float32)
+            query = turn(query + summed(parts, h * size, size), qcos[...], qsin[...])
+            scores[h] = masks + lax.dot_general(
+                query.astype(jnp.bfloat16),
+                keys,
+                (((1,), (1,)), ((), ())),
+                preferred_element_type=jnp.float32,
+            )
+        for h in together:
+            top = jnp.max(scores[h], axis=-1, keepdims=True)
+            probs[h] = jnp.exp2(scores[h] - top).astype(jnp.bfloat16)
+        for h in together:
+            mixed = jnp.dot(probs[h], values, preferred_element_type=jnp.float32)
+            held[h] = (mixed[:, :size] / mixed[:, size:]).astype(jnp.bfloat16)
+            place = out_ref.at[:, h * size : (h + 1) * size]
+            copies.append(pltpu.make_async_copy(held.at[h], place, sem.at[h]))
+            copies[-1].start()
     for copy in copies:
         copy.wait()
 
@@ -338,8 +339,8 @@
     return (head + (1 if head < heads // 2 else 2)) * size
 
 
-def attend(at, own, parts, kv, qcos, qsin, bias):
-    args = (at, own, *parts, *kv, qcos, qsin, bias)
+def attend(own, parts, kv, qcos, qsin, bias):
+    args = (own, *parts, *kv, qcos, qsin, bias)
     rows, width = parts[0].shape
     heads = width // qcos.shape[1]
     steps = [0, *far_first(len(kv))]
@@ -347,7 +348,7 @@
         functools.partial(attend_kernel, len(parts), steps, len(kv)),
         jax.ShapeDtypeStruct(parts[0].shape, jnp.bfloat16),
         args,
-        [pltpu.SMEM] + [pltpu.VMEM] * (len(args) - 1),
+        [pltpu.VMEM] * len(args),
         out_specs=pl.BlockSpec(memory_space=pltpu.HBM),
         scratch_shapes=[
             pltpu.VMEM((heads, rows, width // heads), jnp.bfloat16),
@@ -413,24 +414,22 @@
     row_count = rows_here.shape[0]
     length = doc_ids.shape[2]
     size = key_weight.shape[2]
-    here = lax.axis_index("dp").astype(jnp.int32)[None]
-    at = lax.axis_index("ctx").astype(jnp.int32)[None]
     if count != 4:
         raise ValueError("axis size")
-    away = [3, 1, 2]
+    away = [3, 2, 1]
     weights = [key_weight[0], value_weight[0], query_weight[0]]
-    slabs = cut(rows_here, here, count, away)
+    slabs = cut(rows_here, count, away)
     arrived = {}
     for k, slab in zip(away, slabs):
         arrived[k] = swap_dp(slab, k, count)
 
     weight, part, *meta = prepare(
-        here, rows_here, norm_gain, weights, block_order[0], doc_ids[0], ring <= DIRECT
+        rows_here, norm_gain, weights, block_order[0], doc_ids[0], ring <= DIRECT
     )
     own = to_next_section(part, 0, count, sections)
     meta = meta[0] if meta else describe_long(rows_here, block_order[0], doc_ids[0])
     meta = lax.ppermute(meta, "section", [(i, (i + 1) % sections) for i in range(sections)])
-    kcos, ksin, qcos, qsin, level, bias = tables(at, meta, row_count, size, length)
+    kcos, ksin, qcos, qsin, level, bias = tables(meta, row_count, size, length)
 
     part, *halves = far_product(arrived[3], weight, size)
     kv_parts = [to_next_section(part, 3, count, sections)]
@@ -452,7 +451,7 @@
         pieces = [kv]
         for j in far_first(ring):
             pieces.append(swap_ctx(kv, j, ring))
-        out = attend(at, own, q_parts, pieces, qcos, qsin, bias)
+        out = attend(own, q_parts, pieces, qcos, qsin, bias)
     else:
         everything = lax.all_gather(kv, "ctx", axis=0, tiled=True)
         out = attend_long(own, q_parts, everything, qcos, qsin, bias)

time: 38 us -> 37.8 us (level)
  transfers between devices with their start and end apart: 15 -> 15, of which waited for: 6 -> 6; matrix products, arithmetic and copies ran while one was open for 0% -> 0% of each run, Pallas kernels for 13% -> 14%
where the time goes in v5:
time: 37.8 us; the launch traced here: 37.6 us
  starting transfers between devices  17.9 us (47%)
  waiting for transfers between devices  12 us (32%)
  Pallas kernels  7.51 us (20%)
    ppermute x5, starting transfers between devices, swap_dp(): lax.ppermute(x, 'dp', [(i, partner(i, step, count)) for i in range(count)])  8.18 us
    pallas_call x10, Pallas kernels, local_call(): pl.pallas_call(kernel, out_shape=out_shape, in_specs=in_specs, compiler_p...  7.51 us
    ppermute x3, waiting for transfers between devices, swap_ctx(): lax.ppermute(x, 'ctx', [(i, partner(i, step, ring)) for i in range(ring)])  5.84 us
    ppermute x6, starting transfers between devices, to_next_section(): return lax.ppermute(x, ('dp', 'section'), moves)  5.3 us
    ppermute x5, waiting for transfers between devices, swap_dp(): lax.ppermute(x, 'dp', [(i, partner(i, step, count)) for i in range(count)])  5.1 us
    ppermute x3, starting transfers between devices, swap_ctx(): lax.ppermute(x, 'ctx', [(i, partner(i, step, ring)) for i in range(ring)])  4.45 us
    ppermute x6, waiting for transfers between devices, to_next_section(): return lax.ppermute(x, ('dp', 'section'), moves)  1.1 us
  transfers between devices with their start and end apart: 15, of which 6 were waited for; matrix products, arithmetic and copies ran while one was open for 0% of the time, Pallas kernels for 14%

profile of v5, /device:TPU:0, one launch (start us, length us, event | category | flops | bytes accessed | tf_op | source)
XLA Modules:
  0.0 37.6 jit_solution(2413742349578306515)
XLA Ops:
  0.0 1.1 %shard_map.74 = (bf16[128,1024]{1,0:T(8,128)(2,1)S(1)}, bf16[128,1024]{1,0:T(8,128)(2,1)S(1)}, bf16[128,1024]{1,0:T(8,128)(2,1)S(1)}) custom-call(bf16[128,4096]{1,0:T(8,128)(2,1)} %bitcast.7), custom_call_target="tpu_custom_call" | custom-call | tf_op jit(solution)/shard_map/pallas_call | solution.py:56
  1.1 4.0 %collective-permute-start.2 = (bf16[128,1024]{1,0:T(8,128)(2,1)S(1)}, bf16[128,1024]{1,0:T(8,128)(2,1)S(1)}, u32[]{:S(2)}, u32[]{:S(2)}) collective-permute-start(bf16[128,1024]{1,0:T(8,128)(2,1)S(1)} %get-tuple-element.23), channel_id=1, source_target_pairs={{0,6},{2,4},{4,2},{6,0},{1,7},{3,5},{5,3},{7,1},{8,14},{10,12},{12... | collective-permute-start | bytes 786440 | tf_op jit(solution)/shard_map/ppermute | solution.py:31
  5.1 0.5 %collective-permute-start.1 = (bf16[128,1024]{1,0:T(8,128)(2,1)S(1)}, bf16[128,1024]{1,0:T(8,128)(2,1)S(1)}, u32[]{:S(2)}, u32[]{:S(2)}) collective-permute-start(bf16[128,1024]{1,0:T(8,128)(2,1)S(1)} %get-tuple-element.21), channel_id=1, source_target_pairs={{0,2},{2,0},{4,6},{6,4},{1,3},{3,1},{5,7},{7,5},{8,10},{10,8},{12,... | collective-permute-start | bytes 786440 | tf_op jit(solution)/shard_map/ppermute | solution.py:31
  5.8 3.2 %shard_map.73 = (bf16[1024,768]{1,0:T(8,128)(2,1)S(1)}, bf16[128,768]{1,0:T(8,128)(2,1)S(1)}, f32[1,1152]{1,0:T(1,128)S(1)}) custom-call(bf16[128,4096]{1,0:T(8,128)(2,1)} %bitcast.8, f32[1,4096]{1,0:T(1,128)} %gain_ref.1, bf16[1024,128]{1,0:T(8,128)(2,1)} %bitcast.10, bf16[1024,128]{1,0:T(8,128)(2,1)} %bitcast.11, bf16[1024,512]{1,0:T(8,128)(2,1)} %bitcast.9, ...), custom_call_target="tpu_custom_call" | custom-call | tf_op jit(solution)/shard_map/pallas_call | solution.py:56
  9.0 3.3 %collective-permute-done.2.x_ref = bf16[128,1024]{1,0:T(8,128)(2,1)S(1)} collective-permute-done((bf16[128,1024]{1,0:T(8,128)(2,1)S(1)}, bf16[128,1024]{1,0:T(8,128)(2,1)S(1)}, u32[]{:S(2)}, u32[]{:S(2)}) %collective-permute-start.2) | collective-permute-done | bytes 262176 | tf_op jit(solution)/shard_map/ppermute | solution.py:31
  12.3 0.4 shard_map.75
  12.7 2.1 %collective-permute-start.3 = (bf16[128,256]{1,0:T(8,128)(2,1)S(1)}, bf16[128,256]{1,0:T(8,128)(2,1)S(1)}, u32[]{:S(2)}, u32[]{:S(2)}) collective-permute-start(bf16[128,256]{1,0:T(8,128)(2,1)S(1)} %get-tuple-element.24), channel_id=1, source_target_pairs={{0,4},{2,6},{4,0},{6,2},{1,5},{3,7},{5,1},{7,3},{8,12},{10,14},{12... | collective-permute-start | bytes 196616 | tf_op jit(solution)/shard_map/ppermute | solution.py:31
  14.8 1.5 %collective-permute-start.6 = (bf16[128,256]{1,0:T(8,128)(2,1)S(1)}, bf16[128,256]{1,0:T(8,128)(2,1)S(1)}, u32[]{:S(2)}, u32[]{:S(2)}) collective-permute-start(bf16[128,256]{1,0:T(8,128)(2,1)S(1)} %get-tuple-element.26), channel_id=1, source_target_pairs={{0,2},{2,0},{4,6},{6,4},{1,3},{3,1},{5,7},{7,5},{8,10},{10,8},{12,... | collective-permute-start | bytes 196616 | tf_op jit(solution)/shard_map/ppermute | solution.py:31
  16.3 1.8 %collective-permute-done.1.x_ref = bf16[128,1024]{1,0:T(8,128)(2,1)S(1)} collective-permute-done((bf16[128,1024]{1,0:T(8,128)(2,1)S(1)}, bf16[128,1024]{1,0:T(8,128)(2,1)S(1)}, u32[]{:S(2)}, u32[]{:S(2)}) %collective-permute-start.1) | collective-permute-done | bytes 262176 | tf_op jit(solution)/shard_map/ppermute | solution.py:31
  18.1 0.2 shard_map.78
  18.3 1.7 %collective-permute-start.9 = (bf16[128,256]{1,0:T(8,128)(2,1)S(1)}, bf16[128,256]{1,0:T(8,128)(2,1)S(1)}, u32[]{:S(2)}, u32[]{:S(2)}) collective-permute-start(bf16[128,256]{1,0:T(8,128)(2,1)S(1)} %shard_map.78), channel_id=1, source_target_pairs={{0,3},{1,2},{2,1},{3,0},{4,7},{5,6},{6,5},{7,4},{8,11},{9,10},{10,... | collective-permute-start | bytes 196616 | tf_op jit(solution)/shard_map/ppermute | solution.py:40
  20.0 0.2 shard_map.79
  20.4 1.6 %collective-permute-start.8 = (bf16[128,256]{1,0:T(8,128)(2,1)S(1)}, bf16[128,256]{1,0:T(8,128)(2,1)S(1)}, u32[]{:S(2)}, u32[]{:S(2)}) collective-permute-start(bf16[128,256]{1,0:T(8,128)(2,1)S(1)} %get-tuple-element.27), channel_id=1, source_target_pairs={{0,7},{1,6},{2,5},{3,4},{4,3},{5,2},{6,1},{7,0},{8,15},{9,14},{10,... | collective-permute-start | bytes 196616 | tf_op jit(solution)/shard_map/ppermute | solution.py:40
  22.0 0.3 shard_map.76
  22.3 0.3 shard_map.77
  22.6 0.5 %collective-permute-start.7 = (bf16[128,512]{1,0:T(8,128)(2,1)S(1)}, bf16[128,512]{1,0:T(8,128)(2,1)S(1)}, u32[]{:S(2)}, u32[]{:S(2)}) collective-permute-start(bf16[128,512]{1,0:T(8,128)(2,1)S(1)} %shard_map.77), channel_id=1, source_target_pairs={{0,5},{1,4},{2,7},{3,6},{4,1},{5,0},{6,3},{7,2},{8,13},{9,12},{10,... | collective-permute-start | bytes 393224 | tf_op jit(solution)/shard_map/ppermute | solution.py:40
  23.2 1.3 %collective-permute-start.4 = (bf16[128,512]{1,0:T(8,128)(2,1)S(1)}, bf16[128,512]{1,0:T(8,128)(2,1)S(1)}, u32[]{:S(2)}, u32[]{:S(2)}) collective-permute-start(bf16[128,512]{1,0:T(8,128)(2,1)S(1)} %shard_map.76), channel_id=1, source_target_pairs={{0,3},{1,2},{2,1},{3,0},{4,7},{5,6},{6,5},{7,4},{8,11},{9,10},{10,... | collective-permute-start | bytes 393224 | tf_op jit(solution)/shard_map/ppermute | solution.py:40
  24.4 0.4 shard_map.80
  24.8 1.1 %collective-permute-done.10.refs_2_ = bf16[128,256]{1,0:T(8,128)(2,1)S(1)} collective-permute-done((bf16[128,256]{1,0:T(8,128)(2,1)S(1)}, bf16[128,256]{1,0:T(8,128)(2,1)S(1)}, u32[]{:S(2)}, u32[]{:S(2)}) %collective-permute-start.10) | collective-permute-done | bytes 65568 | tf_op jit(solution)/shard_map/ppermute | solution.py:40
  26.0 1.6 %collective-permute-start.14 = (bf16[128,256]{1,0:T(8,128)(2,1)S(1)}, bf16[128,256]{1,0:T(8,128)(2,1)S(1)}, u32[]{:S(2)}, u32[]{:S(2)}) collective-permute-start(bf16[128,256]{1,0:T(8,128)(2,1)S(1)} %shard_map.81.refs_2_), channel_id=1, source_target_pairs={{0,8},{8,0},{16,24},{24,16},{1,9},{9,1},{17,25},{25,17},{2,10},{10... | collective-permute-start | bytes 196616 | tf_op jit(solution)/shard_map/ppermute | solution.py:44
  27.7 2.6 %collective-permute-start.13 = (bf16[128,256]{1,0:T(8,128)(2,1)S(1)}, bf16[128,256]{1,0:T(8,128)(2,1)S(1)}, u32[]{:S(2)}, u32[]{:S(2)}) collective-permute-start(bf16[128,256]{1,0:T(8,128)(2,1)S(1)} %shard_map.81.refs_2_), channel_id=1, source_target_pairs={{0,16},{8,24},{16,0},{24,8},{1,17},{9,25},{17,1},{25,9},{2,18},{10... | collective-permute-start | bytes 196616 | tf_op jit(solution)/shard_map/ppermute | solution.py:44
  30.6 4.1 %collective-permute-done.13.refs_4_ = bf16[128,256]{1,0:T(8,128)(2,1)S(1)} collective-permute-done((bf16[128,256]{1,0:T(8,128)(2,1)S(1)}, bf16[128,256]{1,0:T(8,128)(2,1)S(1)}, u32[]{:S(2)}, u32[]{:S(2)}) %collective-permute-start.13) | collective-permute-done | bytes 65568 | tf_op jit(solution)/shard_map/ppermute | solution.py:44
  34.7 1.7 %collective-permute-done.12.refs_3_ = bf16[128,256]{1,0:T(8,128)(2,1)S(1)} collective-permute-done((bf16[128,256]{1,0:T(8,128)(2,1)S(1)}, bf16[128,256]{1,0:T(8,128)(2,1)S(1)}, u32[]{:S(2)}, u32[]{:S(2)}) %collective-permute-start.12) | collective-permute-done | bytes 65568 | tf_op jit(solution)/shard_map/ppermute | solution.py:44
  36.3 1.3 %shard_map.82 = bf16[128,512]{1,0:T(8,128)(2,1)} custom-call(bf16[128,768]{1,0:T(8,128)(2,1)S(1)} %collective-permute-done.own_ref, bf16[128,512]{1,0:T(8,128)(2,1)S(1)} %collective-permute-done.4.refs_0_, bf16[128,512]{1,0:T(8,128)(2,1)S(1)} %collective-permute-done.7.refs_1_, bf16[128,256]{1,0:T(8,128)(2,1)S(1)} %shard_map.81.refs_2_, ...), custom_call_target="tpu_custom_call" | custom-call | tf_op jit(solution)/shard_map/pallas_call | solution.py:56
  (16 shorter events, 0.8 us)
Async XLA Ops:
  1.1 11.2 %collective-permute-start.2 = (bf16[128,1024]{1,0:T(8,128)(2,1)S(1)}, bf16[128,1024]{1,0:T(8,128)(2,1)S(1)}, u32[]{:S(2)}, u32[]{:S(2)}) collective-permute-start(bf16[128,1024]{1,0:T(8,128)(2,1)S(1)} %get-tuple-element.23), channel_id=1, source_target_pairs={{0,6},{2,4},{4,2},{6,0},{1,7},{3,5},{5,3},{7,1},{8,14},{10,12},{12... | collective-permute-start | bytes 786440 | tf_op jit(solution)/shard_map/ppermute | solution.py:31
  5.1 12.9 %collective-permute-start.1 = (bf16[128,1024]{1,0:T(8,128)(2,1)S(1)}, bf16[128,1024]{1,0:T(8,128)(2,1)S(1)}, u32[]{:S(2)}, u32[]{:S(2)}) collective-permute-start(bf16[128,1024]{1,0:T(8,128)(2,1)S(1)} %get-tuple-element.21), channel_id=1, source_target_pairs={{0,2},{2,0},{4,6},{6,4},{1,3},{3,1},{5,7},{7,5},{8,10},{10,8},{12,... | collective-permute-start | bytes 786440 | tf_op jit(solution)/shard_map/ppermute | solution.py:31
  5.7 12.6 %collective-permute-start.5 = (bf16[128,1024]{1,0:T(8,128)(2,1)S(1)}, bf16[128,1024]{1,0:T(8,128)(2,1)S(1)}, u32[]{:S(2)}, u32[]{:S(2)}) collective-permute-start(bf16[128,1024]{1,0:T(8,128)(2,1)S(1)} %get-tuple-element.25), channel_id=1, source_target_pairs={{0,4},{2,6},{4,0},{6,2},{1,5},{3,7},{5,1},{7,3},{8,12},{10,14},{12... | collective-permute-start | bytes 786440 | tf_op jit(solution)/shard_map/ppermute | solution.py:31
  8.9 14.2 %collective-permute-start = (bf16[128,768]{1,0:T(8,128)(2,1)S(1)}, bf16[128,768]{1,0:T(8,128)(2,1)S(1)}, u32[]{:S(2)}, u32[]{:S(2)}) collective-permute-start(bf16[128,768]{1,0:T(8,128)(2,1)S(1)} %get-tuple-element.20), channel_id=1, source_target_pairs={{0,1},{1,0},{2,3},{3,2},{4,5},{5,4},{6,7},{7,6},{8,9},{9,8},{10,11... | collective-permute-start | bytes 589832 | tf_op jit(solution)/shard_map/ppermute | solution.py:40
  12.7 7.5 %collective-permute-start.3 = (bf16[128,256]{1,0:T(8,128)(2,1)S(1)}, bf16[128,256]{1,0:T(8,128)(2,1)S(1)}, u32[]{:S(2)}, u32[]{:S(2)}) collective-permute-start(bf16[128,256]{1,0:T(8,128)(2,1)S(1)} %get-tuple-element.24), channel_id=1, source_target_pairs={{0,4},{2,6},{4,0},{6,2},{1,5},{3,7},{5,1},{7,3},{8,12},{10,14},{12... | collective-permute-start | bytes 196616 | tf_op jit(solution)/shard_map/ppermute | solution.py:31
  14.8 5.6 %collective-permute-start.6 = (bf16[128,256]{1,0:T(8,128)(2,1)S(1)}, bf16[128,256]{1,0:T(8,128)(2,1)S(1)}, u32[]{:S(2)}, u32[]{:S(2)}) collective-permute-start(bf16[128,256]{1,0:T(8,128)(2,1)S(1)} %get-tuple-element.26), channel_id=1, source_target_pairs={{0,2},{2,0},{4,6},{6,4},{1,3},{3,1},{5,7},{7,5},{8,10},{10,8},{12,... | collective-permute-start | bytes 196616 | tf_op jit(solution)/shard_map/ppermute | solution.py:31
  18.0 4.6 %collective-permute-start.11 = (f32[1,1152]{1,0:T(1,128)S(1)}, f32[1,1152]{1,0:T(1,128)S(1)}, u32[]{:S(2)}, u32[]{:S(2)}) collective-permute-start(f32[1,1152]{1,0:T(1,128)S(1)} %get-tuple-element.28), channel_id=1, source_target_pairs={{0,1},{1,0},{2,3},{3,2},{4,5},{5,4},{6,7},{7,6},{8,9},{9,8},{10,11... | collective-permute-start | bytes 13832 | tf_op jit(solution)/shard_map/ppermute | solution.py:431
  18.3 6.5 %collective-permute-start.9 = (bf16[128,256]{1,0:T(8,128)(2,1)S(1)}, bf16[128,256]{1,0:T(8,128)(2,1)S(1)}, u32[]{:S(2)}, u32[]{:S(2)}) collective-permute-start(bf16[128,256]{1,0:T(8,128)(2,1)S(1)} %shard_map.78), channel_id=1, source_target_pairs={{0,3},{1,2},{2,1},{3,0},{4,7},{5,6},{6,5},{7,4},{8,11},{9,10},{10,... | collective-permute-start | bytes 196616 | tf_op jit(solution)/shard_map/ppermute | solution.py:40
  20.2 5.7 %collective-permute-start.10 = (bf16[128,256]{1,0:T(8,128)(2,1)S(1)}, bf16[128,256]{1,0:T(8,128)(2,1)S(1)}, u32[]{:S(2)}, u32[]{:S(2)}) collective-permute-start(bf16[128,256]{1,0:T(8,128)(2,1)S(1)} %shard_map.79), channel_id=1, source_target_pairs={{0,5},{1,4},{2,7},{3,6},{4,1},{5,0},{6,3},{7,2},{8,13},{9,12},{10,... | collective-permute-start | bytes 196616 | tf_op jit(solution)/shard_map/ppermute | solution.py:40
  20.4 5.5 %collective-permute-start.8 = (bf16[128,256]{1,0:T(8,128)(2,1)S(1)}, bf16[128,256]{1,0:T(8,128)(2,1)S(1)}, u32[]{:S(2)}, u32[]{:S(2)}) collective-permute-start(bf16[128,256]{1,0:T(8,128)(2,1)S(1)} %get-tuple-element.27), channel_id=1, source_target_pairs={{0,7},{1,6},{2,5},{3,4},{4,3},{5,2},{6,1},{7,0},{8,15},{9,14},{10,... | collective-permute-start | bytes 196616 | tf_op jit(solution)/shard_map/ppermute | solution.py:40
  22.6 13.7 %collective-permute-start.7 = (bf16[128,512]{1,0:T(8,128)(2,1)S(1)}, bf16[128,512]{1,0:T(8,128)(2,1)S(1)}, u32[]{:S(2)}, u32[]{:S(2)}) collective-permute-start(bf16[128,512]{1,0:T(8,128)(2,1)S(1)} %shard_map.77), channel_id=1, source_target_pairs={{0,5},{1,4},{2,7},{3,6},{4,1},{5,0},{6,3},{7,2},{8,13},{9,12},{10,... | collective-permute-start | bytes 393224 | tf_op jit(solution)/shard_map/ppermute | solution.py:40
  23.2 13.2 %collective-permute-start.4 = (bf16[128,512]{1,0:T(8,128)(2,1)S(1)}, bf16[128,512]{1,0:T(8,128)(2,1)S(1)}, u32[]{:S(2)}, u32[]{:S(2)}) collective-permute-start(bf16[128,512]{1,0:T(8,128)(2,1)S(1)} %shard_map.76), channel_id=1, source_target_pairs={{0,3},{1,2},{2,1},{3,0},{4,7},{5,6},{6,5},{7,4},{8,11},{9,10},{10,... | collective-permute-start | bytes 393224 | tf_op jit(solution)/shard_map/ppermute | solution.py:40
  26.0 4.5 %collective-permute-start.14 = (bf16[128,256]{1,0:T(8,128)(2,1)S(1)}, bf16[128,256]{1,0:T(8,128)(2,1)S(1)}, u32[]{:S(2)}, u32[]{:S(2)}) collective-permute-start(bf16[128,256]{1,0:T(8,128)(2,1)S(1)} %shard_map.81.refs_2_), channel_id=1, source_target_pairs={{0,8},{8,0},{16,24},{24,16},{1,9},{9,1},{17,25},{25,17},{2,10},{10... | collective-permute-start | bytes 196616 | tf_op jit(solution)/shard_map/ppermute | solution.py:44
  27.7 7.0 %collective-permute-start.13 = (bf16[128,256]{1,0:T(8,128)(2,1)S(1)}, bf16[128,256]{1,0:T(8,128)(2,1)S(1)}, u32[]{:S(2)}, u32[]{:S(2)}) collective-permute-start(bf16[128,256]{1,0:T(8,128)(2,1)S(1)} %shard_map.81.refs_2_), channel_id=1, source_target_pairs={{0,16},{8,24},{16,0},{24,8},{1,17},{9,25},{17,1},{25,9},{2,18},{10... | collective-permute-start | bytes 196616 | tf_op jit(solution)/shard_map/ppermute | solution.py:44
  30.3 6.1 %collective-permute-start.12 = (bf16[128,256]{1,0:T(8,128)(2,1)S(1)}, bf16[128,256]{1,0:T(8,128)(2,1)S(1)}, u32[]{:S(2)}, u32[]{:S(2)}) collective-permute-start(bf16[128,256]{1,0:T(8,128)(2,1)S(1)} %shard_map.81.refs_2_), channel_id=1, source_target_pairs={{0,24},{8,16},{16,8},{24,0},{1,25},{9,17},{17,9},{25,1},{2,26},{10... | collective-permute-start | bytes 196616 | tf_op jit(solution)/shard_map/ppermute | solution.py:44

commit v6 on v5

--- a/solution.py
+++ b/solution.py
@@ -220,15 +220,6 @@
         [square] * 5 + [on_chip((rows, length), jnp.float32)],
         (meta,),
         (pltpu.VMEM,),
-    )
-
-
-def project(x, weight):
-    return local_call(
-        dot_kernel,
-        on_chip((x.shape[0], weight.shape[1]), jnp.bfloat16),
-        (x, weight),
-        [pltpu.VMEM] * 2,
     )
 
 
@@ -418,7 +409,8 @@
         raise ValueError("axis size")
     away = [3, 2, 1]
     weights = [key_weight[0], value_weight[0], query_weight[0]]
-    slabs = cut(rows_here, count, away)
+    slabs = list(cut(rows_here, count, away[:1]))
+    slabs += cut(rows_here, count, away[1:])
     arrived = {}
     for k, slab in zip(away, slabs):
         arrived[k] = swap_dp(slab, k, count)

time: 37.8 us -> 37.7 us (level)
  waiting for transfers between devices: 12 us -> 11 us
  Pallas kernels: 7.51 us -> 8.38 us
    ppermute x5, waiting for transfers between devices: 5.1 us -> 4.03 us  [swap_dp(): lax.ppermute(x, 'dp', [(i, partner(i, step, count)) for i in range(count)])]
    pallas_call x10 -> x11, Pallas kernels: 7.51 us -> 8.38 us  [local_call(): pl.pallas_call(kernel, out_shape=out_shape, in_specs=in_specs, compiler_p...]
  transfers between devices with their start and end apart: 15 -> 15, of which waited for: 6 -> 6; matrix products, arithmetic and copies ran while one was open for 0% -> 0% of each run, Pallas kernels for 14% -> 16%
where the time goes in v6:
time: 37.7 us; the launch traced here: 37.4 us
  starting transfers between devices  17.9 us (47%)
  waiting for transfers between devices  11 us (29%)
  Pallas kernels  8.38 us (22%)
    pallas_call x11, Pallas kernels, local_call(): pl.pallas_call(kernel, out_shape=out_shape, in_specs=in_specs, compiler_p...  8.38 us
    ppermute x5, starting transfers between devices, swap_dp(): lax.ppermute(x, 'dp', [(i, partner(i, step, count)) for i in range(count)])  8.2 us
    ppermute x3, waiting for transfers between devices, swap_ctx(): lax.ppermute(x, 'ctx', [(i, partner(i, step, ring)) for i in range(ring)])  5.84 us
    ppermute x6, starting transfers between devices, to_next_section(): return lax.ppermute(x, ('dp', 'section'), moves)  5.3 us
    ppermute x3, starting transfers between devices, swap_ctx(): lax.ppermute(x, 'ctx', [(i, partner(i, step, ring)) for i in range(ring)])  4.45 us
    ppermute x5, waiting for transfers between devices, swap_dp(): lax.ppermute(x, 'dp', [(i, partner(i, step, count)) for i in range(count)])  4.03 us
    ppermute x6, waiting for transfers between devices, to_next_section(): return lax.ppermute(x, ('dp', 'section'), moves)  1.11 us
  transfers between devices with their start and end apart: 15, of which 6 were waited for; matrix products, arithmetic and copies ran while one was open for 0% of the time, Pallas kernels for 16%

profile of v6, /device:TPU:0, one launch (start us, length us, event | category | flops | bytes accessed | tf_op | source)
XLA Modules:
  0.0 37.4 jit_solution(15799507108710377302)
XLA Ops:
  0.0 1.0 %shard_map.75 = bf16[128,1024]{1,0:T(8,128)(2,1)S(1)} custom-call(bf16[128,4096]{1,0:T(8,128)(2,1)} %bitcast.7), custom_call_target="tpu_custom_call" | custom-call | tf_op jit(solution)/shard_map/pallas_call | solution.py:56
  1.0 4.0 %collective-permute-start.2 = (bf16[128,1024]{1,0:T(8,128)(2,1)S(1)}, bf16[128,1024]{1,0:T(8,128)(2,1)S(1)}, u32[]{:S(2)}, u32[]{:S(2)}) collective-permute-start(bf16[128,1024]{1,0:T(8,128)(2,1)S(1)} %shard_map.75), channel_id=1, source_target_pairs={{0,6},{2,4},{4,2},{6,0},{1,7},{3,5},{5,3},{7,1},{8,14},{10,12},{12... | collective-permute-start | bytes 786440 | tf_op jit(solution)/shard_map/ppermute | solution.py:31
  5.0 1.0 %shard_map.74 = (bf16[128,1024]{1,0:T(8,128)(2,1)S(1)}, bf16[128,1024]{1,0:T(8,128)(2,1)S(1)}) custom-call(bf16[128,4096]{1,0:T(8,128)(2,1)} %bitcast.8), custom_call_target="tpu_custom_call" | custom-call | tf_op jit(solution)/shard_map/pallas_call | solution.py:56
  6.0 0.6 %collective-permute-start.1 = (bf16[128,1024]{1,0:T(8,128)(2,1)S(1)}, bf16[128,1024]{1,0:T(8,128)(2,1)S(1)}, u32[]{:S(2)}, u32[]{:S(2)}) collective-permute-start(bf16[128,1024]{1,0:T(8,128)(2,1)S(1)} %get-tuple-element.20), channel_id=1, source_target_pairs={{0,2},{2,0},{4,6},{6,4},{1,3},{3,1},{5,7},{7,5},{8,10},{10,8},{12,... | collective-permute-start | bytes 786440 | tf_op jit(solution)/shard_map/ppermute | solution.py:31
  6.7 3.2 %shard_map.73 = (bf16[1024,768]{1,0:T(8,128)(2,1)S(1)}, bf16[128,768]{1,0:T(8,128)(2,1)S(1)}, f32[1,1152]{1,0:T(1,128)S(1)}) custom-call(bf16[128,4096]{1,0:T(8,128)(2,1)} %bitcast.9, f32[1,4096]{1,0:T(1,128)} %gain_ref.1, bf16[1024,128]{1,0:T(8,128)(2,1)} %bitcast.11, bf16[1024,128]{1,0:T(8,128)(2,1)} %bitcast.12, bf16[1024,512]{1,0:T(8,128)(2,1)} %bitcast.10, ...), custom_call_target="tpu_custom_call" | custom-call | tf_op jit(solution)/shard_map/pallas_call | solution.py:56
  9.9 2.2 %collective-permute-done.2.x_ref = bf16[128,1024]{1,0:T(8,128)(2,1)S(1)} collective-permute-done((bf16[128,1024]{1,0:T(8,128)(2,1)S(1)}, bf16[128,1024]{1,0:T(8,128)(2,1)S(1)}, u32[]{:S(2)}, u32[]{:S(2)}) %collective-permute-start.2) | collective-permute-done | bytes 262176 | tf_op jit(solution)/shard_map/ppermute | solution.py:31
  12.2 0.4 shard_map.76
  12.5 2.1 %collective-permute-start.3 = (bf16[128,256]{1,0:T(8,128)(2,1)S(1)}, bf16[128,256]{1,0:T(8,128)(2,1)S(1)}, u32[]{:S(2)}, u32[]{:S(2)}) collective-permute-start(bf16[128,256]{1,0:T(8,128)(2,1)S(1)} %get-tuple-element.22), channel_id=1, source_target_pairs={{0,4},{2,6},{4,0},{6,2},{1,5},{3,7},{5,1},{7,3},{8,12},{10,14},{12... | collective-permute-start | bytes 196616 | tf_op jit(solution)/shard_map/ppermute | solution.py:31
  14.6 1.5 %collective-permute-start.6 = (bf16[128,256]{1,0:T(8,128)(2,1)S(1)}, bf16[128,256]{1,0:T(8,128)(2,1)S(1)}, u32[]{:S(2)}, u32[]{:S(2)}) collective-permute-start(bf16[128,256]{1,0:T(8,128)(2,1)S(1)} %get-tuple-element.24), channel_id=1, source_target_pairs={{0,2},{2,0},{4,6},{6,4},{1,3},{3,1},{5,7},{7,5},{8,10},{10,8},{12,... | collective-permute-start | bytes 196616 | tf_op jit(solution)/shard_map/ppermute | solution.py:31
  16.1 1.8 %collective-permute-done.1.x_ref = bf16[128,1024]{1,0:T(8,128)(2,1)S(1)} collective-permute-done((bf16[128,1024]{1,0:T(8,128)(2,1)S(1)}, bf16[128,1024]{1,0:T(8,128)(2,1)S(1)}, u32[]{:S(2)}, u32[]{:S(2)}) %collective-permute-start.1) | collective-permute-done | bytes 262176 | tf_op jit(solution)/shard_map/ppermute | solution.py:31
  17.9 0.2 shard_map.79
  18.1 1.7 %collective-permute-start.9 = (bf16[128,256]{1,0:T(8,128)(2,1)S(1)}, bf16[128,256]{1,0:T(8,128)(2,1)S(1)}, u32[]{:S(2)}, u32[]{:S(2)}) collective-permute-start(bf16[128,256]{1,0:T(8,128)(2,1)S(1)} %shard_map.79), channel_id=1, source_target_pairs={{0,3},{1,2},{2,1},{3,0},{4,7},{5,6},{6,5},{7,4},{8,11},{9,10},{10,... | collective-permute-start | bytes 196616 | tf_op jit(solution)/shard_map/ppermute | solution.py:40
  20.2 1.6 %collective-permute-start.8 = (bf16[128,256]{1,0:T(8,128)(2,1)S(1)}, bf16[128,256]{1,0:T(8,128)(2,1)S(1)}, u32[]{:S(2)}, u32[]{:S(2)}) collective-permute-start(bf16[128,256]{1,0:T(8,128)(2,1)S(1)} %get-tuple-element.25), channel_id=1, source_target_pairs={{0,7},{1,6},{2,5},{3,4},{4,3},{5,2},{6,1},{7,0},{8,15},{9,14},{10,... | collective-permute-start | bytes 196616 | tf_op jit(solution)/shard_map/ppermute | solution.py:40
  21.8 0.3 shard_map.77
  22.1 0.3 shard_map.78
  22.5 0.5 %collective-permute-start.7 = (bf16[128,512]{1,0:T(8,128)(2,1)S(1)}, bf16[128,512]{1,0:T(8,128)(2,1)S(1)}, u32[]{:S(2)}, u32[]{:S(2)}) collective-permute-start(bf16[128,512]{1,0:T(8,128)(2,1)S(1)} %shard_map.78), channel_id=1, source_target_pairs={{0,5},{1,4},{2,7},{3,6},{4,1},{5,0},{6,3},{7,2},{8,13},{9,12},{10,... | collective-permute-start | bytes 393224 | tf_op jit(solution)/shard_map/ppermute | solution.py:40
  23.0 1.3 %collective-permute-start.4 = (bf16[128,512]{1,0:T(8,128)(2,1)S(1)}, bf16[128,512]{1,0:T(8,128)(2,1)S(1)}, u32[]{:S(2)}, u32[]{:S(2)}) collective-permute-start(bf16[128,512]{1,0:T(8,128)(2,1)S(1)} %shard_map.77), channel_id=1, source_target_pairs={{0,3},{1,2},{2,1},{3,0},{4,7},{5,6},{6,5},{7,4},{8,11},{9,10},{10,... | collective-permute-start | bytes 393224 | tf_op jit(solution)/shard_map/ppermute | solution.py:40
  24.3 0.4 shard_map.81
  24.6 1.1 %collective-permute-done.10.refs_2_ = bf16[128,256]{1,0:T(8,128)(2,1)S(1)} collective-permute-done((bf16[128,256]{1,0:T(8,128)(2,1)S(1)}, bf16[128,256]{1,0:T(8,128)(2,1)S(1)}, u32[]{:S(2)}, u32[]{:S(2)}) %collective-permute-start.10) | collective-permute-done | bytes 65568 | tf_op jit(solution)/shard_map/ppermute | solution.py:40
  25.8 1.6 %collective-permute-start.14 = (bf16[128,256]{1,0:T(8,128)(2,1)S(1)}, bf16[128,256]{1,0:T(8,128)(2,1)S(1)}, u32[]{:S(2)}, u32[]{:S(2)}) collective-permute-start(bf16[128,256]{1,0:T(8,128)(2,1)S(1)} %shard_map.82.refs_2_), channel_id=1, source_target_pairs={{0,8},{8,0},{16,24},{24,16},{1,9},{9,1},{17,25},{25,17},{2,10},{10... | collective-permute-start | bytes 196616 | tf_op jit(solution)/shard_map/ppermute | solution.py:44
  27.5 2.6 %collective-permute-start.13 = (bf16[128,256]{1,0:T(8,128)(2,1)S(1)}, bf16[128,256]{1,0:T(8,128)(2,1)S(1)}, u32[]{:S(2)}, u32[]{:S(2)}) collective-permute-start(bf16[128,256]{1,0:T(8,128)(2,1)S(1)} %shard_map.82.refs_2_), channel_id=1, source_target_pairs={{0,16},{8,24},{16,0},{24,8},{1,17},{9,25},{17,1},{25,9},{2,18},{10... | collective-permute-start | bytes 196616 | tf_op jit(solution)/shard_map/ppermute | solution.py:44
  30.4 4.1 %collective-permute-done.13.refs_4_ = bf16[128,256]{1,0:T(8,128)(2,1)S(1)} collective-permute-done((bf16[128,256]{1,0:T(8,128)(2,1)S(1)}, bf16[128,256]{1,0:T(8,128)(2,1)S(1)}, u32[]{:S(2)}, u32[]{:S(2)}) %collective-permute-start.13) | collective-permute-done | bytes 65568 | tf_op jit(solution)/shard_map/ppermute | solution.py:44
  34.5 1.7 %collective-permute-done.12.refs_3_ = bf16[128,256]{1,0:T(8,128)(2,1)S(1)} collective-permute-done((bf16[128,256]{1,0:T(8,128)(2,1)S(1)}, bf16[128,256]{1,0:T(8,128)(2,1)S(1)}, u32[]{:S(2)}, u32[]{:S(2)}) %collective-permute-start.12) | collective-permute-done | bytes 65568 | tf_op jit(solution)/shard_map/ppermute | solution.py:44
  36.1 1.3 %shard_map.83 = bf16[128,512]{1,0:T(8,128)(2,1)} custom-call(bf16[128,768]{1,0:T(8,128)(2,1)S(1)} %collective-permute-done.own_ref, bf16[128,512]{1,0:T(8,128)(2,1)S(1)} %collective-permute-done.4.refs_0_, bf16[128,512]{1,0:T(8,128)(2,1)S(1)} %collective-permute-done.7.refs_1_, bf16[128,256]{1,0:T(8,128)(2,1)S(1)} %shard_map.82.refs_2_, ...), custom_call_target="tpu_custom_call" | custom-call | tf_op jit(solution)/shard_map/pallas_call | solution.py:56
  (17 shorter events, 1.0 us)
Async XLA Ops:
  1.0 11.2 %collective-permute-start.2 = (bf16[128,1024]{1,0:T(8,128)(2,1)S(1)}, bf16[128,1024]{1,0:T(8,128)(2,1)S(1)}, u32[]{:S(2)}, u32[]{:S(2)}) collective-permute-start(bf16[128,1024]{1,0:T(8,128)(2,1)S(1)} %shard_map.75), channel_id=1, source_target_pairs={{0,6},{2,4},{4,2},{6,0},{1,7},{3,5},{5,3},{7,1},{8,14},{10,12},{12... | collective-permute-start | bytes 786440 | tf_op jit(solution)/shard_map/ppermute | solution.py:31
  6.0 11.9 %collective-permute-start.1 = (bf16[128,1024]{1,0:T(8,128)(2,1)S(1)}, bf16[128,1024]{1,0:T(8,128)(2,1)S(1)}, u32[]{:S(2)}, u32[]{:S(2)}) collective-permute-start(bf16[128,1024]{1,0:T(8,128)(2,1)S(1)} %get-tuple-element.20), channel_id=1, source_target_pairs={{0,2},{2,0},{4,6},{6,4},{1,3},{3,1},{5,7},{7,5},{8,10},{10,8},{12,... | collective-permute-start | bytes 786440 | tf_op jit(solution)/shard_map/ppermute | solution.py:31
  6.6 11.5 %collective-permute-start.5 = (bf16[128,1024]{1,0:T(8,128)(2,1)S(1)}, bf16[128,1024]{1,0:T(8,128)(2,1)S(1)}, u32[]{:S(2)}, u32[]{:S(2)}) collective-permute-start(bf16[128,1024]{1,0:T(8,128)(2,1)S(1)} %get-tuple-element.23), channel_id=1, source_target_pairs={{0,4},{2,6},{4,0},{6,2},{1,5},{3,7},{5,1},{7,3},{8,12},{10,14},{12... | collective-permute-start | bytes 786440 | tf_op jit(solution)/shard_map/ppermute | solution.py:31
  9.8 13.2 %collective-permute-start = (bf16[128,768]{1,0:T(8,128)(2,1)S(1)}, bf16[128,768]{1,0:T(8,128)(2,1)S(1)}, u32[]{:S(2)}, u32[]{:S(2)}) collective-permute-start(bf16[128,768]{1,0:T(8,128)(2,1)S(1)} %get-tuple-element.19), channel_id=1, source_target_pairs={{0,1},{1,0},{2,3},{3,2},{4,5},{5,4},{6,7},{7,6},{8,9},{9,8},{10,11... | collective-permute-start | bytes 589832 | tf_op jit(solution)/shard_map/ppermute | solution.py:40
  12.5 7.5 %collective-permute-start.3 = (bf16[128,256]{1,0:T(8,128)(2,1)S(1)}, bf16[128,256]{1,0:T(8,128)(2,1)S(1)}, u32[]{:S(2)}, u32[]{:S(2)}) collective-permute-start(bf16[128,256]{1,0:T(8,128)(2,1)S(1)} %get-tuple-element.22), channel_id=1, source_target_pairs={{0,4},{2,6},{4,0},{6,2},{1,5},{3,7},{5,1},{7,3},{8,12},{10,14},{12... | collective-permute-start | bytes 196616 | tf_op jit(solution)/shard_map/ppermute | solution.py:31
  14.6 5.6 %collective-permute-start.6 = (bf16[128,256]{1,0:T(8,128)(2,1)S(1)}, bf16[128,256]{1,0:T(8,128)(2,1)S(1)}, u32[]{:S(2)}, u32[]{:S(2)}) collective-permute-start(bf16[128,256]{1,0:T(8,128)(2,1)S(1)} %get-tuple-element.24), channel_id=1, source_target_pairs={{0,2},{2,0},{4,6},{6,4},{1,3},{3,1},{5,7},{7,5},{8,10},{10,8},{12,... | collective-permute-start | bytes 196616 | tf_op jit(solution)/shard_map/ppermute | solution.py:31
  17.9 4.6 %collective-permute-start.11 = (f32[1,1152]{1,0:T(1,128)S(1)}, f32[1,1152]{1,0:T(1,128)S(1)}, u32[]{:S(2)}, u32[]{:S(2)}) collective-permute-start(f32[1,1152]{1,0:T(1,128)S(1)} %get-tuple-element.26), channel_id=1, source_target_pairs={{0,1},{1,0},{2,3},{3,2},{4,5},{5,4},{6,7},{7,6},{8,9},{9,8},{10,11... | collective-permute-start | bytes 13832 | tf_op jit(solution)/shard_map/ppermute | solution.py:423
  18.1 6.5 %collective-permute-start.9 = (bf16[128,256]{1,0:T(8,128)(2,1)S(1)}, bf16[128,256]{1,0:T(8,128)(2,1)S(1)}, u32[]{:S(2)}, u32[]{:S(2)}) collective-permute-start(bf16[128,256]{1,0:T(8,128)(2,1)S(1)} %shard_map.79), channel_id=1, source_target_pairs={{0,3},{1,2},{2,1},{3,0},{4,7},{5,6},{6,5},{7,4},{8,11},{9,10},{10,... | collective-permute-start | bytes 196616 | tf_op jit(solution)/shard_map/ppermute | solution.py:40
  20.0 5.7 %collective-permute-start.10 = (bf16[128,256]{1,0:T(8,128)(2,1)S(1)}, bf16[128,256]{1,0:T(8,128)(2,1)S(1)}, u32[]{:S(2)}, u32[]{:S(2)}) collective-permute-start(bf16[128,256]{1,0:T(8,128)(2,1)S(1)} %shard_map.80), channel_id=1, source_target_pairs={{0,5},{1,4},{2,7},{3,6},{4,1},{5,0},{6,3},{7,2},{8,13},{9,12},{10,... | collective-permute-start | bytes 196616 | tf_op jit(solution)/shard_map/ppermute | solution.py:40
  20.2 5.5 %collective-permute-start.8 = (bf16[128,256]{1,0:T(8,128)(2,1)S(1)}, bf16[128,256]{1,0:T(8,128)(2,1)S(1)}, u32[]{:S(2)}, u32[]{:S(2)}) collective-permute-start(bf16[128,256]{1,0:T(8,128)(2,1)S(1)} %get-tuple-element.25), channel_id=1, source_target_pairs={{0,7},{1,6},{2,5},{3,4},{4,3},{5,2},{6,1},{7,0},{8,15},{9,14},{10,... | collective-permute-start | bytes 196616 | tf_op jit(solution)/shard_map/ppermute | solution.py:40
  22.5 13.7 %collective-permute-start.7 = (bf16[128,512]{1,0:T(8,128)(2,1)S(1)}, bf16[128,512]{1,0:T(8,128)(2,1)S(1)}, u32[]{:S(2)}, u32[]{:S(2)}) collective-permute-start(bf16[128,512]{1,0:T(8,128)(2,1)S(1)} %shard_map.78), channel_id=1, source_target_pairs={{0,5},{1,4},{2,7},{3,6},{4,1},{5,0},{6,3},{7,2},{8,13},{9,12},{10,... | collective-permute-start | bytes 393224 | tf_op jit(solution)/shard_map/ppermute | solution.py:40
  23.0 13.2 %collective-permute-start.4 = (bf16[128,512]{1,0:T(8,128)(2,1)S(1)}, bf16[128,512]{1,0:T(8,128)(2,1)S(1)}, u32[]{:S(2)}, u32[]{:S(2)}) collective-permute-start(bf16[128,512]{1,0:T(8,128)(2,1)S(1)} %shard_map.77), channel_id=1, source_target_pairs={{0,3},{1,2},{2,1},{3,0},{4,7},{5,6},{6,5},{7,4},{8,11},{9,10},{10,... | collective-permute-start | bytes 393224 | tf_op jit(solution)/shard_map/ppermute | solution.py:40
  25.8 4.5 %collective-permute-start.14 = (bf16[128,256]{1,0:T(8,128)(2,1)S(1)}, bf16[128,256]{1,0:T(8,128)(2,1)S(1)}, u32[]{:S(2)}, u32[]{:S(2)}) collective-permute-start(bf16[128,256]{1,0:T(8,128)(2,1)S(1)} %shard_map.82.refs_2_), channel_id=1, source_target_pairs={{0,8},{8,0},{16,24},{24,16},{1,9},{9,1},{17,25},{25,17},{2,10},{10... | collective-permute-start | bytes 196616 | tf_op jit(solution)/shard_map/ppermute | solution.py:44
  27.5 7.0 %collective-permute-start.13 = (bf16[128,256]{1,0:T(8,128)(2,1)S(1)}, bf16[128,256]{1,0:T(8,128)(2,1)S(1)}, u32[]{:S(2)}, u32[]{:S(2)}) collective-permute-start(bf16[128,256]{1,0:T(8,128)(2,1)S(1)} %shard_map.82.refs_2_), channel_id=1, source_target_pairs={{0,16},{8,24},{16,0},{24,8},{1,17},{9,25},{17,1},{25,9},{2,18},{10... | collective-permute-start | bytes 196616 | tf_op jit(solution)/shard_map/ppermute | solution.py:44
  30.1 6.1 %collective-permute-start.12 = (bf16[128,256]{1,0:T(8,128)(2,1)S(1)}, bf16[128,256]{1,0:T(8,128)(2,1)S(1)}, u32[]{:S(2)}, u32[]{:S(2)}) collective-permute-start(bf16[128,256]{1,0:T(8,128)(2,1)S(1)} %shard_map.82.refs_2_), channel_id=1, source_target_pairs={{0,24},{8,16},{16,8},{24,0},{1,25},{9,17},{17,9},{25,1},{2,26},{10... | collective-permute-start | bytes 196616 | tf_op jit(solution)/shard_map/ppermute | solution.py:44
